TPU v7x, 512 devices: a whole 4x8x8 slice. The times are simulated.
512 devices in a mesh: dp: 16 (over z, core), mp: 32 (over y, x).
Axes of the slice: x: 4, y: 8, z: 8, core: 2. Of those that a mesh axis runs over, the one named last changes fastest.
Arguments:
- activations: bfloat16 [32768, 8192], P('dp', 'mp'), as said below
- output_grads: bfloat16 [32768, 28672], P('dp', 'mp'), as said below
- probe_matrix: bfloat16 [28672, 128], P('mp'), may hold values from -6 to 6
Outputs:
- basis: float32 [8192, 128], P('mp')
- projection: float32 [128, 28672], P(None, 'mp')
Inputs may be any that keep to these rules, and one draw needn't show every extreme that they name: `activations`: finite real values of order one. `output_grads`: finite real values of order one.
All inputs are finite; a program needn't handle non-finite values.
Results may differ from a plain program's by a relative error of at most 0.035.
Values may be sent and summed in bfloat16 or wider, within the bound.
No kernel may reach another device: no remote copies, remote signals or barrier semaphores. Data moves between devices by JAX's collectives and lax.ppermute only.
A program may use at most 64 MiB of HBM per device.

v0:
```python
import jax
import jax.numpy as jnp
from jax import lax
from jax.sharding import PartitionSpec as P

H = 8192


def contract_rows(left, right):
    return lax.dot_general(
        left, right, (((0,), (0,)), ((), ())), preferred_element_type=jnp.float32
    )


def token_total(partial_value):
    return lax.psum(partial_value.astype(jnp.bfloat16), "mp")


def gram_of(matrix):
    return lax.dot_general(
        matrix,
        matrix,
        (((0,), (0,)), ((), ())),
        precision=lax.Precision.HIGHEST,
        preferred_element_type=jnp.float32,
    )


def solve_rows(factor, matrix):
    return lax.linalg.triangular_solve(
        factor, matrix, left_side=False, lower=True, transpose_a=True
    )


def orthonormalize(partial_value):
    summed = lax.psum(partial_value, "dp")
    gram_matrix = lax.psum(gram_of(summed), "mp")
    factor = jnp.linalg.cholesky(gram_matrix)
    return solve_rows(factor, summed)


def on_device(activations, output_grads, probe_matrix):
    probe_rows = token_total(
        jnp.dot(output_grads, probe_matrix, preferred_element_type=jnp.float32)
    )
    first_basis = orthonormalize(contract_rows(activations, probe_rows))
    token_rows = token_total(
        jnp.dot(activations, first_basis.astype(jnp.bfloat16), preferred_element_type=jnp.float32)
    )
    second_basis = orthonormalize(contract_rows(output_grads, token_rows))
    unit_rows = token_total(
        jnp.dot(output_grads, second_basis.astype(jnp.bfloat16), preferred_element_type=jnp.float32)
    )
    third_basis = orthonormalize(contract_rows(activations, unit_rows))
    last_rows = token_total(
        jnp.dot(activations, third_basis.astype(jnp.bfloat16), preferred_element_type=jnp.float32)
    )
    projected = contract_rows(last_rows, output_grads)
    projection = lax.psum(projected, "dp")
    basis = third_basis * jnp.sqrt(jnp.float32(H))
    return (basis, projection)


def solution(mesh):
    in_specs = (P("dp", "mp"), P("dp", "mp"), P("mp", None))
    out_specs = (P("mp", None), P(None, "mp"))
    return jax.shard_map(
        on_device, mesh=mesh, in_specs=in_specs, out_specs=out_specs, check_vma=False
    )
```

profile of v0, /device:TPU:1, one launch (start us, length us, event | category | flops | bytes accessed | tf_op | source)
XLA Modules:
  0.0 1659.9 jit_solution(11712549844243807659)
XLA Ops:
  7.2 0.0 all-reduce.12.cloned.1.call-start
  7.2 4.1 convolution_convert_fusion.1
  11.3 0.0 all-reduce.12.cloned.1.call-update
  11.3 0.0 all-reduce.14.cloned.1.call-start
  11.4 159.3 %all-reduce.12.cloned.1.call-done = bf16[2048,128]{1,0:T(8,128)(2,1)} async-done(((bf16[2048,128]{1,0:T(8,128)(2,1)}), bf16[2048,128]{1,0:T(8,128)(2,1)}) %all-reduce.12.cloned.1.call-update) | async-done | bytes 524304 | tf_op jit(solution)/shard_map/psum | solution.py:16
  170.7 2.0 convolution_bitcast_fusion.4
  172.8 0.0 all-reduce.16.cloned.1.call-start
  172.8 116.4 %all-reduce.14.cloned.1.call-done = f32[256,128]{0,1:T(8,128)} async-done(((f32[256,128]{0,1:T(8,128)}), f32[256,128]{0,1:T(8,128)}) %all-reduce.14.cloned.1.call-update) | async-done | bytes 131088 | tf_op jit(solution)/shard_map/psum | solution.py:36
  289.2 1.9 fusion.18
  291.1 0.0 all-reduce.16.cloned.1.call-update
  291.1 0.0 all-reduce.18.cloned.1.call-start
  291.2 148.2 %all-reduce.16.cloned.1.call-done = f32[128,128]{0,1:T(8,128)} async-done(((f32[128,128]{0,1:T(8,128)}), f32[128,128]{0,1:T(8,128)}) %all-reduce.16.cloned.1.call-update) | async-done | bytes 65552 | tf_op jit(solution)/shard_map/psum | solution.py:37
  439.4 0.9 copy.6
  440.3 0.9 fusion.12
  441.2 11.7 cholesky.59
  452.9 0.6 compare_reduce_fusion.2
  453.5 0.7 fusion.4
  454.2 9.8 custom-call.10
  464.0 1.2 fusion.3
  465.2 1.3 fusion.1
  466.6 0.0 all-reduce.20.cloned.1.call-start
  466.6 156.5 %all-reduce.18.cloned.1.call-done = bf16[2048,128]{0,1:T(8,128)(2,1)} async-done(((bf16[2048,128]{0,1:T(8,128)(2,1)}), bf16[2048,128]{0,1:T(8,128)(2,1)}) %all-reduce.18.cloned.1.call-update) | async-done | bytes 524304 | tf_op jit(solution)/shard_map/psum | solution.py:16
  623.1 3.7 convolution_bitcast_fusion
  626.8 0.0 all-reduce.20.cloned.1.call-update
  626.8 0.0 all-reduce.22.cloned.1.call-start
  626.8 116.4 %all-reduce.20.cloned.1.call-done = f32[896,128]{0,1:T(8,128)} async-done(((f32[896,128]{0,1:T(8,128)}), f32[896,128]{0,1:T(8,128)}) %all-reduce.20.cloned.1.call-update) | async-done | bytes 458768 | tf_op jit(solution)/shard_map/psum | solution.py:36
  743.2 2.4 fusion.19
  745.6 0.0 all-reduce.22.cloned.1.call-update
  745.6 0.2 all-reduce.24.cloned.1.call-start
  745.8 145.9 %all-reduce.22.cloned.1.call-done = f32[128,128]{0,1:T(8,128)} async-done(((f32[128,128]{0,1:T(8,128)}), f32[128,128]{0,1:T(8,128)}) %all-reduce.22.cloned.1.call-update) | async-done | bytes 65552 | tf_op jit(solution)/shard_map/psum | solution.py:37
  891.7 0.9 copy.8
  892.7 0.9 fusion.10
  893.5 11.7 cholesky.70
  905.3 0.6 compare_reduce_fusion.1
  905.9 0.7 fusion.5
  906.6 9.8 custom-call.8
  916.4 1.9 convolution_convert_fusion.4
  918.3 4.2 fusion
  922.5 0.0 all-reduce.24.cloned.1.call-update
  922.5 0.0 all-reduce.26.cloned.1.call-start
  922.6 156.4 %all-reduce.24.cloned.1.call-done = bf16[2048,128]{0,1:T(8,128)(2,1)} async-done(((bf16[2048,128]{0,1:T(8,128)(2,1)}), bf16[2048,128]{0,1:T(8,128)(2,1)}) %all-reduce.24.cloned.1.call-update) | async-done | bytes 524304 | tf_op jit(solution)/shard_map/psum | solution.py:16
  1079.0 2.0 convolution_bitcast_fusion.3
  1081.0 0.0 all-reduce.26.cloned.1.call-update
  1081.0 0.0 all-reduce.28.cloned.1.call-start
  1081.1 116.5 %all-reduce.26.cloned.1.call-done = f32[256,128]{0,1:T(8,128)} async-done(((f32[256,128]{0,1:T(8,128)}), f32[256,128]{0,1:T(8,128)}) %all-reduce.26.cloned.1.call-update) | async-done | bytes 131088 | tf_op jit(solution)/shard_map/psum | solution.py:36
  1197.5 1.9 fusion.20
  1199.4 0.3 all-reduce.30.cloned.1.call-start
  1199.7 147.9 %all-reduce.28.cloned.1.call-done = f32[128,128]{0,1:T(8,128)} async-done(((f32[128,128]{0,1:T(8,128)}), f32[128,128]{0,1:T(8,128)}) %all-reduce.28.cloned.1.call-update) | async-done | bytes 65552 | tf_op jit(solution)/shard_map/psum | solution.py:37
  1347.7 0.9 copy.10
  1348.6 0.9 fusion.8
  1349.4 11.7 cholesky.81
  1361.2 0.6 compare_reduce_fusion
  1361.8 0.7 fusion.6
  1362.5 9.8 custom-call.11
  1372.3 1.2 broadcast_multiply_fusion
  1373.5 1.3 fusion.2
  1374.8 0.0 all-reduce.30.cloned.1.call-update
  1374.9 0.0 all-reduce.32.cloned.1.call-start
  1374.9 156.5 %all-reduce.30.cloned.1.call-done = bf16[2048,128]{0,1:T(8,128)(2,1)} async-done(((bf16[2048,128]{0,1:T(8,128)(2,1)}), bf16[2048,128]{0,1:T(8,128)(2,1)}) %all-reduce.30.cloned.1.call-update) | async-done | bytes 524304 | tf_op jit(solution)/shard_map/psum | solution.py:16
  1531.4 3.7 fusion.21
  1535.1 0.0 all-reduce.32.cloned.1.call-update
  1535.1 0.8 copy.11
  1535.9 115.7 %all-reduce.32.cloned.1.call-done = f32[128,896]{1,0:T(8,128)} async-done(((f32[128,896]{1,0:T(8,128)}), f32[128,896]{1,0:T(8,128)}) %all-reduce.32.cloned.1.call-update) | async-done | bytes 458768 | tf_op jit(solution)/shard_map/psum | solution.py:59
  1651.5 1.8 copy.26
  (8 shorter events, 0.2 us)
Async XLA Ops:
  7.2 163.5 %copy-start = (bf16[2048,256]{1,0:T(8,128)(2,1)S(1)}, bf16[2048,256]{1,0:T(8,128)(2,1)}, u32[]{:S(2)}) copy-start(bf16[2048,256]{1,0:T(8,128)(2,1)} %param.6) | copy-start | bytes 3145732
  7.2 163.5 %all-reduce.12.cloned.1.call-start = ((), (), s32[]{:S(2)}) async-start(), calls=%async_computation | async-start | bytes 1048576 | tf_op jit(solution)/shard_map/psum | solution.py:16
  11.3 277.9 %all-reduce.14.cloned.1.call-start = ((), (), s32[]{:S(2)}) async-start(), calls=%async_computation.1 | async-start | bytes 262144 | tf_op jit(solution)/shard_map/psum | solution.py:36
  172.8 266.6 %all-reduce.16.cloned.1.call-start = ((), (), s32[]{:S(2)}) async-start(), calls=%async_computation.2 | async-start | bytes 131072 | tf_op jit(solution)/shard_map/psum | solution.py:37
  291.1 331.9 %all-reduce.18.cloned.1.call-start = ((), (), s32[]{:S(2)}) async-start(), calls=%async_computation.3 | async-start | bytes 1048576 | tf_op jit(solution)/shard_map/psum | solution.py:16
  466.6 276.6 %all-reduce.20.cloned.1.call-start = ((), (), s32[]{:S(2)}) async-start(), calls=%async_computation.4 | async-start | bytes 917504 | tf_op jit(solution)/shard_map/psum | solution.py:36
  626.8 264.9 %all-reduce.22.cloned.1.call-start = ((), (), s32[]{:S(2)}) async-start(), calls=%async_computation.5 | async-start | bytes 131072 | tf_op jit(solution)/shard_map/psum | solution.py:37
  745.6 333.4 %all-reduce.24.cloned.1.call-start = ((), (), s32[]{:S(2)}) async-start(), calls=%async_computation.6 | async-start | bytes 1048576 | tf_op jit(solution)/shard_map/psum | solution.py:16
  922.5 275.0 %all-reduce.26.cloned.1.call-start = ((), (), s32[]{:S(2)}) async-start(), calls=%async_computation.7 | async-start | bytes 262144 | tf_op jit(solution)/shard_map/psum | solution.py:36
  1081.0 266.7 %all-reduce.28.cloned.1.call-start = ((), (), s32[]{:S(2)}) async-start(), calls=%async_computation.8 | async-start | bytes 131072 | tf_op jit(solution)/shard_map/psum | solution.py:37
  1199.4 331.9 %all-reduce.30.cloned.1.call-start = ((), (), s32[]{:S(2)}) async-start(), calls=%async_computation.9 | async-start | bytes 1048576 | tf_op jit(solution)/shard_map/psum | solution.py:16
  1374.9 276.7 %all-reduce.32.cloned.1.call-start = ((), (), s32[]{:S(2)}) async-start(), calls=%async_computation.10 | async-start | bytes 917504 | tf_op jit(solution)/shard_map/psum | solution.py:59
Sparse Core Ops, SparseCore 0:
  11.4 159.2 all-reduce.11
  173.7 115.5 all-reduce.13
  293.3 146.0 all-reduce.15
  466.7 156.3 all-reduce.17
  626.9 116.2 all-reduce.19
  747.1 144.5 all-reduce.21
  922.6 156.2 all-reduce.23
  1082.0 115.5 all-reduce.25
  1201.6 146.0 all-reduce.27
  1375.0 156.3 all-reduce.29
  1535.2 116.2 all-reduce.31
where the time goes:
time: 1660 us
  waiting for transfers between devices  1540 us (93%)
  other arithmetic  71.1 us (4%)
  matrix products  32.8 us (2%)
    psum x4, waiting for transfers between devices, token_total(): return lax.psum(partial_value.astype(jnp.bfloat16), 'mp')  629 us
    psum x3, waiting for transfers between devices, orthonormalize(): gram_matrix = lax.psum(gram_of(summed), 'mp')  442 us
    psum x3, waiting for transfers between devices, orthonormalize(): summed = lax.psum(partial_value, 'dp')  349 us
    psum x1, waiting for transfers between devices, on_device(): projection = lax.psum(projected, 'dp')  116 us
    another operation x9, other arithmetic, orthonormalize(): factor = jnp.linalg.cholesky(gram_matrix)  37.2 us
  transfers between devices with their start and end apart: 11, of which 11 were waited for; matrix products, arithmetic and copies ran while one was open for 0% of the time, Pallas kernels for 0%

commit v1 on v0

v1 whole, which is shorter than its diff:
```python
import jax
import jax.numpy as jnp
from jax import lax
from jax.sharding import PartitionSpec as P

H = 8192
N_MP = 32
N_DP = 16
K = 128
HIGHEST = lax.Precision.HIGHEST


def rows_product(left, right):
    return lax.dot_general(
        left, right, (((0,), (0,)), ((), ())), preferred_element_type=jnp.float32
    )


def split_two(matrix):
    high = matrix.astype(jnp.bfloat16)
    low = (matrix - high.astype(jnp.float32)).astype(jnp.bfloat16)
    return jnp.concatenate([high, low], axis=1)


def exchange(blocks, axis):
    return lax.all_to_all(blocks, axis, 0, 0)


def scatter_sum(blocks, axis):
    return jnp.sum(exchange(blocks, axis).astype(jnp.float32), axis=0)


def gather(block, axis, count):
    return exchange(jnp.broadcast_to(block[None], (count,) + block.shape), axis)


def sum_over_tokens(partial_value):
    rows, columns = partial_value.shape
    mine = scatter_sum(partial_value.reshape(N_DP, rows // N_DP, columns), "dp")
    return gather(mine, "dp", N_DP).reshape(rows, columns)


def token_rows_of(data, sketch):
    tokens = data.shape[0]
    gram = lax.dot_general(
        sketch, sketch, (((0,), (0,)), ((), ())), precision=HIGHEST,
        preferred_element_type=jnp.float32,
    )
    both = jnp.dot(data, split_two(sketch), preferred_element_type=jnp.float32)
    product = both[:, :K] + both[:, K:]
    span = tokens // N_MP
    blocks = jnp.concatenate(
        [product.reshape(N_MP, span, K), gram.reshape(N_MP, K // N_MP, K),
         jnp.zeros((N_MP, K // N_MP, K), jnp.float32)], axis=1
    )
    whole = gather(scatter_sum(blocks, "mp"), "mp", N_MP)
    gram = whole[:, span:span + K // N_MP].reshape(K, K)
    factor = jnp.linalg.cholesky(gram)
    inverse = lax.linalg.triangular_solve(
        factor, jnp.eye(K, dtype=jnp.float32), left_side=False, lower=True, transpose_a=True
    )
    product = whole[:, :span].reshape(tokens, K)
    rows = jnp.dot(product, inverse, precision=HIGHEST, preferred_element_type=jnp.float32)
    return rows.astype(jnp.bfloat16), inverse


def on_device(activations, output_grads, probe_matrix):
    tokens = activations.shape[0]
    partial_value = jnp.dot(output_grads, probe_matrix, preferred_element_type=jnp.float32)
    mine = scatter_sum(partial_value.astype(jnp.bfloat16).reshape(N_MP, tokens // N_MP, K), "mp")
    probe_rows = gather(mine.astype(jnp.bfloat16), "mp", N_MP).reshape(tokens, K)

    sketch = sum_over_tokens(rows_product(activations, probe_rows))
    token_rows, _ = token_rows_of(activations, sketch)
    back_sketch = sum_over_tokens(rows_product(output_grads, token_rows))
    unit_rows, _ = token_rows_of(output_grads, back_sketch)
    power_sketch = sum_over_tokens(rows_product(activations, unit_rows))
    last_rows, inverse = token_rows_of(activations, power_sketch)
    projection = sum_over_tokens(rows_product(last_rows, output_grads))
    third_basis = jnp.dot(
        power_sketch, inverse, precision=HIGHEST, preferred_element_type=jnp.float32
    )
    return (third_basis * jnp.sqrt(jnp.float32(H)), projection)


def solution(mesh):
    in_specs = (P("dp", "mp"), P("dp", "mp"), P("mp", None))
    out_specs = (P("mp", None), P(None, "mp"))
    return jax.shard_map(
        on_device, mesh=mesh, in_specs=in_specs, out_specs=out_specs, check_vma=False
    )
```

time: 1660 us -> 498 us (0.30)
  waiting for transfers between devices: 1540 us -> 22.8 us
  blocking collectives: 0 us -> 369 us
  matrix products: 32.8 us -> 15.6 us
    psum x11 -> x0, waiting for transfers between devices: 1540 us -> none  [the longest x4 629 us: token_total(): return lax.psum(partial_value.astype(jnp.bfloat16), 'mp')]
    all_to_all x0 -> x14, blocking collectives: none -> 369 us  [exchange(): return lax.all_to_all(blocks, axis, 0, 0)]
    all_to_all x0 -> x2, waiting for transfers between devices: none -> 22.8 us  [exchange(): return lax.all_to_all(blocks, axis, 0, 0)]
  transfers between devices with their start and end apart: 11 -> 2, of which waited for: 11 -> 2; matrix products, arithmetic and copies ran while one was open for 0% -> 0% of each run, Pallas kernels for 0% -> 0%
where the time goes in v1:
time: 498 us; the launch traced here: 493 us
  blocking collectives  369 us (74%)
  other arithmetic  69.9 us (14%)
  waiting for transfers between devices  22.8 us (5%)
  matrix products  15.6 us (3%)
  local copies, waits for them, and re-layouts  7.24 us (1%)
  starting transfers between devices  6.87 us (1%)
    all_to_all x14, blocking collectives, exchange(): return lax.all_to_all(blocks, axis, 0, 0)  369 us
    another operation x9, other arithmetic, token_rows_of(): factor = jnp.linalg.cholesky(gram)  37.2 us
    another operation x6, other arithmetic, token_rows_of(): lax.linalg.triangular_solve(factor, jnp.eye(K, dtype=jnp.float32), left_s...  31.4 us
    all_to_all x2, waiting for transfers between devices, exchange(): return lax.all_to_all(blocks, axis, 0, 0)  22.8 us
  transfers between devices with their start and end apart: 2, of which 2 were waited for; matrix products, arithmetic and copies ran while one was open for 0% of the time, Pallas kernels for 0%

profile of v1, /device:TPU:1, one launch (start us, length us, event | category | flops | bytes accessed | tf_op | source)
XLA Modules:
  0.0 492.9 jit_solution(13019323961292640679)
XLA Ops:
  0.6 3.3 convolution_convert_fusion
  3.9 26.6 %all_to_all.80 = bf16[32,64,128]{2,1,0:T(8,128)(2,1)S(1)} all-to-all(bf16[32,64,128]{2,1,0:T(8,128)(2,1)S(1)} %bitcast.126), channel_id=1, replica_groups=mesh['dp'=16,'mp'=32] {'mp'}, dimensions={0} | all-to-all | bytes 1048576 | tf_op jit(solution)/shard_map/all_to_all | solution.py:26
  30.7 20.1 %all_to_all.81 = bf16[32,64,128]{2,1,0:T(8,128)(2,1)S(1)} all-to-all(bf16[32,64,128]{2,1,0:T(8,128)(2,1)S(1)} %broadcast_in_dim.17), channel_id=1, replica_groups=mesh['dp'=16,'mp'=32] {'mp'}, dimensions={0} | all-to-all | bytes 1048576 | tf_op jit(solution)/shard_map/all_to_all | solution.py:26
  50.8 0.4 convolution_bitcast_fusion.6
  51.2 23.0 %all_to_all.82 = f32[16,16,128]{2,1,0:T(8,128)S(1)} all-to-all(f32[16,16,128]{2,1,0:T(8,128)S(1)} %bitcast.138), channel_id=1, replica_groups=mesh['dp'=16,'mp'=32] {'dp'}, dimensions={0} | all-to-all | bytes 262144 | tf_op jit(solution)/shard_map/all_to_all | solution.py:26
  74.3 0.7 broadcast_in_dim.18
  74.9 3.4 all-to-all-start.3
  78.4 8.4 %all-to-all-done.3 = f32[16,16,128]{2,1,0:T(8,128)S(1)} async-done(((f32[16,16,128]{2,1,0:T(8,128)}), f32[16,16,128]{2,1,0:T(8,128)S(1)}, u32[]{:S(2)}, u32[]{:S(2)}) %all-to-all-start.3) | async-done | bytes 131104 | tf_op jit(solution)/shard_map/all_to_all | solution.py:26
  87.0 0.3 fusion.15
  87.3 0.5 convolution_bitcast_fusion.1
  87.8 0.1 slice_add_fusion.2
  88.0 0.3 copy.15
  88.3 0.2 maximum_maximum_fusion
  88.5 36.6 %all_to_all.83 = f32[32,72,128]{2,1,0:T(8,128)S(1)} all-to-all(f32[32,72,128]{2,1,0:T(8,128)S(1)} %maximum_maximum_fusion), channel_id=1, replica_groups=mesh['dp'=16,'mp'=32] {'mp'}, dimensions={0} | all-to-all | bytes 2359296 | tf_op jit(solution)/shard_map/all_to_all | solution.py:26
  125.2 35.1 %all_to_all.84 = f32[32,72,128]{2,1,0:T(8,128)S(1)} all-to-all(f32[32,72,128]{2,1,0:T(8,128)S(1)} %broadcast_in_dim.19), channel_id=1, replica_groups=mesh['dp'=16,'mp'=32] {'mp'}, dimensions={0} | all-to-all | bytes 2359296 | tf_op jit(solution)/shard_map/all_to_all | solution.py:26
  160.4 11.7 %cholesky.59 = f32[128,128]{1,0:T(8,128)S(1)} custom-call(f32[128,128]{1,0:T(8,128)S(1)} %fusion.28), custom_call_target="Cholesky" | custom-call | tf_op jit(solution)/shard_map/jit(cholesky)/cholesky | solution.py:58
  172.1 0.6 compare_reduce_fusion.2
  172.8 0.7 fusion.20
  173.4 9.8 %custom-call.7 = f32[1,128,128]{1,2,0:T(8,128)S(1)} custom-call(f32[1,128,128]{2,1,0:T(8,128)S(1)} %fusion.20), custom_call_target="InvertDiagBlocksLowerTriangular" | custom-call | tf_op jit(solution)/shard_map/triangular_solve/custom-call.0 | solution.py:59
  183.3 0.3 convolution_bitcast_fusion.9
  183.7 1.0 convolution_convert_fusion.3
  184.7 0.9 copy-done.1
  185.6 0.7 convolution_bitcast_fusion.4
  186.3 0.2 copy.20
  186.5 21.3 %all_to_all.85 = f32[16,56,128]{2,1,0:T(8,128)S(1)} all-to-all(f32[16,56,128]{2,1,0:T(8,128)S(1)} %bitcast.131), channel_id=1, replica_groups=mesh['dp'=16,'mp'=32] {'dp'}, dimensions={0} | all-to-all | bytes 917504 | tf_op jit(solution)/shard_map/all_to_all | solution.py:26
  207.9 18.6 %all_to_all.86 = f32[16,56,128]{2,1,0:T(8,128)S(1)} all-to-all(f32[16,56,128]{2,1,0:T(8,128)S(1)} %broadcast_in_dim.20), channel_id=1, replica_groups=mesh['dp'=16,'mp'=32] {'dp'}, dimensions={0} | all-to-all | bytes 917504 | tf_op jit(solution)/shard_map/all_to_all | solution.py:26
  226.5 0.2 copy.22
  226.7 0.1 dot_general.83
  226.9 0.6 fusion.4
  227.6 3.4 convolution_bitcast_fusion.2
  231.0 0.3 copy.21
  231.4 0.2 maximum_maximum_fusion.1
  231.5 35.8 %all_to_all.87 = f32[32,72,128]{2,1,0:T(8,128)S(1)} all-to-all(f32[32,72,128]{2,1,0:T(8,128)S(1)} %maximum_maximum_fusion.1), channel_id=1, replica_groups=mesh['dp'=16,'mp'=32] {'mp'}, dimensions={0} | all-to-all | bytes 2359296 | tf_op jit(solution)/shard_map/all_to_all | solution.py:26
  267.5 35.4 %all_to_all.88 = f32[32,72,128]{2,1,0:T(8,128)S(1)} all-to-all(f32[32,72,128]{2,1,0:T(8,128)S(1)} %broadcast_in_dim.21), channel_id=1, replica_groups=mesh['dp'=16,'mp'=32] {'mp'}, dimensions={0} | all-to-all | bytes 2359296 | tf_op jit(solution)/shard_map/all_to_all | solution.py:26
  303.0 11.7 %cholesky.70 = f32[128,128]{1,0:T(8,128)S(1)} custom-call(f32[128,128]{1,0:T(8,128)S(1)} %fusion.26), custom_call_target="Cholesky" | custom-call | tf_op jit(solution)/shard_map/jit(cholesky)/cholesky | solution.py:58
  314.8 0.6 compare_reduce_fusion.1
  315.4 0.7 fusion.21
  316.1 9.8 %custom-call.8 = f32[1,128,128]{1,2,0:T(8,128)S(1)} custom-call(f32[1,128,128]{2,1,0:T(8,128)S(1)} %fusion.21), custom_call_target="InvertDiagBlocksLowerTriangular" | custom-call | tf_op jit(solution)/shard_map/triangular_solve/custom-call.0 | solution.py:59
  325.9 0.3 convolution_bitcast_fusion.8
  326.3 1.0 convolution_convert_fusion.2
  327.3 0.3 convolution_bitcast_fusion.5
  327.7 13.3 %all_to_all.89 = f32[16,16,128]{2,1,0:T(8,128)S(1)} all-to-all(f32[16,16,128]{2,1,0:T(8,128)S(1)} %bitcast.139), channel_id=1, replica_groups=mesh['dp'=16,'mp'=32] {'dp'}, dimensions={0} | all-to-all | bytes 262144 | tf_op jit(solution)/shard_map/all_to_all | solution.py:26
  341.1 11.6 %all_to_all.90 = f32[16,16,128]{2,1,0:T(8,128)S(1)} all-to-all(f32[16,16,128]{2,1,0:T(8,128)S(1)} %broadcast_in_dim.22), channel_id=1, replica_groups=mesh['dp'=16,'mp'=32] {'dp'}, dimensions={0} | all-to-all | bytes 262144 | tf_op jit(solution)/shard_map/all_to_all | solution.py:26
  352.8 0.3 fusion.13
  353.2 0.5 convolution_bitcast_fusion
  353.7 0.1 slice_add_fusion
  353.8 0.3 copy.27
  354.1 0.2 maximum_maximum_fusion.2
  354.3 36.1 %all_to_all.91 = f32[32,72,128]{2,1,0:T(8,128)S(1)} all-to-all(f32[32,72,128]{2,1,0:T(8,128)S(1)} %maximum_maximum_fusion.2), channel_id=1, replica_groups=mesh['dp'=16,'mp'=32] {'mp'}, dimensions={0} | all-to-all | bytes 2359296 | tf_op jit(solution)/shard_map/all_to_all | solution.py:26
  390.5 34.4 %all_to_all.92 = f32[32,72,128]{2,1,0:T(8,128)S(1)} all-to-all(f32[32,72,128]{2,1,0:T(8,128)S(1)} %broadcast_in_dim.23), channel_id=1, replica_groups=mesh['dp'=16,'mp'=32] {'mp'}, dimensions={0} | all-to-all | bytes 2359296 | tf_op jit(solution)/shard_map/all_to_all | solution.py:26
  425.0 11.7 %cholesky.81 = f32[128,128]{1,0:T(8,128)S(1)} custom-call(f32[128,128]{1,0:T(8,128)S(1)} %fusion.24), custom_call_target="Cholesky" | custom-call | tf_op jit(solution)/shard_map/jit(cholesky)/cholesky | solution.py:58
  436.8 0.6 compare_reduce_fusion
  437.4 0.7 fusion.22
  438.1 9.8 %custom-call.9 = f32[1,128,128]{1,2,0:T(8,128)S(1)} custom-call(f32[1,128,128]{2,1,0:T(8,128)S(1)} %fusion.22), custom_call_target="InvertDiagBlocksLowerTriangular" | custom-call | tf_op jit(solution)/shard_map/triangular_solve/custom-call.0 | solution.py:59
  447.9 0.3 convolution_bitcast_fusion.7
  448.3 1.0 convolution_convert_fusion.1
  449.3 0.9 copy-done.2
  450.2 0.7 convolution_bitcast_fusion.3
  451.0 21.3 %all_to_all.93 = f32[16,8,896]{2,1,0:T(8,128)S(1)} all-to-all(f32[16,8,896]{2,1,0:T(8,128)S(1)} %convolution_bitcast_fusion.3), channel_id=1, replica_groups=mesh['dp'=16,'mp'=32] {'dp'}, dimensions={0} | all-to-all | bytes 917504 | tf_op jit(solution)/shard_map/all_to_all | solution.py:26
  472.3 0.8 broadcast_in_dim.24
  473.1 3.5 all-to-all-start.15
  476.6 0.9 convolution_multiply_fusion
  477.5 14.4 %all-to-all-done.15 = f32[16,8,896]{2,1,0:T(8,128)S(1)} async-done(((f32[16,8,896]{2,1,0:T(8,128)}), f32[16,8,896]{2,1,0:T(8,128)S(1)}, u32[]{:S(2)}, u32[]{:S(2)}) %all-to-all-start.15) | async-done | bytes 458784 | tf_op jit(solution)/shard_map/all_to_all | solution.py:26
  491.9 0.8 copy.39
  (49 shorter events, 2.5 us)
Async XLA Ops:
  0.6 50.1 %copy-start = (bf16[2048,256]{1,0:T(8,128)(2,1)S(1)}, bf16[2048,256]{1,0:T(8,128)(2,1)}, u32[]{:S(2)}) copy-start(bf16[2048,256]{1,0:T(8,128)(2,1)} %param.6) | copy-start | bytes 3145732
  74.9 11.9 %all-to-all-start.3 = ((f32[16,16,128]{2,1,0:T(8,128)}), f32[16,16,128]{2,1,0:T(8,128)S(1)}, u32[]{:S(2)}, u32[]{:S(2)}) async-start(f32[16,16,128]{2,1,0:T(8,128)} %broadcast_in_dim.18), calls=%async_computation.3 | async-start | bytes 262144 | tf_op jit(solution)/shard_map/all_to_all | solution.py:26
  183.6 2.0 copy-start.1
  448.2 2.0 copy-start.2
  473.1 18.8 %all-to-all-start.15 = ((f32[16,8,896]{2,1,0:T(8,128)}), f32[16,8,896]{2,1,0:T(8,128)S(1)}, u32[]{:S(2)}, u32[]{:S(2)}) async-start(f32[16,8,896]{2,1,0:T(8,128)} %broadcast_in_dim.24), calls=%async_computation.15 | async-start | bytes 917504 | tf_op jit(solution)/shard_map/all_to_all | solution.py:26

commit v2 on v1

--- a/solution.py
+++ b/solution.py
@@ -1,14 +1,60 @@
 import jax
 import jax.numpy as jnp
 from jax import lax
+from jax.experimental import pallas as pl
 from jax.sharding import PartitionSpec as P
 
 H = 8192
-N_MP = 32
+K = 128
+N_X = 4
+N_Y = 8
+N_MP = N_X * N_Y
 N_DP = 16
-K = 128
+X_GROUPS = [[y * N_X + x for x in range(N_X)] for y in range(N_Y)]
+Y_GROUPS = [[y * N_X + x for y in range(N_Y)] for x in range(N_X)]
 HIGHEST = lax.Precision.HIGHEST
 
+def inverse_factor(gram_ref, inverse_ref):
+    groups = [gram_ref[8 * g:8 * g + 8, :] for g in range(K // 8)]
+    lanes = lax.broadcasted_iota(jnp.int32, (1, K), 1)
+    sublanes = lax.broadcasted_iota(jnp.int32, (8, 1), 0)
+    for step in range(K):
+        own, inner = step // 8, step % 8
+        row = groups[own][inner:inner + 1, :]
+        pivot = row[:, step:step + 1]
+        left = jnp.where(lanes == step, 1.0, row)
+        inverse_ref[step:step + 1, :] = jnp.where(lanes > step, 0.0, left) * lax.rsqrt(pivot)
+        scaled = left * (1.0 / pivot)
+        for g in range(own, K // 8):
+            column = groups[g][:, step:step + 1]
+            if g == own:
+                if inner == 7:
+                    continue
+                column = jnp.where(sublanes > inner, column, 0.0)
+                kept = jnp.where((lanes == step) & (sublanes > inner), 0.0, groups[g])
+            else:
+                kept = jnp.where(lanes == step, 0.0, groups[g])
+            groups[g] = kept - column * scaled
+
+
+def normalise_kernel(gram_ref, product_ref, rows_ref, inverse_ref):
+    inverse_factor(gram_ref, inverse_ref)
+    rows = lax.dot_general(
+        product_ref[...], inverse_ref[...], (((1,), (1,)), ((), ())),
+        precision=HIGHEST, preferred_element_type=jnp.float32,
+    )
+    rows_ref[...] = rows.astype(rows_ref.dtype)
+
+
+def normalise(gram, product):
+    tokens = product.shape[0]
+    return pl.pallas_call(
+        normalise_kernel,
+        out_shape=(
+            jax.ShapeDtypeStruct((tokens, K), jnp.bfloat16),
+            jax.ShapeDtypeStruct((K, K), jnp.float32),
+        ),
+    )(gram, product)
 
 def rows_product(left, right):
     return lax.dot_general(
@@ -22,16 +68,16 @@
     return jnp.concatenate([high, low], axis=1)
 
 
-def exchange(blocks, axis):
-    return lax.all_to_all(blocks, axis, 0, 0)
+def exchange(blocks, axis, groups=None):
+    return lax.all_to_all(blocks, axis, 0, 0, axis_index_groups=groups)
 
 
-def scatter_sum(blocks, axis):
-    return jnp.sum(exchange(blocks, axis).astype(jnp.float32), axis=0)
+def scatter_sum(blocks, axis, groups=None):
+    return jnp.sum(exchange(blocks, axis, groups).astype(jnp.float32), axis=0)
 
 
-def gather(block, axis, count):
-    return exchange(jnp.broadcast_to(block[None], (count,) + block.shape), axis)
+def gather(block, axis, count, groups=None):
+    return exchange(jnp.broadcast_to(block[None], (count,) + block.shape), axis, groups)
 
 
 def sum_over_tokens(partial_value):
@@ -48,20 +94,19 @@
     )
     both = jnp.dot(data, split_two(sketch), preferred_element_type=jnp.float32)
     product = both[:, :K] + both[:, K:]
-    span = tokens // N_MP
+    quarter, span = tokens // N_X, tokens // N_MP
     blocks = jnp.concatenate(
-        [product.reshape(N_MP, span, K), gram.reshape(N_MP, K // N_MP, K),
-         jnp.zeros((N_MP, K // N_MP, K), jnp.float32)], axis=1
+        [product.reshape(N_X, quarter, K), jnp.broadcast_to(gram[None], (N_X, K, K))], axis=1
     )
-    whole = gather(scatter_sum(blocks, "mp"), "mp", N_MP)
-    gram = whole[:, span:span + K // N_MP].reshape(K, K)
-    factor = jnp.linalg.cholesky(gram)
-    inverse = lax.linalg.triangular_solve(
-        factor, jnp.eye(K, dtype=jnp.float32), left_side=False, lower=True, transpose_a=True
+    mine = scatter_sum(blocks, "mp", X_GROUPS)
+    blocks = jnp.concatenate(
+        [mine[:quarter].reshape(N_Y, span, K), mine[quarter:].reshape(N_Y, K // N_Y, K)], axis=1
     )
-    product = whole[:, :span].reshape(tokens, K)
-    rows = jnp.dot(product, inverse, precision=HIGHEST, preferred_element_type=jnp.float32)
-    return rows.astype(jnp.bfloat16), inverse
+    mine = gather(scatter_sum(blocks, "mp", Y_GROUPS), "mp", N_Y, Y_GROUPS)
+    rows, inverse = normalise(
+        mine[:, span:].reshape(K, K), mine[:, :span].reshape(quarter, K)
+    )
+    return gather(rows, "mp", N_X, X_GROUPS).reshape(tokens, K), inverse
 
 
 def on_device(activations, output_grads, probe_matrix):
@@ -77,8 +122,9 @@
     power_sketch = sum_over_tokens(rows_product(activations, unit_rows))
     last_rows, inverse = token_rows_of(activations, power_sketch)
     projection = sum_over_tokens(rows_product(last_rows, output_grads))
-    third_basis = jnp.dot(
-        power_sketch, inverse, precision=HIGHEST, preferred_element_type=jnp.float32
+    third_basis = lax.dot_general(
+        power_sketch, inverse, (((1,), (1,)), ((), ())), precision=HIGHEST,
+        preferred_element_type=jnp.float32,
     )
     return (third_basis * jnp.sqrt(jnp.float32(H)), projection)
 

time: 498 us -> 437 us (0.88)
  other arithmetic: 69.9 us -> 1.37 us
  Pallas kernels: 0 us -> 38.2 us
  blocking collectives: 369 us -> 350 us
  waiting for transfers between devices: 22.8 us -> 14.4 us
    another operation x15 -> x0, other arithmetic: 68.6 us -> none  [the longest x9 37.2 us: token_rows_of(): factor = jnp.linalg.cholesky(gram)]
    pallas_call x0 -> x3, Pallas kernels: none -> 38.2 us  [normalise(): pl.pallas_call(normalise_kernel, out_shape=(jax.ShapeDtypeStruct((tokens,...]
    all_to_all x14 -> x21, blocking collectives: 369 us -> 350 us  [exchange(): return lax.all_to_all(blocks, axis, 0, 0, axis_index_groups=groups)]
    all_to_all x2 -> x1, waiting for transfers between devices: 22.8 us -> 14.4 us  [exchange(): return lax.all_to_all(blocks, axis, 0, 0, axis_index_groups=groups)]
  transfers between devices with their start and end apart: 2 -> 1, of which waited for: 2 -> 1; matrix products, arithmetic and copies ran while one was open for 0% -> 0% of each run, Pallas kernels for 0% -> 0%
where the time goes in v2:
time: 437 us; the launch traced here: 436 us
  blocking collectives  350 us (80%)
  Pallas kernels  38.2 us (9%)
  matrix products  16.4 us (4%)
  waiting for transfers between devices  14.4 us (3%)
  local copies, waits for them, and re-layouts  10.7 us (2%)
    all_to_all x21, blocking collectives, exchange(): return lax.all_to_all(blocks, axis, 0, 0, axis_index_groups=groups)  350 us
    pallas_call x3, Pallas kernels, normalise(): pl.pallas_call(normalise_kernel, out_shape=(jax.ShapeDtypeStruct((tokens,...  38.2 us
    all_to_all x1, waiting for transfers between devices, exchange(): return lax.all_to_all(blocks, axis, 0, 0, axis_index_groups=groups)  14.4 us
  transfers between devices with their start and end apart: 1, of which 1 were waited for; matrix products, arithmetic and copies ran while one was open for 0% of the time, Pallas kernels for 0%

profile of v2, /device:TPU:1, one launch (start us, length us, event | category | flops | bytes accessed | tf_op | source)
XLA Modules:
  0.0 435.8 jit_solution(2865917282486706335)
XLA Ops:
  0.6 3.3 convolution_convert_fusion
  3.9 26.6 %all_to_all.110 = bf16[32,64,128]{2,1,0:T(8,128)(2,1)S(1)} all-to-all(bf16[32,64,128]{2,1,0:T(8,128)(2,1)S(1)} %bitcast.102), channel_id=1, replica_groups=mesh['dp'=16,'mp'=32] {'mp'}, dimensions={0} | all-to-all | bytes 1048576 | tf_op jit(solution)/shard_map/all_to_all | solution.py:72
  30.6 0.1 broadcast_in_dim.28
  30.7 20.1 %all_to_all.111 = bf16[32,64,128]{2,1,0:T(8,128)(2,1)S(1)} all-to-all(bf16[32,64,128]{2,1,0:T(8,128)(2,1)S(1)} %broadcast_in_dim.28), channel_id=1, replica_groups=mesh['dp'=16,'mp'=32] {'mp'}, dimensions={0} | all-to-all | bytes 1048576 | tf_op jit(solution)/shard_map/all_to_all | solution.py:72
  50.8 0.4 convolution_bitcast_fusion.5
  51.2 23.0 %all_to_all.112 = f32[16,16,128]{2,1,0:T(8,128)S(1)} all-to-all(f32[16,16,128]{2,1,0:T(8,128)S(1)} %bitcast.115), channel_id=1, replica_groups=mesh['dp'=16,'mp'=32] {'dp'}, dimensions={0} | all-to-all | bytes 262144 | tf_op jit(solution)/shard_map/all_to_all | solution.py:72
  74.3 11.6 %all_to_all.113 = f32[16,16,128]{2,1,0:T(8,128)S(1)} all-to-all(f32[16,16,128]{2,1,0:T(8,128)S(1)} %broadcast_in_dim.29), channel_id=1, replica_groups=mesh['dp'=16,'mp'=32] {'dp'}, dimensions={0} | all-to-all | bytes 262144 | tf_op jit(solution)/shard_map/all_to_all | solution.py:72
  85.9 0.5 convolution_bitcast_fusion.1
  86.4 0.1 slice_add_fusion.2
  86.6 0.4 convolution_bitcast_fusion.8
  87.0 0.1 pad_maximum_fusion
  87.2 21.2 %all_to_all.114 = f32[4,640,128]{1,2,0:T(8,128)S(1)} all-to-all(f32[4,640,128]{1,2,0:T(8,128)S(1)} %pad_maximum_fusion), channel_id=1, replica_groups={{0,1,2,3},{4,5,6,7},{8,9,10,11},{12,13,14,15},{16,17,18,19},{20,21,22,2..., dimensions={0} | all-to-all | bytes 2621440 | tf_op jit(solution)/shard_map/all_to_all | solution.py:72
  108.5 0.1 copy.33
  108.6 0.1 copy.34
  108.7 15.1 %all_to_all.115 = f32[8,80,128]{2,1,0:T(8,128)S(1)} all-to-all(f32[8,80,128]{2,1,0:T(8,128)S(1)} %pad_maximum_fusion.3), channel_id=1, replica_groups={{0,4,8,12,16,20,24,28},{1,5,9,13,17,21,25,29},{2,6,10,14,18,22,26,30},{..., dimensions={0} | all-to-all | bytes 655360 | tf_op jit(solution)/shard_map/all_to_all | solution.py:72
  123.9 13.4 %all_to_all.116 = f32[8,80,128]{2,1,0:T(8,128)S(1)} all-to-all(f32[8,80,128]{2,1,0:T(8,128)S(1)} %broadcast_in_dim.31), channel_id=1, replica_groups={{0,4,8,12,16,20,24,28},{1,5,9,13,17,21,25,29},{2,6,10,14,18,22,26,30},{..., dimensions={0} | all-to-all | bytes 655360 | tf_op jit(solution)/shard_map/all_to_all | solution.py:72
  137.2 0.6 slice.76
  137.8 0.7 slice.77
  138.6 12.7 %shard_map.50 = (bf16[512,128]{1,0:T(8,128)(2,1)}, f32[128,128]{1,0:T(8,128)}) custom-call(f32[128,128]{1,0:T(8,128)} %bitcast.117, f32[512,128]{1,0:T(8,128)} %bitcast.109), custom_call_target="tpu_custom_call" | custom-call | tf_op jit(solution)/shard_map/pallas_call | solution.py:51
  151.3 1.0 broadcast_in_dim.32
  152.3 9.3 %all_to_all.117 = bf16[4,512,128]{2,1,0:T(8,128)(2,1)S(1)} all-to-all(bf16[4,512,128]{2,1,0:T(8,128)(2,1)S(1)} %broadcast_in_dim.32), channel_id=1, replica_groups={{0,1,2,3},{4,5,6,7},{8,9,10,11},{12,13,14,15},{16,17,18,19},{20,21,22,2..., dimensions={0} | all-to-all | bytes 1048576 | tf_op jit(solution)/shard_map/all_to_all | solution.py:72
  161.6 2.8 convolution_bitcast_fusion.3
  164.4 0.2 copy.35
  164.6 22.8 %all_to_all.118 = f32[16,56,128]{2,1,0:T(8,128)S(1)} all-to-all(f32[16,56,128]{2,1,0:T(8,128)S(1)} %bitcast.108), channel_id=1, replica_groups=mesh['dp'=16,'mp'=32] {'dp'}, dimensions={0} | all-to-all | bytes 917504 | tf_op jit(solution)/shard_map/all_to_all | solution.py:72
  187.5 18.6 %all_to_all.119 = f32[16,56,128]{2,1,0:T(8,128)S(1)} all-to-all(f32[16,56,128]{2,1,0:T(8,128)S(1)} %broadcast_in_dim.33), channel_id=1, replica_groups=mesh['dp'=16,'mp'=32] {'dp'}, dimensions={0} | all-to-all | bytes 917504 | tf_op jit(solution)/shard_map/all_to_all | solution.py:72
  206.2 3.4 convolution_bitcast_fusion.2
  209.5 0.1 slice_add_fusion.1
  209.8 0.9 convolution_bitcast_fusion.7
  210.7 0.1 pad_maximum_fusion.1
  210.8 20.0 %all_to_all.120 = f32[4,640,128]{1,2,0:T(8,128)S(1)} all-to-all(f32[4,640,128]{1,2,0:T(8,128)S(1)} %pad_maximum_fusion.1), channel_id=1, replica_groups={{0,1,2,3},{4,5,6,7},{8,9,10,11},{12,13,14,15},{16,17,18,19},{20,21,22,2..., dimensions={0} | all-to-all | bytes 2621440 | tf_op jit(solution)/shard_map/all_to_all | solution.py:72
  230.9 0.1 copy.39
  231.1 0.1 copy.40
  231.2 15.5 %all_to_all.121 = f32[8,80,128]{2,1,0:T(8,128)S(1)} all-to-all(f32[8,80,128]{2,1,0:T(8,128)S(1)} %pad_maximum_fusion.4), channel_id=1, replica_groups={{0,4,8,12,16,20,24,28},{1,5,9,13,17,21,25,29},{2,6,10,14,18,22,26,30},{..., dimensions={0} | all-to-all | bytes 655360 | tf_op jit(solution)/shard_map/all_to_all | solution.py:72
  246.8 13.8 %all_to_all.122 = f32[8,80,128]{2,1,0:T(8,128)S(1)} all-to-all(f32[8,80,128]{2,1,0:T(8,128)S(1)} %broadcast_in_dim.35), channel_id=1, replica_groups={{0,4,8,12,16,20,24,28},{1,5,9,13,17,21,25,29},{2,6,10,14,18,22,26,30},{..., dimensions={0} | all-to-all | bytes 655360 | tf_op jit(solution)/shard_map/all_to_all | solution.py:72
  260.6 0.6 slice.82
  261.2 0.7 slice.83
  261.9 12.7 %shard_map.51 = (bf16[512,128]{1,0:T(8,128)(2,1)}, f32[128,128]{1,0:T(8,128)}) custom-call(f32[128,128]{1,0:T(8,128)} %bitcast.118, f32[512,128]{1,0:T(8,128)} %bitcast.110), custom_call_target="tpu_custom_call" | custom-call | tf_op jit(solution)/shard_map/pallas_call | solution.py:51
  274.6 1.0 broadcast_in_dim.36
  275.6 11.9 %all_to_all.123 = bf16[4,512,128]{2,1,0:T(8,128)(2,1)S(1)} all-to-all(bf16[4,512,128]{2,1,0:T(8,128)(2,1)S(1)} %broadcast_in_dim.36), channel_id=1, replica_groups={{0,1,2,3},{4,5,6,7},{8,9,10,11},{12,13,14,15},{16,17,18,19},{20,21,22,2..., dimensions={0} | all-to-all | bytes 1048576 | tf_op jit(solution)/shard_map/all_to_all | solution.py:72
  287.5 0.4 convolution_bitcast_fusion.4
  287.9 14.2 %all_to_all.124 = f32[16,16,128]{2,1,0:T(8,128)S(1)} all-to-all(f32[16,16,128]{2,1,0:T(8,128)S(1)} %bitcast.116), channel_id=1, replica_groups=mesh['dp'=16,'mp'=32] {'dp'}, dimensions={0} | all-to-all | bytes 262144 | tf_op jit(solution)/shard_map/all_to_all | solution.py:72
  302.2 11.6 %all_to_all.125 = f32[16,16,128]{2,1,0:T(8,128)S(1)} all-to-all(f32[16,16,128]{2,1,0:T(8,128)S(1)} %broadcast_in_dim.37), channel_id=1, replica_groups=mesh['dp'=16,'mp'=32] {'dp'}, dimensions={0} | all-to-all | bytes 262144 | tf_op jit(solution)/shard_map/all_to_all | solution.py:72
  313.8 0.5 convolution_bitcast_fusion
  314.3 0.1 slice_add_fusion
  314.5 0.4 convolution_bitcast_fusion.6
  314.9 0.1 pad_maximum_fusion.2
  315.0 20.8 %all_to_all.126 = f32[4,640,128]{1,2,0:T(8,128)S(1)} all-to-all(f32[4,640,128]{1,2,0:T(8,128)S(1)} %pad_maximum_fusion.2), channel_id=1, replica_groups={{0,1,2,3},{4,5,6,7},{8,9,10,11},{12,13,14,15},{16,17,18,19},{20,21,22,2..., dimensions={0} | all-to-all | bytes 2621440 | tf_op jit(solution)/shard_map/all_to_all | solution.py:72
  335.9 0.1 copy.45
  336.2 15.1 %all_to_all.127 = f32[8,80,128]{2,1,0:T(8,128)S(1)} all-to-all(f32[8,80,128]{2,1,0:T(8,128)S(1)} %pad_maximum_fusion.5), channel_id=1, replica_groups={{0,4,8,12,16,20,24,28},{1,5,9,13,17,21,25,29},{2,6,10,14,18,22,26,30},{..., dimensions={0} | all-to-all | bytes 655360 | tf_op jit(solution)/shard_map/all_to_all | solution.py:72
  351.4 13.7 %all_to_all.128 = f32[8,80,128]{2,1,0:T(8,128)S(1)} all-to-all(f32[8,80,128]{2,1,0:T(8,128)S(1)} %broadcast_in_dim.39), channel_id=1, replica_groups={{0,4,8,12,16,20,24,28},{1,5,9,13,17,21,25,29},{2,6,10,14,18,22,26,30},{..., dimensions={0} | all-to-all | bytes 655360 | tf_op jit(solution)/shard_map/all_to_all | solution.py:72
  365.1 0.6 slice.88
  365.7 0.7 slice.89
  366.4 12.7 %shard_map.52 = (bf16[512,128]{1,0:T(8,128)(2,1)}, f32[128,128]{1,0:T(8,128)}) custom-call(f32[128,128]{1,0:T(8,128)} %bitcast.119, f32[512,128]{1,0:T(8,128)} %bitcast.111), custom_call_target="tpu_custom_call" | custom-call | tf_op jit(solution)/shard_map/pallas_call | solution.py:51
  379.1 1.0 copy.47
  380.2 9.3 %all_to_all.129 = bf16[4,512,128]{1,2,0:T(8,128)(2,1)S(1)} all-to-all(bf16[4,512,128]{1,2,0:T(8,128)(2,1)S(1)} %broadcast_in_dim.40), channel_id=1, replica_groups={{0,1,2,3},{4,5,6,7},{8,9,10,11},{12,13,14,15},{16,17,18,19},{20,21,22,2..., dimensions={0} | all-to-all | bytes 1048576 | tf_op jit(solution)/shard_map/all_to_all | solution.py:72
  389.5 0.3 copy.48
  389.8 0.2 copy.49
  390.0 2.8 fusion
  392.8 22.7 %all_to_all.130 = f32[16,8,896]{2,1,0:T(8,128)S(1)} all-to-all(f32[16,8,896]{2,1,0:T(8,128)S(1)} %fusion), channel_id=1, replica_groups=mesh['dp'=16,'mp'=32] {'dp'}, dimensions={0} | all-to-all | bytes 917504 | tf_op jit(solution)/shard_map/all_to_all | solution.py:72
  415.5 0.8 broadcast_in_dim.41
  416.3 3.5 all-to-all-start.21
  419.8 0.9 convolution_multiply_fusion
  420.7 14.4 %all-to-all-done.21 = f32[16,8,896]{2,1,0:T(8,128)S(1)} async-done(((f32[16,8,896]{2,1,0:T(8,128)}), f32[16,8,896]{2,1,0:T(8,128)S(1)}, u32[]{:S(2)}, u32[]{:S(2)}) %all-to-all-start.21) | async-done | bytes 458784 | tf_op jit(solution)/shard_map/all_to_all | solution.py:72
  435.1 0.8 copy.75
  (44 shorter events, 1.5 us)
Async XLA Ops:
  0.6 50.1 %copy-start = (bf16[2048,256]{1,0:T(8,128)(2,1)S(1)}, bf16[2048,256]{1,0:T(8,128)(2,1)}, u32[]{:S(2)}) copy-start(bf16[2048,256]{1,0:T(8,128)(2,1)} %param.3) | copy-start | bytes 3145732
  392.8 27.0 %copy-start.1 = (f32[128,128]{1,0:T(8,128)S(1)}, f32[128,128]{1,0:T(8,128)}, u32[]{:S(2)}) copy-start(f32[128,128]{1,0:T(8,128)} %get-tuple-element.8) | copy-start | bytes 196612
  416.3 18.8 %all-to-all-start.21 = ((f32[16,8,896]{2,1,0:T(8,128)}), f32[16,8,896]{2,1,0:T(8,128)S(1)}, u32[]{:S(2)}, u32[]{:S(2)}) async-start(f32[16,8,896]{2,1,0:T(8,128)} %broadcast_in_dim.41), calls=%async_computation.21 | async-start | bytes 917504 | tf_op jit(solution)/shard_map/all_to_all | solution.py:72

commit v3 on v2

--- a/solution.py
+++ b/solution.py
@@ -2,6 +2,7 @@
 import jax.numpy as jnp
 from jax import lax
 from jax.experimental import pallas as pl
+from jax.experimental.pallas import tpu as pltpu
 from jax.sharding import PartitionSpec as P
 
 H = 8192
@@ -14,47 +15,77 @@
 Y_GROUPS = [[y * N_X + x for y in range(N_Y)] for x in range(N_X)]
 HIGHEST = lax.Precision.HIGHEST
 
-def inverse_factor(gram_ref, inverse_ref):
-    groups = [gram_ref[8 * g:8 * g + 8, :] for g in range(K // 8)]
-    lanes = lax.broadcasted_iota(jnp.int32, (1, K), 1)
-    sublanes = lax.broadcasted_iota(jnp.int32, (8, 1), 0)
-    for step in range(K):
-        own, inner = step // 8, step % 8
-        row = groups[own][inner:inner + 1, :]
-        pivot = row[:, step:step + 1]
-        left = jnp.where(lanes == step, 1.0, row)
-        inverse_ref[step:step + 1, :] = jnp.where(lanes > step, 0.0, left) * lax.rsqrt(pivot)
-        scaled = left * (1.0 / pivot)
-        for g in range(own, K // 8):
-            column = groups[g][:, step:step + 1]
-            if g == own:
-                if inner == 7:
-                    continue
-                column = jnp.where(sublanes > inner, column, 0.0)
-                kept = jnp.where((lanes == step) & (sublanes > inner), 0.0, groups[g])
-            else:
-                kept = jnp.where(lanes == step, 0.0, groups[g])
-            groups[g] = kept - column * scaled
+
+def spread(value):
+    return jnp.broadcast_to(value, (8, K))
 
 
-def normalise_kernel(gram_ref, product_ref, rows_ref, inverse_ref):
-    inverse_factor(gram_ref, inverse_ref)
-    rows = lax.dot_general(
-        product_ref[...], inverse_ref[...], (((1,), (1,)), ((), ())),
-        precision=HIGHEST, preferred_element_type=jnp.float32,
-    )
-    rows_ref[...] = rows.astype(rows_ref.dtype)
+def inverse_factor(groups, inverse_ref):
+    lanes = lax.broadcasted_iota(jnp.int32, (8, K), 1)
+    for own in range(K // 8):
+        first = 8 * own
+        rows = [spread(groups[own][j:j + 1, :]) for j in range(8)]
+        inner = [
+            [spread(rows[i][:, first + j:first + j + 1]) for j in range(i + 1)] for i in range(8)
+        ]
+        factor = [[None] * 8 for _ in range(8)]
+        inverse_pivots = []
+        for j in range(8):
+            inverse_pivots.append(1.0 / inner[j][j])
+            for i in range(j + 1, 8):
+                factor[i][j] = inner[i][j] * inverse_pivots[j]
+            for i in range(j + 1, 8):
+                for m in range(j + 1, i + 1):
+                    inner[i][m] = inner[i][m] - factor[i][j] * inner[m][j]
+        inside = (lanes >= first) & (lanes < first + 8)
+        done = []
+        for j in range(8):
+            row = jnp.where(inside, jnp.where(lanes == first + j, 1.0, 0.0), rows[j])
+            for m in range(j):
+                row = row - factor[j][m] * done[m]
+            done.append(row)
+            scaled = jnp.where(lanes > first + j, 0.0, row * lax.rsqrt(inner[j][j]))
+            inverse_ref[first + j:first + j + 1, :] = scaled[0:1, :]
+        for g in range(own + 1, K // 8):
+            kept = jnp.where(inside, 0.0, groups[g])
+            columns = []
+            for j in range(8):
+                column = spread(groups[g][:, first + j:first + j + 1])
+                for m in range(j):
+                    column = column - columns[m] * factor[j][m]
+                columns.append(column)
+            for j in range(8):
+                kept = kept - (columns[j] * inverse_pivots[j]) * done[j]
+            groups[g] = kept
 
 
-def normalise(gram, product):
-    tokens = product.shape[0]
+def normalise_kernel(pieces_ref, rows_ref, inverse_ref):
+    span = pieces_ref.shape[1] - K // N_Y
+    groups = []
+    for y in range(N_Y):
+        for start in range(span, pieces_ref.shape[1], 8):
+            groups.append(pieces_ref[y, start:start + 8, :])
+    inverse_factor(groups, inverse_ref)
+    for y in range(N_Y):
+        rows = lax.dot_general(
+            pieces_ref[y, :span, :], inverse_ref[...], (((1,), (1,)), ((), ())),
+            precision=HIGHEST, preferred_element_type=jnp.float32,
+        ).astype(rows_ref.dtype)
+        for x in range(N_X):
+            rows_ref[x, span * y:span * (y + 1), :] = rows
+
+
+def normalise(pieces):
+    span = pieces.shape[1] - K // N_Y
     return pl.pallas_call(
         normalise_kernel,
         out_shape=(
-            jax.ShapeDtypeStruct((tokens, K), jnp.bfloat16),
+            jax.ShapeDtypeStruct((N_X, N_Y * span, K), jnp.bfloat16),
             jax.ShapeDtypeStruct((K, K), jnp.float32),
         ),
-    )(gram, product)
+        compiler_params=pltpu.CompilerParams(vmem_limit_bytes=16 << 20),
+    )(pieces)
+
 
 def rows_product(left, right):
     return lax.dot_general(
@@ -83,6 +114,8 @@
 def sum_over_tokens(partial_value):
     rows, columns = partial_value.shape
     mine = scatter_sum(partial_value.reshape(N_DP, rows // N_DP, columns), "dp")
+    if mine.size * 4 * N_DP > 1 << 18:
+        return lax.all_gather(mine, "dp", tiled=True)
     return gather(mine, "dp", N_DP).reshape(rows, columns)
 
 
@@ -103,10 +136,8 @@
         [mine[:quarter].reshape(N_Y, span, K), mine[quarter:].reshape(N_Y, K // N_Y, K)], axis=1
     )
     mine = gather(scatter_sum(blocks, "mp", Y_GROUPS), "mp", N_Y, Y_GROUPS)
-    rows, inverse = normalise(
-        mine[:, span:].reshape(K, K), mine[:, :span].reshape(quarter, K)
-    )
-    return gather(rows, "mp", N_X, X_GROUPS).reshape(tokens, K), inverse
+    rows, inverse = normalise(mine)
+    return exchange(rows, "mp", X_GROUPS).reshape(tokens, K), inverse
 
 
 def on_device(activations, output_grads, probe_matrix):
@@ -121,7 +152,9 @@
     unit_rows, _ = token_rows_of(output_grads, back_sketch)
     power_sketch = sum_over_tokens(rows_product(activations, unit_rows))
     last_rows, inverse = token_rows_of(activations, power_sketch)
-    projection = sum_over_tokens(rows_product(last_rows, output_grads))
+    partial_value = rows_product(last_rows, output_grads).reshape(N_DP, K // N_DP, -1)
+    mine = scatter_sum(partial_value, "dp").astype(jnp.bfloat16)
+    projection = lax.all_gather(mine, "dp", tiled=True).astype(jnp.float32)
     third_basis = lax.dot_general(
         power_sketch, inverse, (((1,), (1,)), ((), ())), precision=HIGHEST,
         preferred_element_type=jnp.float32,

time: 437 us -> 403 us (0.922)
  Pallas kernels: 38.2 us -> 17.2 us
  blocking collectives: 350 us -> 340 us
  local copies, waits for them, and re-layouts: 10.7 us -> 1.82 us
    all_to_all x21 -> x19, blocking collectives: 350 us -> 309 us  [exchange(): return lax.all_to_all(blocks, axis, 0, 0, axis_index_groups=groups)]
    all_gather x0 -> x2, blocking collectives: none -> 31 us  [the longest x1 15.9 us: sum_over_tokens(): return lax.all_gather(mine, 'dp', tiled=True)]
    pallas_call x3, Pallas kernels: 38.2 us -> 17.2 us  [normalise(): pl.pallas_call(normalise_kernel, out_shape=(jax.ShapeDtypeStruct((N_X, N_...]
where the time goes in v3:
time: 403 us; the launch traced here: 402 us
  blocking collectives  340 us (84%)
  matrix products  17.2 us (4%)
  Pallas kernels  17.2 us (4%)
  waiting for transfers between devices  15.1 us (4%)
  starting transfers between devices  7.45 us (2%)
    all_to_all x19, blocking collectives, exchange(): return lax.all_to_all(blocks, axis, 0, 0, axis_index_groups=groups)  309 us
    pallas_call x3, Pallas kernels, normalise(): pl.pallas_call(normalise_kernel, out_shape=(jax.ShapeDtypeStruct((N_X, N_...  17.2 us
    all_gather x1, blocking collectives, sum_over_tokens(): return lax.all_gather(mine, 'dp', tiled=True)  15.9 us
    all_gather x1, blocking collectives, on_device(): projection = lax.all_gather(mine, 'dp', tiled=True).astype(jnp.float32)  15.1 us
    all_to_all x1, waiting for transfers between devices, exchange(): return lax.all_to_all(blocks, axis, 0, 0, axis_index_groups=groups)  15.1 us
  transfers between devices with their start and end apart: 1, of which 1 were waited for; matrix products, arithmetic and copies ran while one was open for 0% of the time, Pallas kernels for 0%

profile of v3, /device:TPU:1, one launch (start us, length us, event | category | flops | bytes accessed | tf_op | source)
XLA Modules:
  0.0 401.9 jit_solution(18134886412946544771)
XLA Ops:
  0.6 3.3 convolution_convert_fusion
  3.9 26.6 %all_to_all.100 = bf16[32,64,128]{2,1,0:T(8,128)(2,1)S(1)} all-to-all(bf16[32,64,128]{2,1,0:T(8,128)(2,1)S(1)} %bitcast.87), channel_id=1, replica_groups=mesh['dp'=16,'mp'=32] {'mp'}, dimensions={0} | all-to-all | bytes 1048576 | tf_op jit(solution)/shard_map/all_to_all | solution.py:103
  30.5 0.1 reduce_sum.102
  30.6 0.1 broadcast_in_dim.18
  30.7 20.1 %all_to_all.101 = bf16[32,64,128]{2,1,0:T(8,128)(2,1)S(1)} all-to-all(bf16[32,64,128]{2,1,0:T(8,128)(2,1)S(1)} %broadcast_in_dim.18), channel_id=1, replica_groups=mesh['dp'=16,'mp'=32] {'mp'}, dimensions={0} | all-to-all | bytes 1048576 | tf_op jit(solution)/shard_map/all_to_all | solution.py:103
  50.8 0.4 convolution_bitcast_fusion.5
  51.1 0.1 copy.29
  51.2 23.0 %all_to_all.102 = f32[16,16,128]{2,1,0:T(8,128)S(1)} all-to-all(f32[16,16,128]{2,1,0:T(8,128)S(1)} %bitcast.96), channel_id=1, replica_groups=mesh['dp'=16,'mp'=32] {'dp'}, dimensions={0} | all-to-all | bytes 262144 | tf_op jit(solution)/shard_map/all_to_all | solution.py:103
  74.3 11.6 %all_to_all.103 = f32[16,16,128]{2,1,0:T(8,128)S(1)} all-to-all(f32[16,16,128]{2,1,0:T(8,128)S(1)} %broadcast_in_dim.19), channel_id=1, replica_groups=mesh['dp'=16,'mp'=32] {'dp'}, dimensions={0} | all-to-all | bytes 262144 | tf_op jit(solution)/shard_map/all_to_all | solution.py:103
  85.9 0.5 convolution_bitcast_fusion.1
  86.4 0.1 slice_add_fusion.2
  86.5 0.1 copy.70
  86.6 0.4 convolution_bitcast_fusion.7
  87.0 0.1 pad_maximum_fusion
  87.2 21.2 %all_to_all.104 = f32[4,640,128]{1,2,0:T(8,128)S(1)} all-to-all(f32[4,640,128]{1,2,0:T(8,128)S(1)} %pad_maximum_fusion), channel_id=1, replica_groups={{0,1,2,3},{4,5,6,7},{8,9,10,11},{12,13,14,15},{16,17,18,19},{20,21,22,2..., dimensions={0} | all-to-all | bytes 2621440 | tf_op jit(solution)/shard_map/all_to_all | solution.py:103
  108.3 0.1 reduce_sum.104
  108.5 0.1 copy.33
  108.6 0.1 copy.34
  108.7 15.1 %all_to_all.105 = f32[8,80,128]{2,1,0:T(8,128)S(1)} all-to-all(f32[8,80,128]{2,1,0:T(8,128)S(1)} %pad_maximum_fusion.3), channel_id=1, replica_groups={{0,4,8,12,16,20,24,28},{1,5,9,13,17,21,25,29},{2,6,10,14,18,22,26,30},{..., dimensions={0} | all-to-all | bytes 655360 | tf_op jit(solution)/shard_map/all_to_all | solution.py:103
  123.9 13.4 %all_to_all.106.pieces_ref = f32[8,80,128]{2,1,0:T(8,128)S(1)} all-to-all(f32[8,80,128]{2,1,0:T(8,128)S(1)} %broadcast_in_dim.21), channel_id=1, replica_groups={{0,4,8,12,16,20,24,28},{1,5,9,13,17,21,25,29},{2,6,10,14,18,22,26,30},{..., dimensions={0} | all-to-all | bytes 655360 | tf_op jit(solution)/shard_map/all_to_all | solution.py:103
  137.2 5.7 %shard_map.50 = (bf16[4,512,128]{2,1,0:T(8,128)(2,1)S(1)}, f32[128,128]{1,0:T(8,128)}) custom-call(f32[8,80,128]{2,1,0:T(8,128)S(1)} %all_to_all.106.pieces_ref), custom_call_target="tpu_custom_call" | custom-call | tf_op jit(solution)/shard_map/pallas_call | solution.py:80
  142.9 9.3 %all_to_all.107 = bf16[4,512,128]{2,1,0:T(8,128)(2,1)S(1)} all-to-all(bf16[4,512,128]{2,1,0:T(8,128)(2,1)S(1)} %get-tuple-element.6), channel_id=1, replica_groups={{0,1,2,3},{4,5,6,7},{8,9,10,11},{12,13,14,15},{16,17,18,19},{20,21,22,2..., dimensions={0} | all-to-all | bytes 1048576 | tf_op jit(solution)/shard_map/all_to_all | solution.py:103
  152.3 2.8 convolution_bitcast_fusion.3
  155.1 0.2 copy.35
  155.3 22.8 %all_to_all.108 = f32[16,56,128]{2,1,0:T(8,128)S(1)} all-to-all(f32[16,56,128]{2,1,0:T(8,128)S(1)} %bitcast.92), channel_id=1, replica_groups=mesh['dp'=16,'mp'=32] {'dp'}, dimensions={0} | all-to-all | bytes 917504 | tf_op jit(solution)/shard_map/all_to_all | solution.py:103
  178.1 15.9 %all_gather.6 = f32[896,128]{1,0:T(8,128)S(1)} all-gather(f32[56,128]{1,0:T(8,128)S(1)} %reduce_sum.106), channel_id=1, replica_groups=mesh['dp'=16,'mp'=32] {'dp'}, dimensions={0}, use_global_device_ids=true | all-gather | bytes 487424 | tf_op jit(solution)/shard_map/all_gather | solution.py:118
  194.0 0.9 fusion.16
  194.9 0.1 subtract_convert_fusion
  195.0 3.4 convolution_bitcast_fusion.2
  198.4 0.1 slice_add_fusion.1
  198.5 0.1 copy.69
  198.6 0.1 pad_maximum_fusion.1
  198.7 20.1 %all_to_all.109 = f32[4,640,128]{1,2,0:T(8,128)S(1)} all-to-all(f32[4,640,128]{1,2,0:T(8,128)S(1)} %pad_maximum_fusion.1), channel_id=1, replica_groups={{0,1,2,3},{4,5,6,7},{8,9,10,11},{12,13,14,15},{16,17,18,19},{20,21,22,2..., dimensions={0} | all-to-all | bytes 2621440 | tf_op jit(solution)/shard_map/all_to_all | solution.py:103
  218.8 0.1 reduce_sum.107
  218.9 0.1 copy.39
  219.0 0.1 copy.40
  219.2 13.4 %all_to_all.110 = f32[8,80,128]{2,1,0:T(8,128)S(1)} all-to-all(f32[8,80,128]{2,1,0:T(8,128)S(1)} %pad_maximum_fusion.4), channel_id=1, replica_groups={{0,4,8,12,16,20,24,28},{1,5,9,13,17,21,25,29},{2,6,10,14,18,22,26,30},{..., dimensions={0} | all-to-all | bytes 655360 | tf_op jit(solution)/shard_map/all_to_all | solution.py:103
  232.6 13.2 %all_to_all.111.pieces_ref = f32[8,80,128]{2,1,0:T(8,128)S(1)} all-to-all(f32[8,80,128]{2,1,0:T(8,128)S(1)} %broadcast_in_dim.23), channel_id=1, replica_groups={{0,4,8,12,16,20,24,28},{1,5,9,13,17,21,25,29},{2,6,10,14,18,22,26,30},{..., dimensions={0} | all-to-all | bytes 655360 | tf_op jit(solution)/shard_map/all_to_all | solution.py:103
  245.8 5.7 %shard_map.51 = (bf16[4,512,128]{2,1,0:T(8,128)(2,1)S(1)}, f32[128,128]{1,0:T(8,128)}) custom-call(f32[8,80,128]{2,1,0:T(8,128)S(1)} %all_to_all.111.pieces_ref), custom_call_target="tpu_custom_call" | custom-call | tf_op jit(solution)/shard_map/pallas_call | solution.py:80
  251.6 9.3 %all_to_all.112 = bf16[4,512,128]{2,1,0:T(8,128)(2,1)S(1)} all-to-all(bf16[4,512,128]{2,1,0:T(8,128)(2,1)S(1)} %get-tuple-element.7), channel_id=1, replica_groups={{0,1,2,3},{4,5,6,7},{8,9,10,11},{12,13,14,15},{16,17,18,19},{20,21,22,2..., dimensions={0} | all-to-all | bytes 1048576 | tf_op jit(solution)/shard_map/all_to_all | solution.py:103
  260.9 0.4 convolution_bitcast_fusion.4
  261.2 0.1 copy.41
  261.3 19.4 %all_to_all.113 = f32[16,16,128]{2,1,0:T(8,128)S(1)} all-to-all(f32[16,16,128]{2,1,0:T(8,128)S(1)} %bitcast.97), channel_id=1, replica_groups=mesh['dp'=16,'mp'=32] {'dp'}, dimensions={0} | all-to-all | bytes 262144 | tf_op jit(solution)/shard_map/all_to_all | solution.py:103
  280.8 11.6 %all_to_all.114 = f32[16,16,128]{2,1,0:T(8,128)S(1)} all-to-all(f32[16,16,128]{2,1,0:T(8,128)S(1)} %broadcast_in_dim.24), channel_id=1, replica_groups=mesh['dp'=16,'mp'=32] {'dp'}, dimensions={0} | all-to-all | bytes 262144 | tf_op jit(solution)/shard_map/all_to_all | solution.py:103
  292.4 0.5 convolution_bitcast_fusion
  292.9 0.1 slice_add_fusion
  293.1 0.1 copy.68
  293.1 0.4 convolution_bitcast_fusion.6
  293.6 0.1 pad_maximum_fusion.2
  293.7 20.8 %all_to_all.115 = f32[4,640,128]{1,2,0:T(8,128)S(1)} all-to-all(f32[4,640,128]{1,2,0:T(8,128)S(1)} %pad_maximum_fusion.2), channel_id=1, replica_groups={{0,1,2,3},{4,5,6,7},{8,9,10,11},{12,13,14,15},{16,17,18,19},{20,21,22,2..., dimensions={0} | all-to-all | bytes 2621440 | tf_op jit(solution)/shard_map/all_to_all | solution.py:103
  314.4 0.1 reduce_sum.110
  314.6 0.1 copy.45
  314.7 0.1 copy.46
  314.8 15.1 %all_to_all.116 = f32[8,80,128]{2,1,0:T(8,128)S(1)} all-to-all(f32[8,80,128]{2,1,0:T(8,128)S(1)} %pad_maximum_fusion.5), channel_id=1, replica_groups={{0,4,8,12,16,20,24,28},{1,5,9,13,17,21,25,29},{2,6,10,14,18,22,26,30},{..., dimensions={0} | all-to-all | bytes 655360 | tf_op jit(solution)/shard_map/all_to_all | solution.py:103
  330.0 13.7 %all_to_all.117.pieces_ref = f32[8,80,128]{2,1,0:T(8,128)S(1)} all-to-all(f32[8,80,128]{2,1,0:T(8,128)S(1)} %broadcast_in_dim.26), channel_id=1, replica_groups={{0,4,8,12,16,20,24,28},{1,5,9,13,17,21,25,29},{2,6,10,14,18,22,26,30},{..., dimensions={0} | all-to-all | bytes 655360 | tf_op jit(solution)/shard_map/all_to_all | solution.py:103
  343.7 5.7 %shard_map.52 = (bf16[4,512,128]{2,1,0:T(8,128)(2,1)S(1)}, f32[128,128]{1,0:T(8,128)S(1)}) custom-call(f32[8,80,128]{2,1,0:T(8,128)S(1)} %all_to_all.117.pieces_ref), custom_call_target="tpu_custom_call" | custom-call | tf_op jit(solution)/shard_map/pallas_call | solution.py:80
  349.4 9.3 %all_to_all.118 = bf16[4,512,128]{2,1,0:T(8,128)(2,1)S(1)} all-to-all(bf16[4,512,128]{2,1,0:T(8,128)(2,1)S(1)} %get-tuple-element.9), channel_id=1, replica_groups={{0,1,2,3},{4,5,6,7},{8,9,10,11},{12,13,14,15},{16,17,18,19},{20,21,22,2..., dimensions={0} | all-to-all | bytes 1048576 | tf_op jit(solution)/shard_map/all_to_all | solution.py:103
  358.8 0.2 copy.47
  359.0 3.5 fusion
  362.5 7.4 %all-to-all-start.19 = ((f32[16,8,896]{2,1,0:T(8,128)}), f32[16,8,896]{2,1,0:T(8,128)S(1)}, u32[]{:S(2)}, u32[]{:S(2)}) async-start(f32[16,8,896]{2,1,0:T(8,128)} %fusion), calls=%async_computation.19 | async-start | bytes 917504 | tf_op jit(solution)/shard_map/all_to_all | solution.py:103
  370.0 0.9 convolution_multiply_fusion
  370.9 15.1 %all-to-all-done.19 = f32[16,8,896]{2,1,0:T(8,128)S(1)} async-done(((f32[16,8,896]{2,1,0:T(8,128)}), f32[16,8,896]{2,1,0:T(8,128)S(1)}, u32[]{:S(2)}, u32[]{:S(2)}) %all-to-all-start.19) | async-done | bytes 458784 | tf_op jit(solution)/shard_map/all_to_all | solution.py:103
  386.0 15.1 %all_gather.7 = bf16[128,896]{1,0:T(8,128)(2,1)S(1)} all-gather(bf16[8,896]{1,0:T(8,128)(2,1)S(1)} %reduce_sum.112), channel_id=1, replica_groups=mesh['dp'=16,'mp'=32] {'dp'}, dimensions={0}, use_global_device_ids=true | all-gather | bytes 243712 | tf_op jit(solution)/shard_map/all_gather | solution.py:157
  401.1 0.8 convert_element_type.49
  (29 shorter events, 0.5 us)
Async XLA Ops:
  0.6 50.1 %copy-start = (bf16[2048,256]{1,0:T(8,128)(2,1)S(1)}, bf16[2048,256]{1,0:T(8,128)(2,1)}, u32[]{:S(2)}) copy-start(bf16[2048,256]{1,0:T(8,128)(2,1)} %param.3) | copy-start | bytes 3145732
  362.5 23.4 %all-to-all-start.19 = ((f32[16,8,896]{2,1,0:T(8,128)}), f32[16,8,896]{2,1,0:T(8,128)S(1)}, u32[]{:S(2)}, u32[]{:S(2)}) async-start(f32[16,8,896]{2,1,0:T(8,128)} %fusion), calls=%async_computation.19 | async-start | bytes 917504 | tf_op jit(solution)/shard_map/all_to_all | solution.py:103

commit v4 on v3

--- a/solution.py
+++ b/solution.py
@@ -10,9 +10,13 @@
 N_X = 4
 N_Y = 8
 N_MP = N_X * N_Y
-N_DP = 16
+N_CORE = 2
+N_Z = 8
+N_DP = N_Z * N_CORE
 X_GROUPS = [[y * N_X + x for x in range(N_X)] for y in range(N_Y)]
 Y_GROUPS = [[y * N_X + x for y in range(N_Y)] for x in range(N_X)]
+CORE_GROUPS = [[z * N_CORE + core for core in range(N_CORE)] for z in range(N_Z)]
+Z_GROUPS = [[z * N_CORE + core for z in range(N_Z)] for core in range(N_CORE)]
 HIGHEST = lax.Precision.HIGHEST
 
 
@@ -114,9 +118,16 @@
 def sum_over_tokens(partial_value):
     rows, columns = partial_value.shape
     mine = scatter_sum(partial_value.reshape(N_DP, rows // N_DP, columns), "dp")
-    if mine.size * 4 * N_DP > 1 << 18:
-        return lax.all_gather(mine, "dp", tiled=True)
     return gather(mine, "dp", N_DP).reshape(rows, columns)
+
+
+def staged_sum_over_tokens(partial_value, held_as):
+    rows, columns = partial_value.shape
+    half = rows // N_CORE
+    mine = scatter_sum(partial_value.reshape(N_CORE, half, columns), "dp", CORE_GROUPS)
+    mine = scatter_sum(mine.reshape(N_Z, half // N_Z, columns), "dp", Z_GROUPS)
+    mine = gather(mine.astype(held_as), "dp", N_Z, Z_GROUPS).reshape(half, columns)
+    return lax.all_gather(mine, "dp", axis_index_groups=CORE_GROUPS, tiled=True)
 
 
 def token_rows_of(data, sketch):
@@ -148,18 +159,16 @@
 
     sketch = sum_over_tokens(rows_product(activations, probe_rows))
     token_rows, _ = token_rows_of(activations, sketch)
-    back_sketch = sum_over_tokens(rows_product(output_grads, token_rows))
+    back_sketch = staged_sum_over_tokens(rows_product(output_grads, token_rows), jnp.float32)
     unit_rows, _ = token_rows_of(output_grads, back_sketch)
     power_sketch = sum_over_tokens(rows_product(activations, unit_rows))
     last_rows, inverse = token_rows_of(activations, power_sketch)
-    partial_value = rows_product(last_rows, output_grads).reshape(N_DP, K // N_DP, -1)
-    mine = scatter_sum(partial_value, "dp").astype(jnp.bfloat16)
-    projection = lax.all_gather(mine, "dp", tiled=True).astype(jnp.float32)
+    projection = staged_sum_over_tokens(rows_product(last_rows, output_grads), jnp.bfloat16)
     third_basis = lax.dot_general(
         power_sketch, inverse, (((1,), (1,)), ((), ())), precision=HIGHEST,
         preferred_element_type=jnp.float32,
     )
-    return (third_basis * jnp.sqrt(jnp.float32(H)), projection)
+    return (third_basis * jnp.sqrt(jnp.float32(H)), projection.astype(jnp.float32))
 
 
 def solution(mesh):

time: 403 us -> 398 us (0.988)
  waiting for transfers between devices: 15.1 us -> 6.62 us
  blocking collectives: 340 us -> 348 us
  starting transfers between devices: 7.45 us -> 3.37 us
    all_to_all x19 -> x23, blocking collectives: 309 us -> 341 us  [exchange(): return lax.all_to_all(blocks, axis, 0, 0, axis_index_groups=groups)]
    all_gather x2, blocking collectives: 31 us -> 7.26 us  [staged_sum_over_tokens(): return lax.all_gather(mine, 'dp', axis_index_groups=CORE_GROUPS, tiled=True)]
    all_to_all x1, waiting for transfers between devices: 15.1 us -> 6.62 us  [exchange(): return lax.all_to_all(blocks, axis, 0, 0, axis_index_groups=groups)]
    all_to_all x1, starting transfers between devices: 7.45 us -> 3.37 us  [exchange(): return lax.all_to_all(blocks, axis, 0, 0, axis_index_groups=groups)]
where the time goes in v4:
time: 398 us; the launch traced here: 397 us
  blocking collectives  348 us (87%)
  Pallas kernels  17.2 us (4%)
  matrix products  16.4 us (4%)
  waiting for transfers between devices  6.62 us (2%)
    all_to_all x23, blocking collectives, exchange(): return lax.all_to_all(blocks, axis, 0, 0, axis_index_groups=groups)  341 us
    pallas_call x3, Pallas kernels, normalise(): pl.pallas_call(normalise_kernel, out_shape=(jax.ShapeDtypeStruct((N_X, N_...  17.2 us
  transfers between devices with their start and end apart: 1, of which 1 were waited for; matrix products, arithmetic and copies ran while one was open for 0% of the time, Pallas kernels for 0%

profile of v4, /device:TPU:1, one launch (start us, length us, event | category | flops | bytes accessed | tf_op | source)
XLA Modules:
  0.0 397.3 jit_solution(12690046871386008095)
XLA Ops:
  0.6 3.3 convolution_convert_fusion
  3.9 26.6 %all_to_all.120 = bf16[32,64,128]{2,1,0:T(8,128)(2,1)S(1)} all-to-all(bf16[32,64,128]{2,1,0:T(8,128)(2,1)S(1)} %bitcast.90), channel_id=1, replica_groups=mesh['dp'=16,'mp'=32] {'mp'}, dimensions={0} | all-to-all | bytes 1048576 | tf_op jit(solution)/shard_map/all_to_all | solution.py:107
  30.5 0.1 reduce_sum.120
  30.6 0.1 broadcast_in_dim.22
  30.7 20.1 %all_to_all.121 = bf16[32,64,128]{2,1,0:T(8,128)(2,1)S(1)} all-to-all(bf16[32,64,128]{2,1,0:T(8,128)(2,1)S(1)} %broadcast_in_dim.22), channel_id=1, replica_groups=mesh['dp'=16,'mp'=32] {'mp'}, dimensions={0} | all-to-all | bytes 1048576 | tf_op jit(solution)/shard_map/all_to_all | solution.py:107
  50.8 0.4 convolution_bitcast_fusion.5
  51.2 23.0 %all_to_all.122 = f32[16,16,128]{2,1,0:T(8,128)S(1)} all-to-all(f32[16,16,128]{2,1,0:T(8,128)S(1)} %bitcast.103), channel_id=1, replica_groups=mesh['dp'=16,'mp'=32] {'dp'}, dimensions={0} | all-to-all | bytes 262144 | tf_op jit(solution)/shard_map/all_to_all | solution.py:107
  74.3 11.6 %all_to_all.123 = f32[16,16,128]{2,1,0:T(8,128)S(1)} all-to-all(f32[16,16,128]{2,1,0:T(8,128)S(1)} %broadcast_in_dim.23), channel_id=1, replica_groups=mesh['dp'=16,'mp'=32] {'dp'}, dimensions={0} | all-to-all | bytes 262144 | tf_op jit(solution)/shard_map/all_to_all | solution.py:107
  85.9 0.5 convolution_bitcast_fusion.1
  86.4 0.1 slice_add_fusion.2
  86.6 0.4 convolution_bitcast_fusion.7
  87.0 0.1 pad_maximum_fusion
  87.2 21.2 %all_to_all.124 = f32[4,640,128]{1,2,0:T(8,128)S(1)} all-to-all(f32[4,640,128]{1,2,0:T(8,128)S(1)} %pad_maximum_fusion), channel_id=1, replica_groups={{0,1,2,3},{4,5,6,7},{8,9,10,11},{12,13,14,15},{16,17,18,19},{20,21,22,2..., dimensions={0} | all-to-all | bytes 2621440 | tf_op jit(solution)/shard_map/all_to_all | solution.py:107
  108.3 0.1 reduce_sum.122
  108.5 0.1 copy.52
  108.6 0.1 copy.53
  108.7 15.1 %all_to_all.125 = f32[8,80,128]{2,1,0:T(8,128)S(1)} all-to-all(f32[8,80,128]{2,1,0:T(8,128)S(1)} %pad_maximum_fusion.3), channel_id=1, replica_groups={{0,4,8,12,16,20,24,28},{1,5,9,13,17,21,25,29},{2,6,10,14,18,22,26,30},{..., dimensions={0} | all-to-all | bytes 655360 | tf_op jit(solution)/shard_map/all_to_all | solution.py:107
  123.9 13.4 %all_to_all.126.pieces_ref = f32[8,80,128]{2,1,0:T(8,128)S(1)} all-to-all(f32[8,80,128]{2,1,0:T(8,128)S(1)} %broadcast_in_dim.25), channel_id=1, replica_groups={{0,4,8,12,16,20,24,28},{1,5,9,13,17,21,25,29},{2,6,10,14,18,22,26,30},{..., dimensions={0} | all-to-all | bytes 655360 | tf_op jit(solution)/shard_map/all_to_all | solution.py:107
  137.2 5.7 %shard_map.50 = (bf16[4,512,128]{2,1,0:T(8,128)(2,1)S(1)}, f32[128,128]{1,0:T(8,128)}) custom-call(f32[8,80,128]{2,1,0:T(8,128)S(1)} %all_to_all.126.pieces_ref), custom_call_target="tpu_custom_call" | custom-call | tf_op jit(solution)/shard_map/pallas_call | solution.py:84
  142.9 9.3 %all_to_all.127 = bf16[4,512,128]{2,1,0:T(8,128)(2,1)S(1)} all-to-all(bf16[4,512,128]{2,1,0:T(8,128)(2,1)S(1)} %get-tuple-element.6), channel_id=1, replica_groups={{0,1,2,3},{4,5,6,7},{8,9,10,11},{12,13,14,15},{16,17,18,19},{20,21,22,2..., dimensions={0} | all-to-all | bytes 1048576 | tf_op jit(solution)/shard_map/all_to_all | solution.py:107
  152.3 2.8 convolution_bitcast_fusion.3
  155.1 0.2 copy.54
  155.3 8.1 %all_to_all.128 = f32[2,448,128]{2,1,0:T(8,128)S(1)} all-to-all(f32[2,448,128]{2,1,0:T(8,128)S(1)} %bitcast.96), channel_id=1, replica_groups={{0,32},{64,96},{128,160},{192,224},{256,288},{320,352},{384,416},{448,4..., dimensions={0} | all-to-all | bytes 917504 | tf_op jit(solution)/shard_map/all_to_all | solution.py:107
  163.4 14.0 %all_to_all.129 = f32[8,56,128]{2,1,0:T(8,128)S(1)} all-to-all(f32[8,56,128]{2,1,0:T(8,128)S(1)} %bitcast.100), channel_id=1, replica_groups={{0,64,128,192,256,320,384,448},{32,96,160,224,288,352,416,480},{1,65,12..., dimensions={0} | all-to-all | bytes 458752 | tf_op jit(solution)/shard_map/all_to_all | solution.py:107
  177.4 12.8 %all_to_all.130 = f32[8,56,128]{2,1,0:T(8,128)S(1)} all-to-all(f32[8,56,128]{2,1,0:T(8,128)S(1)} %broadcast_in_dim.26), channel_id=1, replica_groups={{0,64,128,192,256,320,384,448},{32,96,160,224,288,352,416,480},{1,65,12..., dimensions={0} | all-to-all | bytes 458752 | tf_op jit(solution)/shard_map/all_to_all | solution.py:107
  190.2 3.6 all_gather.6
  193.9 0.9 fusion.15
  194.9 3.4 convolution_bitcast_fusion.2
  198.2 0.1 slice_add_fusion.1
  198.5 0.1 pad_maximum_fusion.1
  198.6 20.1 %all_to_all.131 = f32[4,640,128]{1,2,0:T(8,128)S(1)} all-to-all(f32[4,640,128]{1,2,0:T(8,128)S(1)} %pad_maximum_fusion.1), channel_id=1, replica_groups={{0,1,2,3},{4,5,6,7},{8,9,10,11},{12,13,14,15},{16,17,18,19},{20,21,22,2..., dimensions={0} | all-to-all | bytes 2621440 | tf_op jit(solution)/shard_map/all_to_all | solution.py:107
  218.7 0.1 reduce_sum.126
  218.8 0.1 copy.58
  218.9 0.1 copy.59
  219.1 13.4 %all_to_all.132 = f32[8,80,128]{2,1,0:T(8,128)S(1)} all-to-all(f32[8,80,128]{2,1,0:T(8,128)S(1)} %pad_maximum_fusion.4), channel_id=1, replica_groups={{0,4,8,12,16,20,24,28},{1,5,9,13,17,21,25,29},{2,6,10,14,18,22,26,30},{..., dimensions={0} | all-to-all | bytes 655360 | tf_op jit(solution)/shard_map/all_to_all | solution.py:107
  232.5 13.2 %all_to_all.133.pieces_ref = f32[8,80,128]{2,1,0:T(8,128)S(1)} all-to-all(f32[8,80,128]{2,1,0:T(8,128)S(1)} %broadcast_in_dim.28), channel_id=1, replica_groups={{0,4,8,12,16,20,24,28},{1,5,9,13,17,21,25,29},{2,6,10,14,18,22,26,30},{..., dimensions={0} | all-to-all | bytes 655360 | tf_op jit(solution)/shard_map/all_to_all | solution.py:107
  245.8 5.7 %shard_map.51 = (bf16[4,512,128]{2,1,0:T(8,128)(2,1)S(1)}, f32[128,128]{1,0:T(8,128)}) custom-call(f32[8,80,128]{2,1,0:T(8,128)S(1)} %all_to_all.133.pieces_ref), custom_call_target="tpu_custom_call" | custom-call | tf_op jit(solution)/shard_map/pallas_call | solution.py:84
  251.5 9.3 %all_to_all.134 = bf16[4,512,128]{2,1,0:T(8,128)(2,1)S(1)} all-to-all(bf16[4,512,128]{2,1,0:T(8,128)(2,1)S(1)} %get-tuple-element.7), channel_id=1, replica_groups={{0,1,2,3},{4,5,6,7},{8,9,10,11},{12,13,14,15},{16,17,18,19},{20,21,22,2..., dimensions={0} | all-to-all | bytes 1048576 | tf_op jit(solution)/shard_map/all_to_all | solution.py:107
  260.8 0.4 convolution_bitcast_fusion.4
  261.2 0.1 copy.60
  261.3 17.1 %all_to_all.135 = f32[16,16,128]{2,1,0:T(8,128)S(1)} all-to-all(f32[16,16,128]{2,1,0:T(8,128)S(1)} %bitcast.104), channel_id=1, replica_groups=mesh['dp'=16,'mp'=32] {'dp'}, dimensions={0} | all-to-all | bytes 262144 | tf_op jit(solution)/shard_map/all_to_all | solution.py:107
  278.5 11.6 %all_to_all.136 = f32[16,16,128]{2,1,0:T(8,128)S(1)} all-to-all(f32[16,16,128]{2,1,0:T(8,128)S(1)} %broadcast_in_dim.29), channel_id=1, replica_groups=mesh['dp'=16,'mp'=32] {'dp'}, dimensions={0} | all-to-all | bytes 262144 | tf_op jit(solution)/shard_map/all_to_all | solution.py:107
  290.1 0.5 convolution_bitcast_fusion
  290.6 0.1 slice_add_fusion
  290.8 0.4 convolution_bitcast_fusion.6
  291.2 0.1 pad_maximum_fusion.2
  291.3 20.8 %all_to_all.137 = f32[4,640,128]{1,2,0:T(8,128)S(1)} all-to-all(f32[4,640,128]{1,2,0:T(8,128)S(1)} %pad_maximum_fusion.2), channel_id=1, replica_groups={{0,1,2,3},{4,5,6,7},{8,9,10,11},{12,13,14,15},{16,17,18,19},{20,21,22,2..., dimensions={0} | all-to-all | bytes 2621440 | tf_op jit(solution)/shard_map/all_to_all | solution.py:107
  312.1 0.1 reduce_sum.129
  312.2 0.1 copy.64
  312.4 0.1 copy.65
  312.5 15.1 %all_to_all.138 = f32[8,80,128]{2,1,0:T(8,128)S(1)} all-to-all(f32[8,80,128]{2,1,0:T(8,128)S(1)} %pad_maximum_fusion.5), channel_id=1, replica_groups={{0,4,8,12,16,20,24,28},{1,5,9,13,17,21,25,29},{2,6,10,14,18,22,26,30},{..., dimensions={0} | all-to-all | bytes 655360 | tf_op jit(solution)/shard_map/all_to_all | solution.py:107
  327.7 13.7 %all_to_all.139.pieces_ref = f32[8,80,128]{2,1,0:T(8,128)S(1)} all-to-all(f32[8,80,128]{2,1,0:T(8,128)S(1)} %broadcast_in_dim.31), channel_id=1, replica_groups={{0,4,8,12,16,20,24,28},{1,5,9,13,17,21,25,29},{2,6,10,14,18,22,26,30},{..., dimensions={0} | all-to-all | bytes 655360 | tf_op jit(solution)/shard_map/all_to_all | solution.py:107
  341.4 5.7 %shard_map.52 = (bf16[4,512,128]{2,1,0:T(8,128)(2,1)S(1)}, f32[128,128]{1,0:T(8,128)S(1)}) custom-call(f32[8,80,128]{2,1,0:T(8,128)S(1)} %all_to_all.139.pieces_ref), custom_call_target="tpu_custom_call" | custom-call | tf_op jit(solution)/shard_map/pallas_call | solution.py:84
  347.1 9.3 %all_to_all.140 = bf16[4,512,128]{2,1,0:T(8,128)(2,1)S(1)} all-to-all(bf16[4,512,128]{2,1,0:T(8,128)(2,1)S(1)} %get-tuple-element.9), channel_id=1, replica_groups={{0,1,2,3},{4,5,6,7},{8,9,10,11},{12,13,14,15},{16,17,18,19},{20,21,22,2..., dimensions={0} | all-to-all | bytes 1048576 | tf_op jit(solution)/shard_map/all_to_all | solution.py:107
  356.4 0.2 copy.66
  356.6 2.8 fusion
  359.4 7.8 %all_to_all.141 = f32[2,64,896]{2,1,0:T(8,128)S(1)} all-to-all(f32[2,64,896]{2,1,0:T(8,128)S(1)} %fusion), channel_id=1, replica_groups={{0,32},{64,96},{128,160},{192,224},{256,288},{320,352},{384,416},{448,4..., dimensions={0} | all-to-all | bytes 917504 | tf_op jit(solution)/shard_map/all_to_all | solution.py:107
  367.3 14.0 %all_to_all.142 = f32[8,8,896]{2,1,0:T(8,128)S(1)} all-to-all(f32[8,8,896]{2,1,0:T(8,128)S(1)} %bitcast.101), channel_id=1, replica_groups={{0,64,128,192,256,320,384,448},{32,96,160,224,288,352,416,480},{1,65,12..., dimensions={0} | all-to-all | bytes 458752 | tf_op jit(solution)/shard_map/all_to_all | solution.py:107
  381.2 0.7 broadcast_in_dim.32
  381.9 3.4 all-to-all-start.23
  385.3 0.9 convolution_multiply_fusion
  386.2 6.6 %all-to-all-done.23 = bf16[8,8,896]{2,1,0:T(8,128)(2,1)S(1)} async-done(((bf16[8,8,896]{2,1,0:T(8,128)(2,1)}), bf16[8,8,896]{2,1,0:T(8,128)(2,1)S(1)}, u32[]{:S(2)}, u32[]{:S(2)}) %all-to-all-start.23) | async-done | bytes 114720 | tf_op jit(solution)/shard_map/all_to_all | solution.py:107
  392.8 3.6 all_gather.7
  396.5 0.8 convert_element_type.53
  (37 shorter events, 1.0 us)
Async XLA Ops:
  0.6 50.1 %copy-start = (bf16[2048,256]{1,0:T(8,128)(2,1)S(1)}, bf16[2048,256]{1,0:T(8,128)(2,1)}, u32[]{:S(2)}) copy-start(bf16[2048,256]{1,0:T(8,128)(2,1)} %param.3) | copy-start | bytes 3145732
  381.9 10.9 %all-to-all-start.23 = ((bf16[8,8,896]{2,1,0:T(8,128)(2,1)}), bf16[8,8,896]{2,1,0:T(8,128)(2,1)S(1)}, u32[]{:S(2)}, u32[]{:S(2)}) async-start(bf16[8,8,896]{2,1,0:T(8,128)(2,1)} %broadcast_in_dim.32), calls=%async_computation.23 | async-start | bytes 229376 | tf_op jit(solution)/shard_map/all_to_all | solution.py:107

commit v5 on v4

--- a/solution.py
+++ b/solution.py
@@ -10,6 +10,7 @@
 N_X = 4
 N_Y = 8
 N_MP = N_X * N_Y
+PARTS = 3
 N_CORE = 2
 N_Z = 8
 N_DP = N_Z * N_CORE
@@ -64,23 +65,27 @@
 
 
 def normalise_kernel(pieces_ref, rows_ref, inverse_ref):
-    span = pieces_ref.shape[1] - K // N_Y
+    parts = 1 if pieces_ref.dtype == jnp.float32 else PARTS
+    depth = K // N_Y
+    span = pieces_ref.shape[1] - parts * depth
     groups = []
     for y in range(N_Y):
-        for start in range(span, pieces_ref.shape[1], 8):
-            groups.append(pieces_ref[y, start:start + 8, :])
+        whole = pieces_ref[y, span:span + depth, :].astype(jnp.float32)
+        for part in range(1, parts):
+            start = span + part * depth
+            whole = whole + pieces_ref[y, start:start + depth, :].astype(jnp.float32)
+        groups += [whole[start:start + 8, :] for start in range(0, depth, 8)]
     inverse_factor(groups, inverse_ref)
     for y in range(N_Y):
         rows = lax.dot_general(
-            pieces_ref[y, :span, :], inverse_ref[...], (((1,), (1,)), ((), ())),
-            precision=HIGHEST, preferred_element_type=jnp.float32,
+            pieces_ref[y, :span, :].astype(jnp.float32), inverse_ref[...],
+            (((1,), (1,)), ((), ())), precision=HIGHEST, preferred_element_type=jnp.float32,
         ).astype(rows_ref.dtype)
         for x in range(N_X):
             rows_ref[x, span * y:span * (y + 1), :] = rows
 
 
-def normalise(pieces):
-    span = pieces.shape[1] - K // N_Y
+def normalise(pieces, span):
     return pl.pallas_call(
         normalise_kernel,
         out_shape=(
@@ -97,10 +102,13 @@
     )
 
 
-def split_two(matrix):
-    high = matrix.astype(jnp.bfloat16)
-    low = (matrix - high.astype(jnp.float32)).astype(jnp.bfloat16)
-    return jnp.concatenate([high, low], axis=1)
+def split(matrix, count):
+    parts = []
+    for _ in range(count):
+        high = lax.reduce_precision(matrix, 8, 7)
+        parts.append(high.astype(jnp.bfloat16))
+        matrix = matrix - high
+    return parts
 
 
 def exchange(blocks, axis, groups=None):
@@ -124,45 +132,63 @@
 def staged_sum_over_tokens(partial_value, held_as):
     rows, columns = partial_value.shape
     half = rows // N_CORE
-    mine = scatter_sum(partial_value.reshape(N_CORE, half, columns), "dp", CORE_GROUPS)
-    mine = scatter_sum(mine.reshape(N_Z, half // N_Z, columns), "dp", Z_GROUPS)
+    blocks = partial_value.reshape(N_CORE, N_Z, half // N_Z, columns).swapaxes(0, 1)
+    mine = scatter_sum(blocks.reshape(N_DP, half // N_Z, columns), "dp")
     mine = gather(mine.astype(held_as), "dp", N_Z, Z_GROUPS).reshape(half, columns)
     return lax.all_gather(mine, "dp", axis_index_groups=CORE_GROUPS, tiled=True)
 
 
-def token_rows_of(data, sketch):
+def token_rows_of(data, sketch, held_as):
     tokens = data.shape[0]
+    parts = 1 if held_as == jnp.float32 else PARTS
+    quarter, span, depth = tokens // N_X, tokens // N_MP, K // N_Y
+
+    def parts_of(gram):
+        return [gram] if parts == 1 else split(gram, parts)
+
+    def total(received, rows):
+        received = received.astype(jnp.float32)
+        pieces = received[:, rows:].reshape(received.shape[0], parts, -1, K)
+        return jnp.sum(received[:, :rows], axis=0), jnp.sum(jnp.sum(pieces, axis=1), axis=0)
+
     gram = lax.dot_general(
         sketch, sketch, (((0,), (0,)), ((), ())), precision=HIGHEST,
         preferred_element_type=jnp.float32,
     )
-    both = jnp.dot(data, split_two(sketch), preferred_element_type=jnp.float32)
-    product = both[:, :K] + both[:, K:]
-    quarter, span = tokens // N_X, tokens // N_MP
+    both = jnp.dot(
+        data, jnp.concatenate(split(sketch, 2), axis=1), preferred_element_type=jnp.float32
+    )
+    product = (both[:, :K] + both[:, K:]).astype(held_as)
     blocks = jnp.concatenate(
-        [product.reshape(N_X, quarter, K), jnp.broadcast_to(gram[None], (N_X, K, K))], axis=1
-    )
-    mine = scatter_sum(blocks, "mp", X_GROUPS)
+        [product.reshape(N_X, quarter, K)]
+        + [jnp.broadcast_to(part[None], (N_X, K, K)) for part in parts_of(gram)], axis=1
+    )
+    product, gram = total(exchange(blocks, "mp", X_GROUPS), quarter)
     blocks = jnp.concatenate(
-        [mine[:quarter].reshape(N_Y, span, K), mine[quarter:].reshape(N_Y, K // N_Y, K)], axis=1
-    )
-    mine = gather(scatter_sum(blocks, "mp", Y_GROUPS), "mp", N_Y, Y_GROUPS)
-    rows, inverse = normalise(mine)
+        [product.astype(held_as).reshape(N_Y, span, K)]
+        + [part.reshape(N_Y, depth, K) for part in parts_of(gram)], axis=1
+    )
+    product, gram = total(exchange(blocks, "mp", Y_GROUPS), span)
+    pieces = jnp.concatenate([product.astype(held_as)] + parts_of(gram), axis=0)
+    rows, inverse = normalise(gather(pieces, "mp", N_Y, Y_GROUPS), span)
     return exchange(rows, "mp", X_GROUPS).reshape(tokens, K), inverse
 
 
 def on_device(activations, output_grads, probe_matrix):
     tokens = activations.shape[0]
     partial_value = jnp.dot(output_grads, probe_matrix, preferred_element_type=jnp.float32)
-    mine = scatter_sum(partial_value.astype(jnp.bfloat16).reshape(N_MP, tokens // N_MP, K), "mp")
-    probe_rows = gather(mine.astype(jnp.bfloat16), "mp", N_MP).reshape(tokens, K)
+    partial_value = partial_value.astype(jnp.bfloat16).reshape(N_X, tokens // N_X, K)
+    mine = scatter_sum(partial_value, "mp", X_GROUPS).astype(jnp.bfloat16)
+    mine = scatter_sum(mine.reshape(N_Y, tokens // N_MP, K), "mp", Y_GROUPS).astype(jnp.bfloat16)
+    mine = gather(mine, "mp", N_Y, Y_GROUPS).reshape(tokens // N_X, K)
+    probe_rows = gather(mine, "mp", N_X, X_GROUPS).reshape(tokens, K)
 
     sketch = sum_over_tokens(rows_product(activations, probe_rows))
-    token_rows, _ = token_rows_of(activations, sketch)
+    token_rows, _ = token_rows_of(activations, sketch, jnp.float32)
     back_sketch = staged_sum_over_tokens(rows_product(output_grads, token_rows), jnp.float32)
-    unit_rows, _ = token_rows_of(output_grads, back_sketch)
+    unit_rows, _ = token_rows_of(output_grads, back_sketch, jnp.float32)
     power_sketch = sum_over_tokens(rows_product(activations, unit_rows))
-    last_rows, inverse = token_rows_of(activations, power_sketch)
+    last_rows, inverse = token_rows_of(activations, power_sketch, jnp.bfloat16)
     projection = staged_sum_over_tokens(rows_product(last_rows, output_grads), jnp.bfloat16)
     third_basis = lax.dot_general(
         power_sketch, inverse, (((1,), (1,)), ((), ())), precision=HIGHEST,

time: 398 us -> 392 us (0.985)
  blocking collectives: 348 us -> 342 us
where the time goes in v5:
time: 392 us; the launch traced here: 391 us
  blocking collectives  342 us (87%)
  Pallas kernels  17.2 us (4%)
  matrix products  14.4 us (4%)
  waiting for transfers between devices  8.24 us (2%)
    all_to_all x23, blocking collectives, exchange(): return lax.all_to_all(blocks, axis, 0, 0, axis_index_groups=groups)  337 us
    pallas_call x3, Pallas kernels, normalise(): pl.pallas_call(normalise_kernel, out_shape=(jax.ShapeDtypeStruct((N_X, N_...  17.2 us
    all_to_all x1, waiting for transfers between devices, exchange(): return lax.all_to_all(blocks, axis, 0, 0, axis_index_groups=groups)  8.24 us
  transfers between devices with their start and end apart: 1, of which 1 were waited for; matrix products, arithmetic and copies ran while one was open for 0% of the time, Pallas kernels for 0%

profile of v5, /device:TPU:1, one launch (start us, length us, event | category | flops | bytes accessed | tf_op | source)
XLA Modules:
  0.0 391.3 jit_solution(6410157141418055791)
XLA Ops:
  0.6 3.3 convolution_convert_fusion
  3.9 11.6 %all_to_all.120 = bf16[4,512,128]{2,1,0:T(8,128)(2,1)S(1)} all-to-all(bf16[4,512,128]{2,1,0:T(8,128)(2,1)S(1)} %bitcast.95), channel_id=1, replica_groups={{0,1,2,3},{4,5,6,7},{8,9,10,11},{12,13,14,15},{16,17,18,19},{20,21,22,2..., dimensions={0} | all-to-all | bytes 1048576 | tf_op jit(solution)/shard_map/all_to_all | solution.py:115
  15.6 16.3 %all_to_all.121 = bf16[8,64,128]{2,1,0:T(8,128)(2,1)S(1)} all-to-all(bf16[8,64,128]{2,1,0:T(8,128)(2,1)S(1)} %bitcast.114), channel_id=1, replica_groups={{0,4,8,12,16,20,24,28},{1,5,9,13,17,21,25,29},{2,6,10,14,18,22,26,30},{..., dimensions={0} | all-to-all | bytes 262144 | tf_op jit(solution)/shard_map/all_to_all | solution.py:115
  31.9 10.4 %all_to_all.122 = bf16[8,64,128]{2,1,0:T(8,128)(2,1)S(1)} all-to-all(bf16[8,64,128]{2,1,0:T(8,128)(2,1)S(1)} %broadcast_in_dim.30), channel_id=1, replica_groups={{0,4,8,12,16,20,24,28},{1,5,9,13,17,21,25,29},{2,6,10,14,18,22,26,30},{..., dimensions={0} | all-to-all | bytes 262144 | tf_op jit(solution)/shard_map/all_to_all | solution.py:115
  42.4 9.3 %all_to_all.123 = bf16[4,512,128]{2,1,0:T(8,128)(2,1)S(1)} all-to-all(bf16[4,512,128]{2,1,0:T(8,128)(2,1)S(1)} %broadcast_in_dim.32), channel_id=1, replica_groups={{0,1,2,3},{4,5,6,7},{8,9,10,11},{12,13,14,15},{16,17,18,19},{20,21,22,2..., dimensions={0} | all-to-all | bytes 1048576 | tf_op jit(solution)/shard_map/all_to_all | solution.py:115
  51.7 0.4 convolution_bitcast_fusion.5
  52.1 0.1 copy.68
  52.2 24.7 %all_to_all.124 = f32[16,16,128]{2,1,0:T(8,128)S(1)} all-to-all(f32[16,16,128]{2,1,0:T(8,128)S(1)} %bitcast.112), channel_id=1, replica_groups=mesh['dp'=16,'mp'=32] {'dp'}, dimensions={0} | all-to-all | bytes 262144 | tf_op jit(solution)/shard_map/all_to_all | solution.py:115
  76.9 11.6 %all_to_all.125 = f32[16,16,128]{2,1,0:T(8,128)S(1)} all-to-all(f32[16,16,128]{2,1,0:T(8,128)S(1)} %broadcast_in_dim.33), channel_id=1, replica_groups=mesh['dp'=16,'mp'=32] {'dp'}, dimensions={0} | all-to-all | bytes 262144 | tf_op jit(solution)/shard_map/all_to_all | solution.py:115
  88.5 0.5 convolution_bitcast_fusion.1
  89.0 0.1 slice_add_fusion.2
  89.2 0.4 convolution_bitcast_fusion.7
  89.6 0.1 pad_maximum_fusion
  89.7 20.8 %all_to_all.126 = f32[4,640,128]{1,2,0:T(8,128)S(1)} all-to-all(f32[4,640,128]{1,2,0:T(8,128)S(1)} %pad_maximum_fusion), channel_id=1, replica_groups={{0,1,2,3},{4,5,6,7},{8,9,10,11},{12,13,14,15},{16,17,18,19},{20,21,22,2..., dimensions={0} | all-to-all | bytes 2621440 | tf_op jit(solution)/shard_map/all_to_all | solution.py:115
  110.6 0.1 copy.72
  110.7 0.1 copy.74
  110.9 15.4 %all_to_all.127 = f32[8,80,128]{2,1,0:T(8,128)S(1)} all-to-all(f32[8,80,128]{2,1,0:T(8,128)S(1)} %pad_maximum_fusion.3), channel_id=1, replica_groups={{0,4,8,12,16,20,24,28},{1,5,9,13,17,21,25,29},{2,6,10,14,18,22,26,30},{..., dimensions={0} | all-to-all | bytes 655360 | tf_op jit(solution)/shard_map/all_to_all | solution.py:115
  126.3 13.4 %all_to_all.128.pieces_ref = f32[8,80,128]{2,1,0:T(8,128)S(1)} all-to-all(f32[8,80,128]{2,1,0:T(8,128)S(1)} %broadcast_in_dim.35), channel_id=1, replica_groups={{0,4,8,12,16,20,24,28},{1,5,9,13,17,21,25,29},{2,6,10,14,18,22,26,30},{..., dimensions={0} | all-to-all | bytes 655360 | tf_op jit(solution)/shard_map/all_to_all | solution.py:115
  139.7 5.7 %shard_map.50 = (bf16[4,512,128]{2,1,0:T(8,128)(2,1)S(1)}, f32[128,128]{1,0:T(8,128)}) custom-call(f32[8,80,128]{2,1,0:T(8,128)S(1)} %all_to_all.128.pieces_ref), custom_call_target="tpu_custom_call" | custom-call | tf_op jit(solution)/shard_map/pallas_call | solution.py:89
  145.5 9.3 %all_to_all.129 = bf16[4,512,128]{2,1,0:T(8,128)(2,1)S(1)} all-to-all(bf16[4,512,128]{2,1,0:T(8,128)(2,1)S(1)} %get-tuple-element.6), channel_id=1, replica_groups={{0,1,2,3},{4,5,6,7},{8,9,10,11},{12,13,14,15},{16,17,18,19},{20,21,22,2..., dimensions={0} | all-to-all | bytes 1048576 | tf_op jit(solution)/shard_map/all_to_all | solution.py:115
  154.8 0.7 convolution_bitcast_fusion.3
  155.5 0.2 copy.75
  155.8 22.8 %all_to_all.130 = f32[16,56,128]{2,1,0:T(8,128)S(1)} all-to-all(f32[16,56,128]{2,1,0:T(8,128)S(1)} %bitcast.103), channel_id=1, replica_groups=mesh['dp'=16,'mp'=32] {'dp'}, dimensions={0} | all-to-all | bytes 917504 | tf_op jit(solution)/shard_map/all_to_all | solution.py:115
  178.6 14.1 %all_to_all.131 = f32[8,56,128]{2,1,0:T(8,128)S(1)} all-to-all(f32[8,56,128]{2,1,0:T(8,128)S(1)} %broadcast_in_dim.36), channel_id=1, replica_groups={{0,64,128,192,256,320,384,448},{32,96,160,224,288,352,416,480},{1,65,12..., dimensions={0} | all-to-all | bytes 458752 | tf_op jit(solution)/shard_map/all_to_all | solution.py:115
  192.7 2.4 all_gather.6
  195.1 0.9 fusion.30
  196.1 3.4 convolution_bitcast_fusion.2
  199.4 0.1 slice_add_fusion.1
  199.7 0.1 pad_maximum_fusion.1
  199.8 20.1 %all_to_all.132 = f32[4,640,128]{1,2,0:T(8,128)S(1)} all-to-all(f32[4,640,128]{1,2,0:T(8,128)S(1)} %pad_maximum_fusion.1), channel_id=1, replica_groups={{0,1,2,3},{4,5,6,7},{8,9,10,11},{12,13,14,15},{16,17,18,19},{20,21,22,2..., dimensions={0} | all-to-all | bytes 2621440 | tf_op jit(solution)/shard_map/all_to_all | solution.py:115
  220.0 0.1 copy.80
  220.1 0.1 copy.82
  220.2 13.5 %all_to_all.133 = f32[8,80,128]{2,1,0:T(8,128)S(1)} all-to-all(f32[8,80,128]{2,1,0:T(8,128)S(1)} %pad_maximum_fusion.4), channel_id=1, replica_groups={{0,4,8,12,16,20,24,28},{1,5,9,13,17,21,25,29},{2,6,10,14,18,22,26,30},{..., dimensions={0} | all-to-all | bytes 655360 | tf_op jit(solution)/shard_map/all_to_all | solution.py:115
  233.8 13.2 %all_to_all.134.pieces_ref = f32[8,80,128]{2,1,0:T(8,128)S(1)} all-to-all(f32[8,80,128]{2,1,0:T(8,128)S(1)} %broadcast_in_dim.38), channel_id=1, replica_groups={{0,4,8,12,16,20,24,28},{1,5,9,13,17,21,25,29},{2,6,10,14,18,22,26,30},{..., dimensions={0} | all-to-all | bytes 655360 | tf_op jit(solution)/shard_map/all_to_all | solution.py:115
  247.0 5.7 %shard_map.51 = (bf16[4,512,128]{2,1,0:T(8,128)(2,1)S(1)}, f32[128,128]{1,0:T(8,128)}) custom-call(f32[8,80,128]{2,1,0:T(8,128)S(1)} %all_to_all.134.pieces_ref), custom_call_target="tpu_custom_call" | custom-call | tf_op jit(solution)/shard_map/pallas_call | solution.py:89
  252.7 9.3 %all_to_all.135 = bf16[4,512,128]{2,1,0:T(8,128)(2,1)S(1)} all-to-all(bf16[4,512,128]{2,1,0:T(8,128)(2,1)S(1)} %get-tuple-element.7), channel_id=1, replica_groups={{0,1,2,3},{4,5,6,7},{8,9,10,11},{12,13,14,15},{16,17,18,19},{20,21,22,2..., dimensions={0} | all-to-all | bytes 1048576 | tf_op jit(solution)/shard_map/all_to_all | solution.py:115
  262.1 0.4 convolution_bitcast_fusion.4
  262.4 0.1 copy.83
  262.5 17.2 %all_to_all.136 = f32[16,16,128]{2,1,0:T(8,128)S(1)} all-to-all(f32[16,16,128]{2,1,0:T(8,128)S(1)} %bitcast.113), channel_id=1, replica_groups=mesh['dp'=16,'mp'=32] {'dp'}, dimensions={0} | all-to-all | bytes 262144 | tf_op jit(solution)/shard_map/all_to_all | solution.py:115
  279.7 11.6 %all_to_all.137 = f32[16,16,128]{2,1,0:T(8,128)S(1)} all-to-all(f32[16,16,128]{2,1,0:T(8,128)S(1)} %broadcast_in_dim.39), channel_id=1, replica_groups=mesh['dp'=16,'mp'=32] {'dp'}, dimensions={0} | all-to-all | bytes 262144 | tf_op jit(solution)/shard_map/all_to_all | solution.py:115
  291.3 0.4 reduce-precision_convert_fusion.6
  291.7 0.1 copy.84
  291.8 0.1 copy.86
  291.9 0.1 copy.85
  292.1 0.5 convolution_bitcast_fusion
  292.6 0.1 fusion.5
  292.8 0.1 pad_maximum_fusion.2
  293.0 16.5 %all_to_all.138 = bf16[4,896,128]{1,2,0:T(8,128)(2,1)S(1)} all-to-all(bf16[4,896,128]{1,2,0:T(8,128)(2,1)S(1)} %pad_maximum_fusion.2), channel_id=1, replica_groups={{0,1,2,3},{4,5,6,7},{8,9,10,11},{12,13,14,15},{16,17,18,19},{20,21,22,2..., dimensions={0} | all-to-all | bytes 1835008 | tf_op jit(solution)/shard_map/all_to_all | solution.py:115
  309.5 0.1 convert_element_type.95
  309.7 0.1 copy.91
  309.9 0.1 copy.89
  310.1 12.9 %all_to_all.139 = bf16[8,112,128]{2,1,0:T(8,128)(2,1)S(1)} all-to-all(bf16[8,112,128]{2,1,0:T(8,128)(2,1)S(1)} %pad_maximum_fusion.5), channel_id=1, replica_groups={{0,4,8,12,16,20,24,28},{1,5,9,13,17,21,25,29},{2,6,10,14,18,22,26,30},{..., dimensions={0} | all-to-all | bytes 458752 | tf_op jit(solution)/shard_map/all_to_all | solution.py:115
  323.2 11.6 %all_to_all.140.pieces_ref = bf16[8,112,128]{2,1,0:T(8,128)(2,1)S(1)} all-to-all(bf16[8,112,128]{2,1,0:T(8,128)(2,1)S(1)} %broadcast_in_dim.43), channel_id=1, replica_groups={{0,4,8,12,16,20,24,28},{1,5,9,13,17,21,25,29},{2,6,10,14,18,22,26,30},{..., dimensions={0} | all-to-all | bytes 458752 | tf_op jit(solution)/shard_map/all_to_all | solution.py:115
  334.7 5.7 %shard_map.52 = (bf16[4,512,128]{2,1,0:T(8,128)(2,1)S(1)}, f32[128,128]{1,0:T(8,128)S(1)}) custom-call(bf16[8,112,128]{2,1,0:T(8,128)(2,1)S(1)} %all_to_all.140.pieces_ref), custom_call_target="tpu_custom_call" | custom-call | tf_op jit(solution)/shard_map/pallas_call | solution.py:89
  340.5 9.3 %all_to_all.141 = bf16[4,512,128]{2,1,0:T(8,128)(2,1)S(1)} all-to-all(bf16[4,512,128]{2,1,0:T(8,128)(2,1)S(1)} %get-tuple-element.9), channel_id=1, replica_groups={{0,1,2,3},{4,5,6,7},{8,9,10,11},{12,13,14,15},{16,17,18,19},{20,21,22,2..., dimensions={0} | all-to-all | bytes 1048576 | tf_op jit(solution)/shard_map/all_to_all | solution.py:115
  349.8 0.2 copy.92
  350.0 2.8 fusion.2
  352.8 22.4 %all_to_all.142 = f32[16,8,896]{2,1,0:T(8,128)S(1)} all-to-all(f32[16,8,896]{2,1,0:T(8,128)S(1)} %bitcast.104), channel_id=1, replica_groups=mesh['dp'=16,'mp'=32] {'dp'}, dimensions={0} | all-to-all | bytes 917504 | tf_op jit(solution)/shard_map/all_to_all | solution.py:115
  375.3 0.7 broadcast_in_dim.44
  375.9 3.4 all-to-all-start.23
  379.3 0.9 convolution_multiply_fusion
  380.2 8.2 %all-to-all-done.23 = bf16[8,8,896]{2,1,0:T(8,128)(2,1)S(1)} async-done(((bf16[8,8,896]{2,1,0:T(8,128)(2,1)}), bf16[8,8,896]{2,1,0:T(8,128)(2,1)S(1)}, u32[]{:S(2)}, u32[]{:S(2)}) %all-to-all-start.23) | async-done | bytes 114720 | tf_op jit(solution)/shard_map/all_to_all | solution.py:115
  388.5 2.0 all_gather.7
  390.5 0.8 convert_element_type.107
  (54 shorter events, 1.4 us)
Async XLA Ops:
  0.6 51.1 %copy-start = (bf16[2048,256]{1,0:T(8,128)(2,1)S(1)}, bf16[2048,256]{1,0:T(8,128)(2,1)}, u32[]{:S(2)}) copy-start(bf16[2048,256]{1,0:T(8,128)(2,1)} %param.3) | copy-start | bytes 3145732
  110.8 44.0 %copy-start.1 = (bf16[2048,896]{1,0:T(8,128)(2,1)S(1)}, bf16[2048,896]{1,0:T(8,128)(2,1)}, u32[]{:S(2)}) copy-start(bf16[2048,896]{1,0:T(8,128)(2,1)} %param.4) | copy-start | bytes 11010052
  375.9 12.6 %all-to-all-start.23 = ((bf16[8,8,896]{2,1,0:T(8,128)(2,1)}), bf16[8,8,896]{2,1,0:T(8,128)(2,1)S(1)}, u32[]{:S(2)}, u32[]{:S(2)}) async-start(bf16[8,8,896]{2,1,0:T(8,128)(2,1)} %broadcast_in_dim.44), calls=%async_computation.23 | async-start | bytes 229376 | tf_op jit(solution)/shard_map/all_to_all | solution.py:115

commit v6 on v5

--- a/solution.py
+++ b/solution.py
@@ -1,3 +1,5 @@
+import functools
+
 import jax
 import jax.numpy as jnp
 from jax import lax
@@ -11,6 +13,7 @@
 N_Y = 8
 N_MP = N_X * N_Y
 PARTS = 3
+CHUNKS = 8
 N_CORE = 2
 N_Z = 8
 N_DP = N_Z * N_CORE
@@ -64,7 +67,14 @@
             groups[g] = kept
 
 
-def normalise_kernel(pieces_ref, rows_ref, inverse_ref):
+def nt_product(left, right):
+    return lax.dot_general(
+        left, right, (((1,), (1,)), ((), ())), precision=HIGHEST,
+        preferred_element_type=jnp.float32,
+    )
+
+
+def normalise_kernel(transposed, pieces_ref, rows_ref, inverse_ref):
     parts = 1 if pieces_ref.dtype == jnp.float32 else PARTS
     depth = K // N_Y
     span = pieces_ref.shape[1] - parts * depth
@@ -77,23 +87,93 @@
         groups += [whole[start:start + 8, :] for start in range(0, depth, 8)]
     inverse_factor(groups, inverse_ref)
     for y in range(N_Y):
-        rows = lax.dot_general(
-            pieces_ref[y, :span, :].astype(jnp.float32), inverse_ref[...],
-            (((1,), (1,)), ((), ())), precision=HIGHEST, preferred_element_type=jnp.float32,
-        ).astype(rows_ref.dtype)
+        product = pieces_ref[y, :span, :].astype(jnp.float32)
+        spot = slice(span * y, span * (y + 1))
+        if transposed:
+            rows = nt_product(inverse_ref[...], product).astype(rows_ref.dtype)
+        else:
+            rows = nt_product(product, inverse_ref[...]).astype(rows_ref.dtype)
         for x in range(N_X):
-            rows_ref[x, span * y:span * (y + 1), :] = rows
-
-
-def normalise(pieces, span):
+            if transposed:
+                rows_ref[x, :, spot] = rows
+            else:
+                rows_ref[x, spot, :] = rows
+
+
+def normalise(pieces, span, transposed):
+    quarter = N_Y * span
+    shape = (N_X, K, quarter) if transposed else (N_X, quarter, K)
     return pl.pallas_call(
-        normalise_kernel,
+        functools.partial(normalise_kernel, transposed),
         out_shape=(
-            jax.ShapeDtypeStruct((N_X, N_Y * span, K), jnp.bfloat16),
-            jax.ShapeDtypeStruct((K, K), jnp.float32),
+            jax.ShapeDtypeStruct(shape, jnp.bfloat16), jax.ShapeDtypeStruct((K, K), jnp.float32)
         ),
         compiler_params=pltpu.CompilerParams(vmem_limit_bytes=16 << 20),
     )(pieces)
+
+
+def parts_in(matrix, count):
+    parts = []
+    for _ in range(count):
+        parts.append(matrix.astype(jnp.bfloat16))
+        matrix = matrix - parts[-1].astype(jnp.float32)
+    return parts
+
+
+def products_kernel(data_ref, sketch_ref, blocks_ref):
+    tokens = data_ref.shape[0]
+    quarter, chunk = tokens // N_X, tokens // CHUNKS
+    sketch = sketch_ref[...]
+    gram = lax.dot_general(
+        sketch, sketch, (((0,), (0,)), ((), ())), precision=HIGHEST,
+        preferred_element_type=jnp.float32,
+    )
+    whole = blocks_ref.dtype == jnp.float32
+    for i, part in enumerate([gram] if whole else parts_in(gram, PARTS)):
+        for x in range(N_X):
+            blocks_ref[x, quarter + K * i:quarter + K * (i + 1), :] = part
+    both = jnp.concatenate(parts_in(sketch, 2), axis=1)
+    for i in range(CHUNKS):
+        product = jnp.dot(
+            data_ref[chunk * i:chunk * (i + 1), :], both, preferred_element_type=jnp.float32
+        )
+        product = product[:, :K] + product[:, K:]
+        start = chunk * i % quarter
+        blocks_ref[chunk * i // quarter, start:start + chunk, :] = product.astype(blocks_ref.dtype)
+
+
+def product_blocks(data, sketch, held_as):
+    rows = data.shape[0] // N_X + K * (1 if held_as == jnp.float32 else PARTS)
+    return pl.pallas_call(
+        products_kernel,
+        out_shape=jax.ShapeDtypeStruct((N_X, rows, K), held_as),
+        in_specs=[pl.BlockSpec(memory_space=pltpu.VMEM)] * 2,
+        compiler_params=pltpu.CompilerParams(vmem_limit_bytes=24 << 20),
+    )(data, sketch)
+
+
+def projection_kernel(rows_ref, grads_ref, blocks_ref):
+    quarter = rows_ref.shape[2]
+    total = jnp.zeros((K, grads_ref.shape[1]), jnp.float32)
+    for x in range(N_X):
+        total = total + jnp.dot(
+            rows_ref[x], grads_ref[quarter * x:quarter * (x + 1), :],
+            preferred_element_type=jnp.float32,
+        )
+    depth = K // N_DP
+    for z in range(N_Z):
+        for core in range(N_CORE):
+            start = (core * N_Z + z) * depth
+            blocks_ref[z * N_CORE + core] = total[start:start + depth, :]
+
+
+def projection_blocks(rows, grads):
+    return pl.pallas_call(
+        projection_kernel,
+        out_shape=jax.ShapeDtypeStruct((N_DP, K // N_DP, grads.shape[1]), jnp.float32),
+        in_specs=[pl.BlockSpec(memory_space=pltpu.VMEM)] * 2,
+        compiler_params=pltpu.CompilerParams(vmem_limit_bytes=24 << 20),
+    )(rows, grads)
 
 
 def rows_product(left, right):
@@ -129,16 +209,19 @@
     return gather(mine, "dp", N_DP).reshape(rows, columns)
 
 
-def staged_sum_over_tokens(partial_value, held_as):
+def blocks_over_tokens(partial_value):
     rows, columns = partial_value.shape
-    half = rows // N_CORE
-    blocks = partial_value.reshape(N_CORE, N_Z, half // N_Z, columns).swapaxes(0, 1)
-    mine = scatter_sum(blocks.reshape(N_DP, half // N_Z, columns), "dp")
-    mine = gather(mine.astype(held_as), "dp", N_Z, Z_GROUPS).reshape(half, columns)
+    blocks = partial_value.reshape(N_CORE, N_Z, rows // N_DP, columns).swapaxes(0, 1)
+    return blocks.reshape(N_DP, rows // N_DP, columns)
+
+
+def staged_sum_over_tokens(blocks, held_as):
+    mine = scatter_sum(blocks, "dp").astype(held_as)
+    mine = gather(mine, "dp", N_Z, Z_GROUPS).reshape(-1, blocks.shape[2])
     return lax.all_gather(mine, "dp", axis_index_groups=CORE_GROUPS, tiled=True)
 
 
-def token_rows_of(data, sketch, held_as):
+def token_rows_of(data, sketch, held_as, transposed):
     tokens = data.shape[0]
     parts = 1 if held_as == jnp.float32 else PARTS
     quarter, span, depth = tokens // N_X, tokens // N_MP, K // N_Y
@@ -151,18 +234,7 @@
         pieces = received[:, rows:].reshape(received.shape[0], parts, -1, K)
         return jnp.sum(received[:, :rows], axis=0), jnp.sum(jnp.sum(pieces, axis=1), axis=0)
 
-    gram = lax.dot_general(
-        sketch, sketch, (((0,), (0,)), ((), ())), precision=HIGHEST,
-        preferred_element_type=jnp.float32,
-    )
-    both = jnp.dot(
-        data, jnp.concatenate(split(sketch, 2), axis=1), preferred_element_type=jnp.float32
-    )
-    product = (both[:, :K] + both[:, K:]).astype(held_as)
-    blocks = jnp.concatenate(
-        [product.reshape(N_X, quarter, K)]
-        + [jnp.broadcast_to(part[None], (N_X, K, K)) for part in parts_of(gram)], axis=1
-    )
+    blocks = product_blocks(data, sketch, held_as)
     product, gram = total(exchange(blocks, "mp", X_GROUPS), quarter)
     blocks = jnp.concatenate(
         [product.astype(held_as).reshape(N_Y, span, K)]
@@ -170,26 +242,25 @@
     )
     product, gram = total(exchange(blocks, "mp", Y_GROUPS), span)
     pieces = jnp.concatenate([product.astype(held_as)] + parts_of(gram), axis=0)
-    rows, inverse = normalise(gather(pieces, "mp", N_Y, Y_GROUPS), span)
-    return exchange(rows, "mp", X_GROUPS).reshape(tokens, K), inverse
+    rows, inverse = normalise(gather(pieces, "mp", N_Y, Y_GROUPS), span, transposed)
+    return exchange(rows, "mp", X_GROUPS), inverse
 
 
 def on_device(activations, output_grads, probe_matrix):
     tokens = activations.shape[0]
     partial_value = jnp.dot(output_grads, probe_matrix, preferred_element_type=jnp.float32)
-    partial_value = partial_value.astype(jnp.bfloat16).reshape(N_X, tokens // N_X, K)
-    mine = scatter_sum(partial_value, "mp", X_GROUPS).astype(jnp.bfloat16)
-    mine = scatter_sum(mine.reshape(N_Y, tokens // N_MP, K), "mp", Y_GROUPS).astype(jnp.bfloat16)
-    mine = gather(mine, "mp", N_Y, Y_GROUPS).reshape(tokens // N_X, K)
-    probe_rows = gather(mine, "mp", N_X, X_GROUPS).reshape(tokens, K)
+    partial_value = partial_value.astype(jnp.bfloat16).reshape(N_MP, tokens // N_MP, K)
+    mine = scatter_sum(partial_value, "mp").astype(jnp.bfloat16)
+    probe_rows = gather(mine, "mp", N_MP).reshape(tokens, K)
 
     sketch = sum_over_tokens(rows_product(activations, probe_rows))
-    token_rows, _ = token_rows_of(activations, sketch, jnp.float32)
-    back_sketch = staged_sum_over_tokens(rows_product(output_grads, token_rows), jnp.float32)
-    unit_rows, _ = token_rows_of(output_grads, back_sketch, jnp.float32)
-    power_sketch = sum_over_tokens(rows_product(activations, unit_rows))
-    last_rows, inverse = token_rows_of(activations, power_sketch, jnp.bfloat16)
-    projection = staged_sum_over_tokens(rows_product(last_rows, output_grads), jnp.bfloat16)
+    token_rows, _ = token_rows_of(activations, sketch, jnp.float32, False)
+    partial_value = rows_product(output_grads, token_rows.reshape(tokens, K))
+    back_sketch = staged_sum_over_tokens(blocks_over_tokens(partial_value), jnp.float32)
+    unit_rows, _ = token_rows_of(output_grads, back_sketch, jnp.float32, False)
+    power_sketch = sum_over_tokens(rows_product(activations, unit_rows.reshape(tokens, K)))
+    last_rows, inverse = token_rows_of(activations, power_sketch, jnp.bfloat16, True)
+    projection = staged_sum_over_tokens(projection_blocks(last_rows, output_grads), jnp.bfloat16)
     third_basis = lax.dot_general(
         power_sketch, inverse, (((1,), (1,)), ((), ())), precision=HIGHEST,
         preferred_element_type=jnp.float32,

time: 392 us -> 387 us (0.987)
  matrix products: 14.4 us -> 5.54 us
    dot_general x6 -> x0, matrix products: 6.02 us -> none  [the longest x3 4.33 us: token_rows_of(): jnp.dot(data, jnp.concatenate(split(sketch, 2), axis=1), preferred_elemen...]
    unnamed x4 -> x10, local copies, waits for them, and re-layouts: 0.02 us -> 5.03 us
    pallas_call x3 -> x7, Pallas kernels: 17.2 us -> 20.2 us  [the longest x3 16.7 us: normalise(): pl.pallas_call(functools.partial(normalise_kernel, transposed), out_shape...]
    all_to_all x23 -> x21, blocking collectives: 337 us -> 335 us  [exchange(): return lax.all_to_all(blocks, axis, 0, 0, axis_index_groups=groups)]
where the time goes in v6:
time: 387 us; the launch traced here: 386 us
  blocking collectives  339 us (88%)
  Pallas kernels  20.2 us (5%)
  waiting for transfers between devices  8.24 us (2%)
  local copies, waits for them, and re-layouts  6.3 us (2%)
  matrix products  5.54 us (1%)
    all_to_all x21, blocking collectives, exchange(): return lax.all_to_all(blocks, axis, 0, 0, axis_index_groups=groups)  335 us
    pallas_call x3, Pallas kernels, normalise(): pl.pallas_call(functools.partial(normalise_kernel, transposed), out_shape...  16.7 us
    all_to_all x1, waiting for transfers between devices, exchange(): return lax.all_to_all(blocks, axis, 0, 0, axis_index_groups=groups)  8.24 us
  transfers between devices with their start and end apart: 1, of which 1 were waited for; matrix products, arithmetic and copies ran while one was open for 0% of the time, Pallas kernels for 0%

profile of v6, /device:TPU:1, one launch (start us, length us, event | category | flops | bytes accessed | tf_op | source)
XLA Modules:
  0.0 385.6 jit_solution(6553666784576120571)
XLA Ops:
  0.6 0.0 copy-start
  0.6 0.9 copy-done
  1.6 3.2 convolution_convert_fusion
  4.7 0.0 copy-start.4
  4.8 26.7 %all_to_all.110 = bf16[32,64,128]{2,1,0:T(8,128)(2,1)S(1)} all-to-all(bf16[32,64,128]{2,1,0:T(8,128)(2,1)S(1)} %bitcast.41), channel_id=1, replica_groups=mesh['dp'=16,'mp'=32] {'mp'}, dimensions={0} | all-to-all | bytes 1048576 | tf_op jit(solution)/shard_map/all_to_all | solution.py:195
  31.5 0.1 reduce_sum.196
  31.5 0.1 broadcast_in_dim.16
  31.7 20.1 %all_to_all.111 = bf16[32,64,128]{2,1,0:T(8,128)(2,1)S(1)} all-to-all(bf16[32,64,128]{2,1,0:T(8,128)(2,1)S(1)} %broadcast_in_dim.16), channel_id=1, replica_groups=mesh['dp'=16,'mp'=32] {'mp'}, dimensions={0} | all-to-all | bytes 1048576 | tf_op jit(solution)/shard_map/all_to_all | solution.py:195
  51.7 0.0 copy-done.4
  51.7 0.4 convolution_bitcast_fusion.2
  52.1 0.1 copy.9
  52.2 23.0 %all_to_all.112 = f32[16,16,128]{2,1,0:T(8,128)S(1)} all-to-all(f32[16,16,128]{2,1,0:T(8,128)S(1)} %bitcast.52), channel_id=1, replica_groups=mesh['dp'=16,'mp'=32] {'dp'}, dimensions={0} | all-to-all | bytes 262144 | tf_op jit(solution)/shard_map/all_to_all | solution.py:195
  75.3 11.6 %all_to_all.113 = f32[16,16,128]{2,1,0:T(8,128)S(1)} all-to-all(f32[16,16,128]{2,1,0:T(8,128)S(1)} %broadcast_in_dim.17), channel_id=1, replica_groups=mesh['dp'=16,'mp'=32] {'dp'}, dimensions={0} | all-to-all | bytes 262144 | tf_op jit(solution)/shard_map/all_to_all | solution.py:195
  86.9 0.6 shard_map.50
  87.5 21.2 %all_to_all.114 = f32[4,640,128]{2,1,0:T(8,128)S(1)} all-to-all(f32[4,640,128]{2,1,0:T(8,128)S(1)} %shard_map.50), channel_id=1, replica_groups={{0,1,2,3},{4,5,6,7},{8,9,10,11},{12,13,14,15},{16,17,18,19},{20,21,22,2..., dimensions={0} | all-to-all | bytes 2621440 | tf_op jit(solution)/shard_map/all_to_all | solution.py:195
  108.7 0.1 slice_reduce_fusion.2
  108.7 0.0 copy-start.1
  108.8 15.3 %all_to_all.115 = f32[8,80,128]{2,1,0:T(8,128)S(1)} all-to-all(f32[8,80,128]{2,1,0:T(8,128)S(1)} %pad_maximum_fusion), channel_id=1, replica_groups={{0,4,8,12,16,20,24,28},{1,5,9,13,17,21,25,29},{2,6,10,14,18,22,26,30},{..., dimensions={0} | all-to-all | bytes 655360 | tf_op jit(solution)/shard_map/all_to_all | solution.py:195
  124.1 13.3 %all_to_all.116.pieces_ref = f32[8,80,128]{2,1,0:T(8,128)S(1)} all-to-all(f32[8,80,128]{2,1,0:T(8,128)S(1)} %broadcast_in_dim.18), channel_id=1, replica_groups={{0,4,8,12,16,20,24,28},{1,5,9,13,17,21,25,29},{2,6,10,14,18,22,26,30},{..., dimensions={0} | all-to-all | bytes 655360 | tf_op jit(solution)/shard_map/all_to_all | solution.py:195
  137.5 5.7 %shard_map.51 = (bf16[4,512,128]{2,1,0:T(8,128)(2,1)S(1)}, f32[128,128]{1,0:T(8,128)}) custom-call(f32[8,80,128]{2,1,0:T(8,128)S(1)} %all_to_all.116.pieces_ref), custom_call_target="tpu_custom_call" | custom-call | tf_op jit(solution)/shard_map/pallas_call | solution.py:106
  143.2 9.3 %all_to_all.117 = bf16[4,512,128]{2,1,0:T(8,128)(2,1)S(1)} all-to-all(bf16[4,512,128]{2,1,0:T(8,128)(2,1)S(1)} %get-tuple-element.6), channel_id=1, replica_groups={{0,1,2,3},{4,5,6,7},{8,9,10,11},{12,13,14,15},{16,17,18,19},{20,21,22,2..., dimensions={0} | all-to-all | bytes 1048576 | tf_op jit(solution)/shard_map/all_to_all | solution.py:195
  152.6 0.0 copy-done.1
  152.6 0.7 convolution_bitcast_fusion
  153.3 0.2 copy.10
  153.5 22.8 %all_to_all.118 = f32[16,56,128]{2,1,0:T(8,128)S(1)} all-to-all(f32[16,56,128]{2,1,0:T(8,128)S(1)} %bitcast.46), channel_id=1, replica_groups=mesh['dp'=16,'mp'=32] {'dp'}, dimensions={0} | all-to-all | bytes 917504 | tf_op jit(solution)/shard_map/all_to_all | solution.py:195
  176.4 14.1 %all_to_all.119 = f32[8,56,128]{2,1,0:T(8,128)S(1)} all-to-all(f32[8,56,128]{2,1,0:T(8,128)S(1)} %broadcast_in_dim.19), channel_id=1, replica_groups={{0,64,128,192,256,320,384,448},{32,96,160,224,288,352,416,480},{1,65,12..., dimensions={0} | all-to-all | bytes 458752 | tf_op jit(solution)/shard_map/all_to_all | solution.py:195
  190.5 2.2 all_gather.6.sketch_ref
  192.7 0.0 copy-start.2
  192.7 2.0 copy-done.2
  194.8 1.7 shard_map.52
  196.4 20.1 %all_to_all.120 = f32[4,640,128]{2,1,0:T(8,128)S(1)} all-to-all(f32[4,640,128]{2,1,0:T(8,128)S(1)} %shard_map.52), channel_id=1, replica_groups={{0,1,2,3},{4,5,6,7},{8,9,10,11},{12,13,14,15},{16,17,18,19},{20,21,22,2..., dimensions={0} | all-to-all | bytes 2621440 | tf_op jit(solution)/shard_map/all_to_all | solution.py:195
  216.6 0.1 slice_reduce_fusion.1
  216.6 13.4 %all_to_all.121 = f32[8,80,128]{2,1,0:T(8,128)S(1)} all-to-all(f32[8,80,128]{2,1,0:T(8,128)S(1)} %pad_maximum_fusion.1), channel_id=1, replica_groups={{0,4,8,12,16,20,24,28},{1,5,9,13,17,21,25,29},{2,6,10,14,18,22,26,30},{..., dimensions={0} | all-to-all | bytes 655360 | tf_op jit(solution)/shard_map/all_to_all | solution.py:195
  230.1 13.2 %all_to_all.122.pieces_ref = f32[8,80,128]{2,1,0:T(8,128)S(1)} all-to-all(f32[8,80,128]{2,1,0:T(8,128)S(1)} %broadcast_in_dim.20), channel_id=1, replica_groups={{0,4,8,12,16,20,24,28},{1,5,9,13,17,21,25,29},{2,6,10,14,18,22,26,30},{..., dimensions={0} | all-to-all | bytes 655360 | tf_op jit(solution)/shard_map/all_to_all | solution.py:195
  243.3 5.7 %shard_map.53 = (bf16[4,512,128]{2,1,0:T(8,128)(2,1)S(1)}, f32[128,128]{1,0:T(8,128)}) custom-call(f32[8,80,128]{2,1,0:T(8,128)S(1)} %all_to_all.122.pieces_ref), custom_call_target="tpu_custom_call" | custom-call | tf_op jit(solution)/shard_map/pallas_call | solution.py:106
  249.1 9.3 %all_to_all.123 = bf16[4,512,128]{2,1,0:T(8,128)(2,1)S(1)} all-to-all(bf16[4,512,128]{2,1,0:T(8,128)(2,1)S(1)} %get-tuple-element.7), channel_id=1, replica_groups={{0,1,2,3},{4,5,6,7},{8,9,10,11},{12,13,14,15},{16,17,18,19},{20,21,22,2..., dimensions={0} | all-to-all | bytes 1048576 | tf_op jit(solution)/shard_map/all_to_all | solution.py:195
  258.4 0.4 convolution_bitcast_fusion.1
  258.8 0.1 copy.12
  258.9 17.1 %all_to_all.124 = f32[16,16,128]{2,1,0:T(8,128)S(1)} all-to-all(f32[16,16,128]{2,1,0:T(8,128)S(1)} %bitcast.53), channel_id=1, replica_groups=mesh['dp'=16,'mp'=32] {'dp'}, dimensions={0} | all-to-all | bytes 262144 | tf_op jit(solution)/shard_map/all_to_all | solution.py:195
  276.1 11.6 %all_to_all.125 = f32[16,16,128]{2,1,0:T(8,128)S(1)} all-to-all(f32[16,16,128]{2,1,0:T(8,128)S(1)} %broadcast_in_dim.21), channel_id=1, replica_groups=mesh['dp'=16,'mp'=32] {'dp'}, dimensions={0} | all-to-all | bytes 262144 | tf_op jit(solution)/shard_map/all_to_all | solution.py:195
  287.6 0.6 shard_map.54
  288.2 16.5 %all_to_all.126 = bf16[4,896,128]{2,1,0:T(8,128)(2,1)S(1)} all-to-all(bf16[4,896,128]{2,1,0:T(8,128)(2,1)S(1)} %shard_map.54), channel_id=1, replica_groups={{0,1,2,3},{4,5,6,7},{8,9,10,11},{12,13,14,15},{16,17,18,19},{20,21,22,2..., dimensions={0} | all-to-all | bytes 1835008 | tf_op jit(solution)/shard_map/all_to_all | solution.py:195
  304.8 0.1 convert_element_type.53
  304.9 0.1 slice_reduce_fusion
  305.1 12.9 %all_to_all.127 = bf16[8,112,128]{2,1,0:T(8,128)(2,1)S(1)} all-to-all(bf16[8,112,128]{2,1,0:T(8,128)(2,1)S(1)} %pad_maximum_fusion.2), channel_id=1, replica_groups={{0,4,8,12,16,20,24,28},{1,5,9,13,17,21,25,29},{2,6,10,14,18,22,26,30},{..., dimensions={0} | all-to-all | bytes 458752 | tf_op jit(solution)/shard_map/all_to_all | solution.py:195
  318.1 11.2 %all_to_all.128.pieces_ref = bf16[8,112,128]{2,1,0:T(8,128)(2,1)S(1)} all-to-all(bf16[8,112,128]{2,1,0:T(8,128)(2,1)S(1)} %broadcast_in_dim.22), channel_id=1, replica_groups={{0,4,8,12,16,20,24,28},{1,5,9,13,17,21,25,29},{2,6,10,14,18,22,26,30},{..., dimensions={0} | all-to-all | bytes 458752 | tf_op jit(solution)/shard_map/all_to_all | solution.py:195
  329.4 5.2 %shard_map.55 = (bf16[4,128,512]{2,1,0:T(8,128)(2,1)S(1)}, f32[128,128]{1,0:T(8,128)S(1)}) custom-call(bf16[8,112,128]{2,1,0:T(8,128)(2,1)S(1)} %all_to_all.128.pieces_ref), custom_call_target="tpu_custom_call" | custom-call | tf_op jit(solution)/shard_map/pallas_call | solution.py:106
  334.6 9.3 %all_to_all.129.rows_ref = bf16[4,128,512]{2,1,0:T(8,128)(2,1)S(1)} all-to-all(bf16[4,128,512]{2,1,0:T(8,128)(2,1)S(1)} %get-tuple-element.9), channel_id=1, replica_groups={{0,1,2,3},{4,5,6,7},{8,9,10,11},{12,13,14,15},{16,17,18,19},{20,21,22,2..., dimensions={0} | all-to-all | bytes 1048576 | tf_op jit(solution)/shard_map/all_to_all | solution.py:195
  343.9 0.0 copy-start.3
  343.9 2.0 copy-done.3
  346.0 0.7 shard_map.56
  346.7 22.8 %all_to_all.130 = f32[16,8,896]{2,1,0:T(8,128)S(1)} all-to-all(f32[16,8,896]{2,1,0:T(8,128)S(1)} %shard_map.56), channel_id=1, replica_groups=mesh['dp'=16,'mp'=32] {'dp'}, dimensions={0} | all-to-all | bytes 917504 | tf_op jit(solution)/shard_map/all_to_all | solution.py:195
  369.6 0.7 broadcast_in_dim.23
  370.2 3.4 all-to-all-start.21
  373.6 0.9 convolution_multiply_fusion
  374.5 8.2 %all-to-all-done.21 = bf16[8,8,896]{2,1,0:T(8,128)(2,1)S(1)} async-done(((bf16[8,8,896]{2,1,0:T(8,128)(2,1)}), bf16[8,8,896]{2,1,0:T(8,128)(2,1)S(1)}, u32[]{:S(2)}, u32[]{:S(2)}) %all-to-all-start.21) | async-done | bytes 114720 | tf_op jit(solution)/shard_map/all_to_all | solution.py:195
  382.8 2.0 all_gather.7
  384.8 0.8 convert_element_type.65
  (31 shorter events, 0.6 us)
Async XLA Ops:
  0.6 0.9 copy-start
  4.7 47.0 %copy-start.4 = (bf16[2048,256]{1,0:T(8,128)(2,1)S(1)}, bf16[2048,256]{1,0:T(8,128)(2,1)}, u32[]{:S(2)}) copy-start(bf16[2048,256]{1,0:T(8,128)(2,1)} %data_ref.5) | copy-start | bytes 3145732
  108.7 43.9 %copy-start.1 = (bf16[2048,896]{1,0:T(8,128)(2,1)S(1)}, bf16[2048,896]{1,0:T(8,128)(2,1)}, u32[]{:S(2)}) copy-start(bf16[2048,896]{1,0:T(8,128)(2,1)} %grads_ref.1) | copy-start | bytes 11010052
  192.7 2.0 copy-start.2
  343.9 2.0 copy-start.3
  370.2 12.6 %all-to-all-start.21 = ((bf16[8,8,896]{2,1,0:T(8,128)(2,1)}), bf16[8,8,896]{2,1,0:T(8,128)(2,1)S(1)}, u32[]{:S(2)}, u32[]{:S(2)}) async-start(bf16[8,8,896]{2,1,0:T(8,128)(2,1)} %broadcast_in_dim.23), calls=%async_computation.21 | async-start | bytes 229376 | tf_op jit(solution)/shard_map/all_to_all | solution.py:195

commit v7 on v6

--- a/solution.py
+++ b/solution.py
@@ -22,6 +22,7 @@
 CORE_GROUPS = [[z * N_CORE + core for core in range(N_CORE)] for z in range(N_Z)]
 Z_GROUPS = [[z * N_CORE + core for z in range(N_Z)] for core in range(N_CORE)]
 HIGHEST = lax.Precision.HIGHEST
+VMEM_SPEC = pl.BlockSpec(memory_space=pltpu.VMEM)
 
 
 def spread(value):
@@ -74,10 +75,9 @@
     )
 
 
-def normalise_kernel(transposed, pieces_ref, rows_ref, inverse_ref):
+def gram_groups(pieces_ref, span):
     parts = 1 if pieces_ref.dtype == jnp.float32 else PARTS
     depth = K // N_Y
-    span = pieces_ref.shape[1] - parts * depth
     groups = []
     for y in range(N_Y):
         whole = pieces_ref[y, span:span + depth, :].astype(jnp.float32)
@@ -85,28 +85,39 @@
             start = span + part * depth
             whole = whole + pieces_ref[y, start:start + depth, :].astype(jnp.float32)
         groups += [whole[start:start + 8, :] for start in range(0, depth, 8)]
-    inverse_factor(groups, inverse_ref)
+    return groups
+
+
+def inverse_kernel(span, pieces_ref, inverse_ref):
+    inverse_factor(gram_groups(pieces_ref, span), inverse_ref)
+
+
+def inverse_of(pieces, span):
+    return pl.pallas_call(
+        functools.partial(inverse_kernel, span),
+        out_shape=jax.ShapeDtypeStruct((K, K), jnp.float32),
+        in_specs=[VMEM_SPEC],
+        compiler_params=pltpu.CompilerParams(vmem_limit_bytes=16 << 20),
+        cost_estimate=pl.CostEstimate(
+            flops=4 * K ** 3, bytes_accessed=pieces.size * 2 + 4 * K * K, transcendentals=K
+        ),
+    )(pieces)
+
+
+def normalise_kernel(span, pieces_ref, rows_ref, inverse_ref):
+    inverse_factor(gram_groups(pieces_ref, span), inverse_ref)
     for y in range(N_Y):
-        product = pieces_ref[y, :span, :].astype(jnp.float32)
-        spot = slice(span * y, span * (y + 1))
-        if transposed:
-            rows = nt_product(inverse_ref[...], product).astype(rows_ref.dtype)
-        else:
-            rows = nt_product(product, inverse_ref[...]).astype(rows_ref.dtype)
+        rows = nt_product(pieces_ref[y, :span, :], inverse_ref[...]).astype(rows_ref.dtype)
         for x in range(N_X):
-            if transposed:
-                rows_ref[x, :, spot] = rows
-            else:
-                rows_ref[x, spot, :] = rows
-
-
-def normalise(pieces, span, transposed):
-    quarter = N_Y * span
-    shape = (N_X, K, quarter) if transposed else (N_X, quarter, K)
+            rows_ref[x, span * y:span * (y + 1), :] = rows
+
+
+def normalise(pieces, span):
     return pl.pallas_call(
-        functools.partial(normalise_kernel, transposed),
+        functools.partial(normalise_kernel, span),
         out_shape=(
-            jax.ShapeDtypeStruct(shape, jnp.bfloat16), jax.ShapeDtypeStruct((K, K), jnp.float32)
+            jax.ShapeDtypeStruct((N_X, N_Y * span, K), jnp.bfloat16),
+            jax.ShapeDtypeStruct((K, K), jnp.float32),
         ),
         compiler_params=pltpu.CompilerParams(vmem_limit_bytes=16 << 20),
     )(pieces)
@@ -120,60 +131,102 @@
     return parts
 
 
-def products_kernel(data_ref, sketch_ref, blocks_ref):
-    tokens = data_ref.shape[0]
-    quarter, chunk = tokens // N_X, tokens // CHUNKS
+def streaming(kernel):
+    def streamed(wide_ref, *refs):
+        refs, held_ref, arrived = refs[:-2], refs[-2], refs[-1]
+        chunk = wide_ref.shape[0] // CHUNKS
+        copies = []
+        for i in range(CHUNKS):
+            rows = pl.ds(chunk * i, chunk)
+            copies.append(
+                pltpu.make_async_copy(wide_ref.at[rows], held_ref.at[rows], arrived.at[i])
+            )
+            copies[i].start()
+
+        def wide(i):
+            copies[i].wait()
+            return held_ref[chunk * i:chunk * (i + 1), :]
+
+        kernel(wide, *refs)
+
+    return streamed
+
+
+def call_streaming(kernel, out_shape, wide, *others):
+    return pl.pallas_call(
+        streaming(kernel),
+        out_shape=out_shape,
+        in_specs=[pl.BlockSpec(memory_space=pltpu.HBM)] + [VMEM_SPEC] * len(others),
+        scratch_shapes=[
+            pltpu.VMEM(wide.shape, wide.dtype), pltpu.SemaphoreType.DMA((CHUNKS,))
+        ],
+        compiler_params=pltpu.CompilerParams(vmem_limit_bytes=51 << 20),
+    )(wide, *others)
+
+
+def probe_kernel(wide, probe_ref, product_ref):
+    chunk = product_ref.shape[0] // CHUNKS
+    for i in range(CHUNKS):
+        product = jnp.dot(wide(i), probe_ref[...], preferred_element_type=jnp.float32)
+        product_ref[chunk * i:chunk * (i + 1), :] = product.astype(product_ref.dtype)
+
+
+def products_kernel(wide, sketch_ref, blocks_ref):
+    whole = blocks_ref.dtype == jnp.float32
+    quarter = blocks_ref.shape[1] - K * (1 if whole else PARTS)
+    chunk = N_X * quarter // CHUNKS
     sketch = sketch_ref[...]
     gram = lax.dot_general(
         sketch, sketch, (((0,), (0,)), ((), ())), precision=HIGHEST,
         preferred_element_type=jnp.float32,
     )
-    whole = blocks_ref.dtype == jnp.float32
     for i, part in enumerate([gram] if whole else parts_in(gram, PARTS)):
         for x in range(N_X):
             blocks_ref[x, quarter + K * i:quarter + K * (i + 1), :] = part
     both = jnp.concatenate(parts_in(sketch, 2), axis=1)
     for i in range(CHUNKS):
-        product = jnp.dot(
-            data_ref[chunk * i:chunk * (i + 1), :], both, preferred_element_type=jnp.float32
-        )
+        product = jnp.dot(wide(i), both, preferred_element_type=jnp.float32)
         product = product[:, :K] + product[:, K:]
         start = chunk * i % quarter
         blocks_ref[chunk * i // quarter, start:start + chunk, :] = product.astype(blocks_ref.dtype)
 
 
-def product_blocks(data, sketch, held_as):
+def resident_products_kernel(data_ref, sketch_ref, blocks_ref):
+    chunk = data_ref.shape[0] // CHUNKS
+    products_kernel(lambda i: data_ref[chunk * i:chunk * (i + 1), :], sketch_ref, blocks_ref)
+
+
+def product_blocks(data, sketch, held_as, streamed):
     rows = data.shape[0] // N_X + K * (1 if held_as == jnp.float32 else PARTS)
+    out_shape = jax.ShapeDtypeStruct((N_X, rows, K), held_as)
+    if streamed:
+        return call_streaming(products_kernel, out_shape, data, sketch)
     return pl.pallas_call(
-        products_kernel,
-        out_shape=jax.ShapeDtypeStruct((N_X, rows, K), held_as),
-        in_specs=[pl.BlockSpec(memory_space=pltpu.VMEM)] * 2,
+        resident_products_kernel,
+        out_shape=out_shape,
+        in_specs=[VMEM_SPEC] * 2,
         compiler_params=pltpu.CompilerParams(vmem_limit_bytes=24 << 20),
     )(data, sketch)
 
 
-def projection_kernel(rows_ref, grads_ref, blocks_ref):
-    quarter = rows_ref.shape[2]
-    total = jnp.zeros((K, grads_ref.shape[1]), jnp.float32)
-    for x in range(N_X):
-        total = total + jnp.dot(
-            rows_ref[x], grads_ref[quarter * x:quarter * (x + 1), :],
-            preferred_element_type=jnp.float32,
+def projection_kernel(wide, rows_ref, inverse_ref, blocks_ref):
+    quarter = rows_ref.shape[1]
+    chunk = N_X * quarter // CHUNKS
+    total = jnp.zeros((K, blocks_ref.shape[2]), jnp.float32)
+    for i in range(CHUNKS):
+        start = chunk * i % quarter
+        rows = rows_ref[chunk * i // quarter, start:start + chunk, :]
+        total = total + lax.dot_general(
+            rows, wide(i), (((0,), (0,)), ((), ())), preferred_element_type=jnp.float32
         )
+    total = jnp.dot(
+        inverse_ref[...], total, precision=HIGHEST, preferred_element_type=jnp.float32
+    )
     depth = K // N_DP
     for z in range(N_Z):
         for core in range(N_CORE):
             start = (core * N_Z + z) * depth
             blocks_ref[z * N_CORE + core] = total[start:start + depth, :]
-
-
-def projection_blocks(rows, grads):
-    return pl.pallas_call(
-        projection_kernel,
-        out_shape=jax.ShapeDtypeStruct((N_DP, K // N_DP, grads.shape[1]), jnp.float32),
-        in_specs=[pl.BlockSpec(memory_space=pltpu.VMEM)] * 2,
-        compiler_params=pltpu.CompilerParams(vmem_limit_bytes=24 << 20),
-    )(rows, grads)
 
 
 def rows_product(left, right):
@@ -217,11 +270,11 @@
 
 def staged_sum_over_tokens(blocks, held_as):
     mine = scatter_sum(blocks, "dp").astype(held_as)
-    mine = gather(mine, "dp", N_Z, Z_GROUPS).reshape(-1, blocks.shape[2])
+    mine = gather(mine, "dp", N_Z, Z_GROUPS).reshape(-1, blocks.shape[2]).astype(jnp.float32)
     return lax.all_gather(mine, "dp", axis_index_groups=CORE_GROUPS, tiled=True)
 
 
-def token_rows_of(data, sketch, held_as, transposed):
+def token_sums_of(data, sketch, held_as, streamed):
     tokens = data.shape[0]
     parts = 1 if held_as == jnp.float32 else PARTS
     quarter, span, depth = tokens // N_X, tokens // N_MP, K // N_Y
@@ -234,7 +287,7 @@
         pieces = received[:, rows:].reshape(received.shape[0], parts, -1, K)
         return jnp.sum(received[:, :rows], axis=0), jnp.sum(jnp.sum(pieces, axis=1), axis=0)
 
-    blocks = product_blocks(data, sketch, held_as)
+    blocks = product_blocks(data, sketch, held_as, streamed)
     product, gram = total(exchange(blocks, "mp", X_GROUPS), quarter)
     blocks = jnp.concatenate(
         [product.astype(held_as).reshape(N_Y, span, K)]
@@ -242,30 +295,42 @@
     )
     product, gram = total(exchange(blocks, "mp", Y_GROUPS), span)
     pieces = jnp.concatenate([product.astype(held_as)] + parts_of(gram), axis=0)
-    rows, inverse = normalise(gather(pieces, "mp", N_Y, Y_GROUPS), span, transposed)
-    return exchange(rows, "mp", X_GROUPS), inverse
+    return gather(pieces, "mp", N_Y, Y_GROUPS), span
+
+
+def token_rows_of(data, sketch, streamed):
+    rows, _ = normalise(*token_sums_of(data, sketch, jnp.float32, streamed))
+    return exchange(rows, "mp", X_GROUPS).reshape(data.shape[0], K)
 
 
 def on_device(activations, output_grads, probe_matrix):
     tokens = activations.shape[0]
-    partial_value = jnp.dot(output_grads, probe_matrix, preferred_element_type=jnp.float32)
-    partial_value = partial_value.astype(jnp.bfloat16).reshape(N_MP, tokens // N_MP, K)
-    mine = scatter_sum(partial_value, "mp").astype(jnp.bfloat16)
+    partial_value = call_streaming(
+        probe_kernel, jax.ShapeDtypeStruct((tokens, K), jnp.bfloat16), output_grads, probe_matrix
+    )
+    mine = scatter_sum(partial_value.reshape(N_MP, tokens // N_MP, K), "mp").astype(jnp.bfloat16)
     probe_rows = gather(mine, "mp", N_MP).reshape(tokens, K)
 
     sketch = sum_over_tokens(rows_product(activations, probe_rows))
-    token_rows, _ = token_rows_of(activations, sketch, jnp.float32, False)
-    partial_value = rows_product(output_grads, token_rows.reshape(tokens, K))
+    token_rows = token_rows_of(activations, sketch, False)
+    partial_value = rows_product(output_grads, token_rows)
     back_sketch = staged_sum_over_tokens(blocks_over_tokens(partial_value), jnp.float32)
-    unit_rows, _ = token_rows_of(output_grads, back_sketch, jnp.float32, False)
-    power_sketch = sum_over_tokens(rows_product(activations, unit_rows.reshape(tokens, K)))
-    last_rows, inverse = token_rows_of(activations, power_sketch, jnp.bfloat16, True)
-    projection = staged_sum_over_tokens(projection_blocks(last_rows, output_grads), jnp.bfloat16)
+    unit_rows = token_rows_of(output_grads, back_sketch, True)
+    power_sketch = sum_over_tokens(rows_product(activations, unit_rows))
+    pieces, span = token_sums_of(activations, power_sketch, jnp.bfloat16, False)
+    inverse = inverse_of(pieces, span)
+    products = gather(pieces[:, :span].reshape(tokens // N_X, K), "mp", N_X, X_GROUPS)
+    blocks = call_streaming(
+        projection_kernel,
+        jax.ShapeDtypeStruct((N_DP, K // N_DP, output_grads.shape[1]), jnp.float32),
+        output_grads, products, inverse,
+    )
+    projection = staged_sum_over_tokens(blocks, jnp.bfloat16)
     third_basis = lax.dot_general(
         power_sketch, inverse, (((1,), (1,)), ((), ())), precision=HIGHEST,
         preferred_element_type=jnp.float32,
     )
-    return (third_basis * jnp.sqrt(jnp.float32(H)), projection.astype(jnp.float32))
+    return (third_basis * jnp.sqrt(jnp.float32(H)), projection)
 
 
 def solution(mesh):

time: 387 us -> 386 us (level)
  blocking collectives: 339 us -> 330 us
  Pallas kernels: 20.2 us -> 28.4 us
    all_to_all x21 -> x20, blocking collectives: 335 us -> 326 us  [exchange(): return lax.all_to_all(blocks, axis, 0, 0, axis_index_groups=groups)]
    pallas_call x7 -> x8, Pallas kernels: 20.2 us -> 28.4 us  [the longest x3 11.8 us: call_streaming(): pl.pallas_call(streaming(kernel), out_shape=out_shape, in_specs=[pl.Block...]
    all_to_all x1 -> x2, waiting for transfers between devices: 8.24 us -> 10.9 us  [exchange(): return lax.all_to_all(blocks, axis, 0, 0, axis_index_groups=groups)]
  transfers between devices with their start and end apart: 1 -> 2, of which waited for: 1 -> 2; matrix products, arithmetic and copies ran while one was open for 0% -> 0% of each run, Pallas kernels for 0% -> 1%
where the time goes in v7:
time: 386 us; the launch traced here: 385 us
  blocking collectives  330 us (85%)
  Pallas kernels  28.4 us (7%)
  waiting for transfers between devices  10.9 us (3%)
  starting transfers between devices  7.06 us (2%)
    all_to_all x20, blocking collectives, exchange(): return lax.all_to_all(blocks, axis, 0, 0, axis_index_groups=groups)  326 us
    pallas_call x3, Pallas kernels, call_streaming(): pl.pallas_call(streaming(kernel), out_shape=out_shape, in_specs=[pl.Block...  11.8 us
    pallas_call x2, Pallas kernels, normalise(): pl.pallas_call(functools.partial(normalise_kernel, span), out_shape=(jax....  11.4 us
    all_to_all x2, waiting for transfers between devices, exchange(): return lax.all_to_all(blocks, axis, 0, 0, axis_index_groups=groups)  10.9 us
  transfers between devices with their start and end apart: 2, of which 2 were waited for; matrix products, arithmetic and copies ran while one was open for 0% of the time, Pallas kernels for 1%

profile of v7, /device:TPU:1, one launch (start us, length us, event | category | flops | bytes accessed | tf_op | source)
XLA Modules:
  0.0 384.8 jit_solution(11504007341151619898)
XLA Ops:
  0.6 0.0 copy-start.1
  0.6 0.9 copy-done.1
  1.6 3.4 shard_map.50
  5.0 26.6 %all_to_all.110 = bf16[32,64,128]{2,1,0:T(8,128)(2,1)S(1)} all-to-all(bf16[32,64,128]{2,1,0:T(8,128)(2,1)S(1)} %bitcast.39), channel_id=1, replica_groups=mesh['dp'=16,'mp'=32] {'mp'}, dimensions={0} | all-to-all | bytes 1048576 | tf_op jit(solution)/shard_map/all_to_all | solution.py:248
  31.5 0.0 copy-start
  31.5 0.1 reduce_sum.196
  31.6 0.1 broadcast_in_dim.20
  31.7 20.2 %all_to_all.111 = bf16[32,64,128]{2,1,0:T(8,128)(2,1)S(1)} all-to-all(bf16[32,64,128]{2,1,0:T(8,128)(2,1)S(1)} %broadcast_in_dim.20), channel_id=1, replica_groups=mesh['dp'=16,'mp'=32] {'mp'}, dimensions={0} | all-to-all | bytes 1048576 | tf_op jit(solution)/shard_map/all_to_all | solution.py:248
  51.9 0.0 copy-done
  52.0 0.4 convolution_bitcast_fusion.2
  52.3 0.1 copy.9
  52.4 23.0 %all_to_all.112 = f32[16,16,128]{2,1,0:T(8,128)S(1)} all-to-all(f32[16,16,128]{2,1,0:T(8,128)S(1)} %bitcast.54), channel_id=1, replica_groups=mesh['dp'=16,'mp'=32] {'dp'}, dimensions={0} | all-to-all | bytes 262144 | tf_op jit(solution)/shard_map/all_to_all | solution.py:248
  75.5 11.6 %all_to_all.113 = f32[16,16,128]{2,1,0:T(8,128)S(1)} all-to-all(f32[16,16,128]{2,1,0:T(8,128)S(1)} %broadcast_in_dim.21), channel_id=1, replica_groups=mesh['dp'=16,'mp'=32] {'dp'}, dimensions={0} | all-to-all | bytes 262144 | tf_op jit(solution)/shard_map/all_to_all | solution.py:248
  87.1 0.6 shard_map.51
  87.7 21.2 %all_to_all.114 = f32[4,640,128]{2,1,0:T(8,128)S(1)} all-to-all(f32[4,640,128]{2,1,0:T(8,128)S(1)} %shard_map.51), channel_id=1, replica_groups={{0,1,2,3},{4,5,6,7},{8,9,10,11},{12,13,14,15},{16,17,18,19},{20,21,22,2..., dimensions={0} | all-to-all | bytes 2621440 | tf_op jit(solution)/shard_map/all_to_all | solution.py:248
  108.9 0.1 slice_reduce_fusion.2
  108.9 0.0 copy-start.2
  109.0 15.3 %all_to_all.115 = f32[8,80,128]{2,1,0:T(8,128)S(1)} all-to-all(f32[8,80,128]{2,1,0:T(8,128)S(1)} %pad_maximum_fusion), channel_id=1, replica_groups={{0,4,8,12,16,20,24,28},{1,5,9,13,17,21,25,29},{2,6,10,14,18,22,26,30},{..., dimensions={0} | all-to-all | bytes 655360 | tf_op jit(solution)/shard_map/all_to_all | solution.py:248
  124.4 13.3 %all_to_all.116.pieces_ref = f32[8,80,128]{2,1,0:T(8,128)S(1)} all-to-all(f32[8,80,128]{2,1,0:T(8,128)S(1)} %broadcast_in_dim.22), channel_id=1, replica_groups={{0,4,8,12,16,20,24,28},{1,5,9,13,17,21,25,29},{2,6,10,14,18,22,26,30},{..., dimensions={0} | all-to-all | bytes 655360 | tf_op jit(solution)/shard_map/all_to_all | solution.py:248
  137.7 5.7 %shard_map.52 = (bf16[4,512,128]{2,1,0:T(8,128)(2,1)S(1)}, f32[128,128]{1,0:T(8,128)}) custom-call(f32[8,80,128]{2,1,0:T(8,128)S(1)} %all_to_all.116.pieces_ref), custom_call_target="tpu_custom_call" | custom-call | tf_op jit(solution)/shard_map/pallas_call | solution.py:116
  143.4 9.3 %all_to_all.117 = bf16[4,512,128]{2,1,0:T(8,128)(2,1)S(1)} all-to-all(bf16[4,512,128]{2,1,0:T(8,128)(2,1)S(1)} %get-tuple-element.4), channel_id=1, replica_groups={{0,1,2,3},{4,5,6,7},{8,9,10,11},{12,13,14,15},{16,17,18,19},{20,21,22,2..., dimensions={0} | all-to-all | bytes 1048576 | tf_op jit(solution)/shard_map/all_to_all | solution.py:248
  152.8 0.0 copy-done.2
  152.8 0.7 convolution_bitcast_fusion
  153.5 0.2 copy.10
  153.8 22.8 %all_to_all.118 = f32[16,56,128]{2,1,0:T(8,128)S(1)} all-to-all(f32[16,56,128]{2,1,0:T(8,128)S(1)} %bitcast.47), channel_id=1, replica_groups=mesh['dp'=16,'mp'=32] {'dp'}, dimensions={0} | all-to-all | bytes 917504 | tf_op jit(solution)/shard_map/all_to_all | solution.py:248
  176.7 14.1 %all_to_all.119 = f32[8,56,128]{2,1,0:T(8,128)S(1)} all-to-all(f32[8,56,128]{2,1,0:T(8,128)S(1)} %broadcast_in_dim.23), channel_id=1, replica_groups={{0,64,128,192,256,320,384,448},{32,96,160,224,288,352,416,480},{1,65,12..., dimensions={0} | all-to-all | bytes 458752 | tf_op jit(solution)/shard_map/all_to_all | solution.py:248
  190.7 2.4 all_gather.6.refs_0_
  193.1 4.8 %shard_map.53 = f32[4,640,128]{2,1,0:T(8,128)S(1)} custom-call(bf16[2048,896]{1,0:T(8,128)(2,1)} %wide_ref.5, f32[896,128]{1,0:T(8,128)S(1)} %all_gather.6.refs_0_), custom_call_target="tpu_custom_call" | custom-call | tf_op jit(solution)/shard_map/pallas_call | solution.py:156
  197.9 20.1 %all_to_all.120 = f32[4,640,128]{2,1,0:T(8,128)S(1)} all-to-all(f32[4,640,128]{2,1,0:T(8,128)S(1)} %shard_map.53), channel_id=1, replica_groups={{0,1,2,3},{4,5,6,7},{8,9,10,11},{12,13,14,15},{16,17,18,19},{20,21,22,2..., dimensions={0} | all-to-all | bytes 2621440 | tf_op jit(solution)/shard_map/all_to_all | solution.py:248
  218.0 0.1 slice_reduce_fusion.1
  218.1 13.4 %all_to_all.121 = f32[8,80,128]{2,1,0:T(8,128)S(1)} all-to-all(f32[8,80,128]{2,1,0:T(8,128)S(1)} %pad_maximum_fusion.1), channel_id=1, replica_groups={{0,4,8,12,16,20,24,28},{1,5,9,13,17,21,25,29},{2,6,10,14,18,22,26,30},{..., dimensions={0} | all-to-all | bytes 655360 | tf_op jit(solution)/shard_map/all_to_all | solution.py:248
  231.6 13.2 %all_to_all.122.pieces_ref = f32[8,80,128]{2,1,0:T(8,128)S(1)} all-to-all(f32[8,80,128]{2,1,0:T(8,128)S(1)} %broadcast_in_dim.24), channel_id=1, replica_groups={{0,4,8,12,16,20,24,28},{1,5,9,13,17,21,25,29},{2,6,10,14,18,22,26,30},{..., dimensions={0} | all-to-all | bytes 655360 | tf_op jit(solution)/shard_map/all_to_all | solution.py:248
  244.8 5.7 %shard_map.54 = (bf16[4,512,128]{2,1,0:T(8,128)(2,1)S(1)}, f32[128,128]{1,0:T(8,128)}) custom-call(f32[8,80,128]{2,1,0:T(8,128)S(1)} %all_to_all.122.pieces_ref), custom_call_target="tpu_custom_call" | custom-call | tf_op jit(solution)/shard_map/pallas_call | solution.py:116
  250.5 9.3 %all_to_all.123 = bf16[4,512,128]{2,1,0:T(8,128)(2,1)S(1)} all-to-all(bf16[4,512,128]{2,1,0:T(8,128)(2,1)S(1)} %get-tuple-element.5), channel_id=1, replica_groups={{0,1,2,3},{4,5,6,7},{8,9,10,11},{12,13,14,15},{16,17,18,19},{20,21,22,2..., dimensions={0} | all-to-all | bytes 1048576 | tf_op jit(solution)/shard_map/all_to_all | solution.py:248
  259.9 0.4 convolution_bitcast_fusion.1
  260.2 0.1 copy.12
  260.3 17.1 %all_to_all.124 = f32[16,16,128]{2,1,0:T(8,128)S(1)} all-to-all(f32[16,16,128]{2,1,0:T(8,128)S(1)} %bitcast.55), channel_id=1, replica_groups=mesh['dp'=16,'mp'=32] {'dp'}, dimensions={0} | all-to-all | bytes 262144 | tf_op jit(solution)/shard_map/all_to_all | solution.py:248
  277.5 11.6 %all_to_all.125 = f32[16,16,128]{2,1,0:T(8,128)S(1)} all-to-all(f32[16,16,128]{2,1,0:T(8,128)S(1)} %broadcast_in_dim.25), channel_id=1, replica_groups=mesh['dp'=16,'mp'=32] {'dp'}, dimensions={0} | all-to-all | bytes 262144 | tf_op jit(solution)/shard_map/all_to_all | solution.py:248
  289.1 0.6 shard_map.55
  289.7 16.5 %all_to_all.126 = bf16[4,896,128]{2,1,0:T(8,128)(2,1)S(1)} all-to-all(bf16[4,896,128]{2,1,0:T(8,128)(2,1)S(1)} %shard_map.55), channel_id=1, replica_groups={{0,1,2,3},{4,5,6,7},{8,9,10,11},{12,13,14,15},{16,17,18,19},{20,21,22,2..., dimensions={0} | all-to-all | bytes 1835008 | tf_op jit(solution)/shard_map/all_to_all | solution.py:248
  306.2 0.1 convert_element_type.52
  306.3 0.1 slice_reduce_fusion
  306.5 12.9 %all_to_all.127 = bf16[8,112,128]{2,1,0:T(8,128)(2,1)S(1)} all-to-all(bf16[8,112,128]{2,1,0:T(8,128)(2,1)S(1)} %pad_maximum_fusion.2), channel_id=1, replica_groups={{0,4,8,12,16,20,24,28},{1,5,9,13,17,21,25,29},{2,6,10,14,18,22,26,30},{..., dimensions={0} | all-to-all | bytes 458752 | tf_op jit(solution)/shard_map/all_to_all | solution.py:248
  319.6 11.2 %all_to_all.128.pieces_ref = bf16[8,112,128]{2,1,0:T(8,128)(2,1)S(1)} all-to-all(bf16[8,112,128]{2,1,0:T(8,128)(2,1)S(1)} %broadcast_in_dim.26), channel_id=1, replica_groups={{0,4,8,12,16,20,24,28},{1,5,9,13,17,21,25,29},{2,6,10,14,18,22,26,30},{..., dimensions={0} | all-to-all | bytes 458752 | tf_op jit(solution)/shard_map/all_to_all | solution.py:248
  330.9 0.9 broadcast_in_dim.28
  331.7 3.7 all-to-all-start.19
  335.4 4.0 %shard_map.56.refs_1_ = f32[128,128]{1,0:T(8,128)S(1)} custom-call(bf16[8,112,128]{2,1,0:T(8,128)(2,1)S(1)} %all_to_all.128.pieces_ref), custom_call_target="tpu_custom_call" | custom-call | flops 8388608 | bytes 294912 | tf_op jit(solution)/shard_map/pallas_call | solution.py:96
  339.4 2.7 all-to-all-done.19.refs_0_
  342.1 3.7 shard_map.57
  345.8 22.9 %all_to_all.129 = f32[16,8,896]{2,1,0:T(8,128)S(1)} all-to-all(f32[16,8,896]{2,1,0:T(8,128)S(1)} %shard_map.57), channel_id=1, replica_groups=mesh['dp'=16,'mp'=32] {'dp'}, dimensions={0} | all-to-all | bytes 917504 | tf_op jit(solution)/shard_map/all_to_all | solution.py:248
  368.7 0.7 broadcast_in_dim.29
  369.3 3.4 all-to-all-start.21
  372.7 0.9 convolution_multiply_fusion
  373.6 8.2 %all-to-all-done.21 = bf16[8,8,896]{2,1,0:T(8,128)(2,1)S(1)} async-done(((bf16[8,8,896]{2,1,0:T(8,128)(2,1)}), bf16[8,8,896]{2,1,0:T(8,128)(2,1)S(1)}, u32[]{:S(2)}, u32[]{:S(2)}) %all-to-all-start.21) | async-done | bytes 114720 | tf_op jit(solution)/shard_map/all_to_all | solution.py:248
  381.9 2.2 all_gather.7
  384.1 0.8 copy.14
  (33 shorter events, 0.6 us)
Async XLA Ops:
  0.6 0.9 copy-start.1
  31.5 20.4 %copy-start = (bf16[2048,256]{1,0:T(8,128)(2,1)S(1)}, bf16[2048,256]{1,0:T(8,128)(2,1)}, u32[]{:S(2)}) copy-start(bf16[2048,256]{1,0:T(8,128)(2,1)} %data_ref.3) | copy-start | bytes 3145732
  108.9 43.9 %copy-start.2 = (bf16[2048,896]{1,0:T(8,128)(2,1)S(1)}, bf16[2048,896]{1,0:T(8,128)(2,1)}, u32[]{:S(2)}) copy-start(bf16[2048,896]{1,0:T(8,128)(2,1)} %wide_ref.5) | copy-start | bytes 11010052
  331.7 10.4 %all-to-all-start.19 = ((bf16[4,512,128]{2,1,0:T(8,128)(2,1)}), bf16[4,512,128]{2,1,0:T(8,128)(2,1)S(1)}, u32[]{:S(2)}, u32[]{:S(2)}) async-start(bf16[4,512,128]{2,1,0:T(8,128)(2,1)} %broadcast_in_dim.28), calls=%async_computation.19 | async-start | bytes 1048576 | tf_op jit(solution)/shard_map/all_to_all | solution.py:248
  369.3 12.6 %all-to-all-start.21 = ((bf16[8,8,896]{2,1,0:T(8,128)(2,1)}), bf16[8,8,896]{2,1,0:T(8,128)(2,1)S(1)}, u32[]{:S(2)}, u32[]{:S(2)}) async-start(bf16[8,8,896]{2,1,0:T(8,128)(2,1)} %broadcast_in_dim.29), calls=%async_computation.21 | async-start | bytes 229376 | tf_op jit(solution)/shard_map/all_to_all | solution.py:248

commit v8 on v6

--- a/solution.py
+++ b/solution.py
@@ -22,6 +22,7 @@
 CORE_GROUPS = [[z * N_CORE + core for core in range(N_CORE)] for z in range(N_Z)]
 Z_GROUPS = [[z * N_CORE + core for z in range(N_Z)] for core in range(N_CORE)]
 HIGHEST = lax.Precision.HIGHEST
+VMEM_SPEC = pl.BlockSpec(memory_space=pltpu.VMEM)
 
 
 def spread(value):
@@ -74,10 +75,9 @@
     )
 
 
-def normalise_kernel(transposed, pieces_ref, rows_ref, inverse_ref):
+def gram_groups(pieces_ref, span):
     parts = 1 if pieces_ref.dtype == jnp.float32 else PARTS
     depth = K // N_Y
-    span = pieces_ref.shape[1] - parts * depth
     groups = []
     for y in range(N_Y):
         whole = pieces_ref[y, span:span + depth, :].astype(jnp.float32)
@@ -85,28 +85,39 @@
             start = span + part * depth
             whole = whole + pieces_ref[y, start:start + depth, :].astype(jnp.float32)
         groups += [whole[start:start + 8, :] for start in range(0, depth, 8)]
-    inverse_factor(groups, inverse_ref)
+    return groups
+
+
+def inverse_kernel(span, pieces_ref, inverse_ref):
+    inverse_factor(gram_groups(pieces_ref, span), inverse_ref)
+
+
+def inverse_of(pieces, span):
+    return pl.pallas_call(
+        functools.partial(inverse_kernel, span),
+        out_shape=jax.ShapeDtypeStruct((K, K), jnp.float32),
+        in_specs=[VMEM_SPEC],
+        compiler_params=pltpu.CompilerParams(vmem_limit_bytes=16 << 20),
+        cost_estimate=pl.CostEstimate(
+            flops=4 * K ** 3, bytes_accessed=pieces.size * 2 + 4 * K * K, transcendentals=K
+        ),
+    )(pieces)
+
+
+def normalise_kernel(span, pieces_ref, rows_ref, inverse_ref):
+    inverse_factor(gram_groups(pieces_ref, span), inverse_ref)
     for y in range(N_Y):
-        product = pieces_ref[y, :span, :].astype(jnp.float32)
-        spot = slice(span * y, span * (y + 1))
-        if transposed:
-            rows = nt_product(inverse_ref[...], product).astype(rows_ref.dtype)
-        else:
-            rows = nt_product(product, inverse_ref[...]).astype(rows_ref.dtype)
+        rows = nt_product(pieces_ref[y, :span, :], inverse_ref[...]).astype(rows_ref.dtype)
         for x in range(N_X):
-            if transposed:
-                rows_ref[x, :, spot] = rows
-            else:
-                rows_ref[x, spot, :] = rows
-
-
-def normalise(pieces, span, transposed):
-    quarter = N_Y * span
-    shape = (N_X, K, quarter) if transposed else (N_X, quarter, K)
-    return pl.pallas_call(
-        functools.partial(normalise_kernel, transposed),
+            rows_ref[x, span * y:span * (y + 1), :] = rows
+
+
+def normalise(pieces, span):
+    return pl.pallas_call(
+        functools.partial(normalise_kernel, span),
         out_shape=(
-            jax.ShapeDtypeStruct(shape, jnp.bfloat16), jax.ShapeDtypeStruct((K, K), jnp.float32)
+            jax.ShapeDtypeStruct((N_X, N_Y * span, K), jnp.bfloat16),
+            jax.ShapeDtypeStruct((K, K), jnp.float32),
         ),
         compiler_params=pltpu.CompilerParams(vmem_limit_bytes=16 << 20),
     )(pieces)
@@ -147,19 +158,22 @@
     return pl.pallas_call(
         products_kernel,
         out_shape=jax.ShapeDtypeStruct((N_X, rows, K), held_as),
-        in_specs=[pl.BlockSpec(memory_space=pltpu.VMEM)] * 2,
+        in_specs=[VMEM_SPEC] * 2,
         compiler_params=pltpu.CompilerParams(vmem_limit_bytes=24 << 20),
     )(data, sketch)
 
 
-def projection_kernel(rows_ref, grads_ref, blocks_ref):
-    quarter = rows_ref.shape[2]
+def projection_kernel(grads_ref, rows_ref, inverse_ref, blocks_ref):
+    quarter = rows_ref.shape[1]
     total = jnp.zeros((K, grads_ref.shape[1]), jnp.float32)
     for x in range(N_X):
-        total = total + jnp.dot(
-            rows_ref[x], grads_ref[quarter * x:quarter * (x + 1), :],
+        total = total + lax.dot_general(
+            rows_ref[x], grads_ref[quarter * x:quarter * (x + 1), :], (((0,), (0,)), ((), ())),
             preferred_element_type=jnp.float32,
         )
+    total = jnp.dot(
+        inverse_ref[...], total, precision=HIGHEST, preferred_element_type=jnp.float32
+    )
     depth = K // N_DP
     for z in range(N_Z):
         for core in range(N_CORE):
@@ -167,13 +181,13 @@
             blocks_ref[z * N_CORE + core] = total[start:start + depth, :]
 
 
-def projection_blocks(rows, grads):
+def projection_blocks(grads, rows, inverse):
     return pl.pallas_call(
         projection_kernel,
         out_shape=jax.ShapeDtypeStruct((N_DP, K // N_DP, grads.shape[1]), jnp.float32),
-        in_specs=[pl.BlockSpec(memory_space=pltpu.VMEM)] * 2,
+        in_specs=[VMEM_SPEC] * 3,
         compiler_params=pltpu.CompilerParams(vmem_limit_bytes=24 << 20),
-    )(rows, grads)
+    )(grads, rows, inverse)
 
 
 def rows_product(left, right):
@@ -217,11 +231,11 @@
 
 def staged_sum_over_tokens(blocks, held_as):
     mine = scatter_sum(blocks, "dp").astype(held_as)
-    mine = gather(mine, "dp", N_Z, Z_GROUPS).reshape(-1, blocks.shape[2])
+    mine = gather(mine, "dp", N_Z, Z_GROUPS).reshape(-1, blocks.shape[2]).astype(jnp.float32)
     return lax.all_gather(mine, "dp", axis_index_groups=CORE_GROUPS, tiled=True)
 
 
-def token_rows_of(data, sketch, held_as, transposed):
+def token_sums_of(data, sketch, held_as):
     tokens = data.shape[0]
     parts = 1 if held_as == jnp.float32 else PARTS
     quarter, span, depth = tokens // N_X, tokens // N_MP, K // N_Y
@@ -242,30 +256,37 @@
     )
     product, gram = total(exchange(blocks, "mp", Y_GROUPS), span)
     pieces = jnp.concatenate([product.astype(held_as)] + parts_of(gram), axis=0)
-    rows, inverse = normalise(gather(pieces, "mp", N_Y, Y_GROUPS), span, transposed)
-    return exchange(rows, "mp", X_GROUPS), inverse
+    return gather(pieces, "mp", N_Y, Y_GROUPS), span
+
+
+def token_rows_of(data, sketch):
+    rows, _ = normalise(*token_sums_of(data, sketch, jnp.float32))
+    return exchange(rows, "mp", X_GROUPS).reshape(data.shape[0], K)
 
 
 def on_device(activations, output_grads, probe_matrix):
     tokens = activations.shape[0]
     partial_value = jnp.dot(output_grads, probe_matrix, preferred_element_type=jnp.float32)
-    partial_value = partial_value.astype(jnp.bfloat16).reshape(N_MP, tokens // N_MP, K)
-    mine = scatter_sum(partial_value, "mp").astype(jnp.bfloat16)
+    partial_value = partial_value.astype(jnp.bfloat16)
+    mine = scatter_sum(partial_value.reshape(N_MP, tokens // N_MP, K), "mp").astype(jnp.bfloat16)
     probe_rows = gather(mine, "mp", N_MP).reshape(tokens, K)
 
     sketch = sum_over_tokens(rows_product(activations, probe_rows))
-    token_rows, _ = token_rows_of(activations, sketch, jnp.float32, False)
-    partial_value = rows_product(output_grads, token_rows.reshape(tokens, K))
+    token_rows = token_rows_of(activations, sketch)
+    partial_value = rows_product(output_grads, token_rows)
     back_sketch = staged_sum_over_tokens(blocks_over_tokens(partial_value), jnp.float32)
-    unit_rows, _ = token_rows_of(output_grads, back_sketch, jnp.float32, False)
-    power_sketch = sum_over_tokens(rows_product(activations, unit_rows.reshape(tokens, K)))
-    last_rows, inverse = token_rows_of(activations, power_sketch, jnp.bfloat16, True)
-    projection = staged_sum_over_tokens(projection_blocks(last_rows, output_grads), jnp.bfloat16)
+    unit_rows = token_rows_of(output_grads, back_sketch)
+    power_sketch = sum_over_tokens(rows_product(activations, unit_rows))
+    pieces, span = token_sums_of(activations, power_sketch, jnp.bfloat16)
+    inverse = inverse_of(pieces, span)
+    products = gather(pieces[:, :span].reshape(tokens // N_X, K), "mp", N_X, X_GROUPS)
+    blocks = projection_blocks(output_grads, products, inverse)
+    projection = staged_sum_over_tokens(blocks, jnp.bfloat16)
     third_basis = lax.dot_general(
         power_sketch, inverse, (((1,), (1,)), ((), ())), precision=HIGHEST,
         preferred_element_type=jnp.float32,
     )
-    return (third_basis * jnp.sqrt(jnp.float32(H)), projection.astype(jnp.float32))
+    return (third_basis * jnp.sqrt(jnp.float32(H)), projection)
 
 
 def solution(mesh):

time: 387 us -> 384 us (level)
  blocking collectives: 339 us -> 330 us
    all_to_all x21 -> x20, blocking collectives: 335 us -> 326 us  [exchange(): return lax.all_to_all(blocks, axis, 0, 0, axis_index_groups=groups)]
    all_to_all x1 -> x2, waiting for transfers between devices: 8.24 us -> 11.1 us  [exchange(): return lax.all_to_all(blocks, axis, 0, 0, axis_index_groups=groups)]
  transfers between devices with their start and end apart: 1 -> 2, of which waited for: 1 -> 2; matrix products, arithmetic and copies ran while one was open for 0% -> 0% of each run, Pallas kernels for 0% -> 1%
where the time goes in v8:
time: 384 us; the launch traced here: 383 us
  blocking collectives  330 us (86%)
  Pallas kernels  19.4 us (5%)
  waiting for transfers between devices  11.1 us (3%)
  local copies, waits for them, and re-layouts  7.94 us (2%)
  starting transfers between devices  6.84 us (2%)
  matrix products  5.54 us (1%)
    all_to_all x20, blocking collectives, exchange(): return lax.all_to_all(blocks, axis, 0, 0, axis_index_groups=groups)  326 us
    pallas_call x2, Pallas kernels, normalise(): pl.pallas_call(functools.partial(normalise_kernel, span), out_shape=(jax....  11.4 us
    all_to_all x2, waiting for transfers between devices, exchange(): return lax.all_to_all(blocks, axis, 0, 0, axis_index_groups=groups)  11.1 us
  transfers between devices with their start and end apart: 2, of which 2 were waited for; matrix products, arithmetic and copies ran while one was open for 0% of the time, Pallas kernels for 1%

profile of v8, /device:TPU:1, one launch (start us, length us, event | category | flops | bytes accessed | tf_op | source)
XLA Modules:
  0.0 382.9 jit_solution(10306792662640338381)
XLA Ops:
  0.6 0.0 copy-start
  0.6 0.9 copy-done
  1.6 3.2 convolution_convert_fusion
  4.7 0.0 copy-start.4
  4.8 26.7 %all_to_all.110 = bf16[32,64,128]{2,1,0:T(8,128)(2,1)S(1)} all-to-all(bf16[32,64,128]{2,1,0:T(8,128)(2,1)S(1)} %bitcast.44), channel_id=1, replica_groups=mesh['dp'=16,'mp'=32] {'mp'}, dimensions={0} | all-to-all | bytes 1048576 | tf_op jit(solution)/shard_map/all_to_all | solution.py:209
  31.5 0.1 reduce_sum.196
  31.5 0.1 broadcast_in_dim.20
  31.7 20.1 %all_to_all.111 = bf16[32,64,128]{2,1,0:T(8,128)(2,1)S(1)} all-to-all(bf16[32,64,128]{2,1,0:T(8,128)(2,1)S(1)} %broadcast_in_dim.20), channel_id=1, replica_groups=mesh['dp'=16,'mp'=32] {'mp'}, dimensions={0} | all-to-all | bytes 1048576 | tf_op jit(solution)/shard_map/all_to_all | solution.py:209
  51.7 0.0 copy-done.4
  51.7 0.4 convolution_bitcast_fusion.2
  52.1 0.1 copy.9
  52.2 23.0 %all_to_all.112 = f32[16,16,128]{2,1,0:T(8,128)S(1)} all-to-all(f32[16,16,128]{2,1,0:T(8,128)S(1)} %bitcast.56), channel_id=1, replica_groups=mesh['dp'=16,'mp'=32] {'dp'}, dimensions={0} | all-to-all | bytes 262144 | tf_op jit(solution)/shard_map/all_to_all | solution.py:209
  75.3 11.6 %all_to_all.113 = f32[16,16,128]{2,1,0:T(8,128)S(1)} all-to-all(f32[16,16,128]{2,1,0:T(8,128)S(1)} %broadcast_in_dim.21), channel_id=1, replica_groups=mesh['dp'=16,'mp'=32] {'dp'}, dimensions={0} | all-to-all | bytes 262144 | tf_op jit(solution)/shard_map/all_to_all | solution.py:209
  86.9 0.6 shard_map.50
  87.5 21.2 %all_to_all.114 = f32[4,640,128]{2,1,0:T(8,128)S(1)} all-to-all(f32[4,640,128]{2,1,0:T(8,128)S(1)} %shard_map.50), channel_id=1, replica_groups={{0,1,2,3},{4,5,6,7},{8,9,10,11},{12,13,14,15},{16,17,18,19},{20,21,22,2..., dimensions={0} | all-to-all | bytes 2621440 | tf_op jit(solution)/shard_map/all_to_all | solution.py:209
  108.7 0.1 slice_reduce_fusion.2
  108.7 0.0 copy-start.1
  108.8 15.3 %all_to_all.115 = f32[8,80,128]{2,1,0:T(8,128)S(1)} all-to-all(f32[8,80,128]{2,1,0:T(8,128)S(1)} %pad_maximum_fusion), channel_id=1, replica_groups={{0,4,8,12,16,20,24,28},{1,5,9,13,17,21,25,29},{2,6,10,14,18,22,26,30},{..., dimensions={0} | all-to-all | bytes 655360 | tf_op jit(solution)/shard_map/all_to_all | solution.py:209
  124.1 13.3 %all_to_all.116.pieces_ref = f32[8,80,128]{2,1,0:T(8,128)S(1)} all-to-all(f32[8,80,128]{2,1,0:T(8,128)S(1)} %broadcast_in_dim.22), channel_id=1, replica_groups={{0,4,8,12,16,20,24,28},{1,5,9,13,17,21,25,29},{2,6,10,14,18,22,26,30},{..., dimensions={0} | all-to-all | bytes 655360 | tf_op jit(solution)/shard_map/all_to_all | solution.py:209
  137.5 5.7 %shard_map.51 = (bf16[4,512,128]{2,1,0:T(8,128)(2,1)S(1)}, f32[128,128]{1,0:T(8,128)}) custom-call(f32[8,80,128]{2,1,0:T(8,128)S(1)} %all_to_all.116.pieces_ref), custom_call_target="tpu_custom_call" | custom-call | tf_op jit(solution)/shard_map/pallas_call | solution.py:116
  143.2 9.3 %all_to_all.117 = bf16[4,512,128]{2,1,0:T(8,128)(2,1)S(1)} all-to-all(bf16[4,512,128]{2,1,0:T(8,128)(2,1)S(1)} %get-tuple-element.4), channel_id=1, replica_groups={{0,1,2,3},{4,5,6,7},{8,9,10,11},{12,13,14,15},{16,17,18,19},{20,21,22,2..., dimensions={0} | all-to-all | bytes 1048576 | tf_op jit(solution)/shard_map/all_to_all | solution.py:209
  152.6 0.0 copy-done.1
  152.6 0.7 convolution_bitcast_fusion
  153.3 0.2 copy.10
  153.5 22.8 %all_to_all.118 = f32[16,56,128]{2,1,0:T(8,128)S(1)} all-to-all(f32[16,56,128]{2,1,0:T(8,128)S(1)} %bitcast.49), channel_id=1, replica_groups=mesh['dp'=16,'mp'=32] {'dp'}, dimensions={0} | all-to-all | bytes 917504 | tf_op jit(solution)/shard_map/all_to_all | solution.py:209
  176.4 14.1 %all_to_all.119 = f32[8,56,128]{2,1,0:T(8,128)S(1)} all-to-all(f32[8,56,128]{2,1,0:T(8,128)S(1)} %broadcast_in_dim.23), channel_id=1, replica_groups={{0,64,128,192,256,320,384,448},{32,96,160,224,288,352,416,480},{1,65,12..., dimensions={0} | all-to-all | bytes 458752 | tf_op jit(solution)/shard_map/all_to_all | solution.py:209
  190.5 2.2 all_gather.6.sketch_ref
  192.7 0.0 copy-start.2
  192.7 2.0 copy-done.2
  194.8 1.7 shard_map.52
  196.4 20.1 %all_to_all.120 = f32[4,640,128]{2,1,0:T(8,128)S(1)} all-to-all(f32[4,640,128]{2,1,0:T(8,128)S(1)} %shard_map.52), channel_id=1, replica_groups={{0,1,2,3},{4,5,6,7},{8,9,10,11},{12,13,14,15},{16,17,18,19},{20,21,22,2..., dimensions={0} | all-to-all | bytes 2621440 | tf_op jit(solution)/shard_map/all_to_all | solution.py:209
  216.6 0.1 slice_reduce_fusion.1
  216.6 13.4 %all_to_all.121 = f32[8,80,128]{2,1,0:T(8,128)S(1)} all-to-all(f32[8,80,128]{2,1,0:T(8,128)S(1)} %pad_maximum_fusion.1), channel_id=1, replica_groups={{0,4,8,12,16,20,24,28},{1,5,9,13,17,21,25,29},{2,6,10,14,18,22,26,30},{..., dimensions={0} | all-to-all | bytes 655360 | tf_op jit(solution)/shard_map/all_to_all | solution.py:209
  230.1 13.2 %all_to_all.122.pieces_ref = f32[8,80,128]{2,1,0:T(8,128)S(1)} all-to-all(f32[8,80,128]{2,1,0:T(8,128)S(1)} %broadcast_in_dim.24), channel_id=1, replica_groups={{0,4,8,12,16,20,24,28},{1,5,9,13,17,21,25,29},{2,6,10,14,18,22,26,30},{..., dimensions={0} | all-to-all | bytes 655360 | tf_op jit(solution)/shard_map/all_to_all | solution.py:209
  243.3 5.7 %shard_map.53 = (bf16[4,512,128]{2,1,0:T(8,128)(2,1)S(1)}, f32[128,128]{1,0:T(8,128)}) custom-call(f32[8,80,128]{2,1,0:T(8,128)S(1)} %all_to_all.122.pieces_ref), custom_call_target="tpu_custom_call" | custom-call | tf_op jit(solution)/shard_map/pallas_call | solution.py:116
  249.1 9.3 %all_to_all.123 = bf16[4,512,128]{2,1,0:T(8,128)(2,1)S(1)} all-to-all(bf16[4,512,128]{2,1,0:T(8,128)(2,1)S(1)} %get-tuple-element.5), channel_id=1, replica_groups={{0,1,2,3},{4,5,6,7},{8,9,10,11},{12,13,14,15},{16,17,18,19},{20,21,22,2..., dimensions={0} | all-to-all | bytes 1048576 | tf_op jit(solution)/shard_map/all_to_all | solution.py:209
  258.4 0.4 convolution_bitcast_fusion.1
  258.8 0.1 copy.12
  258.9 17.1 %all_to_all.124 = f32[16,16,128]{2,1,0:T(8,128)S(1)} all-to-all(f32[16,16,128]{2,1,0:T(8,128)S(1)} %bitcast.57), channel_id=1, replica_groups=mesh['dp'=16,'mp'=32] {'dp'}, dimensions={0} | all-to-all | bytes 262144 | tf_op jit(solution)/shard_map/all_to_all | solution.py:209
  276.1 11.6 %all_to_all.125 = f32[16,16,128]{2,1,0:T(8,128)S(1)} all-to-all(f32[16,16,128]{2,1,0:T(8,128)S(1)} %broadcast_in_dim.25), channel_id=1, replica_groups=mesh['dp'=16,'mp'=32] {'dp'}, dimensions={0} | all-to-all | bytes 262144 | tf_op jit(solution)/shard_map/all_to_all | solution.py:209
  287.6 0.6 shard_map.54
  288.2 16.5 %all_to_all.126 = bf16[4,896,128]{2,1,0:T(8,128)(2,1)S(1)} all-to-all(bf16[4,896,128]{2,1,0:T(8,128)(2,1)S(1)} %shard_map.54), channel_id=1, replica_groups={{0,1,2,3},{4,5,6,7},{8,9,10,11},{12,13,14,15},{16,17,18,19},{20,21,22,2..., dimensions={0} | all-to-all | bytes 1835008 | tf_op jit(solution)/shard_map/all_to_all | solution.py:209
  304.8 0.1 convert_element_type.56
  304.9 0.1 slice_reduce_fusion
  305.1 12.9 %all_to_all.127 = bf16[8,112,128]{2,1,0:T(8,128)(2,1)S(1)} all-to-all(bf16[8,112,128]{2,1,0:T(8,128)(2,1)S(1)} %pad_maximum_fusion.2), channel_id=1, replica_groups={{0,4,8,12,16,20,24,28},{1,5,9,13,17,21,25,29},{2,6,10,14,18,22,26,30},{..., dimensions={0} | all-to-all | bytes 458752 | tf_op jit(solution)/shard_map/all_to_all | solution.py:209
  318.1 11.2 %all_to_all.128.pieces_ref = bf16[8,112,128]{2,1,0:T(8,128)(2,1)S(1)} all-to-all(bf16[8,112,128]{2,1,0:T(8,128)(2,1)S(1)} %broadcast_in_dim.26), channel_id=1, replica_groups={{0,4,8,12,16,20,24,28},{1,5,9,13,17,21,25,29},{2,6,10,14,18,22,26,30},{..., dimensions={0} | all-to-all | bytes 458752 | tf_op jit(solution)/shard_map/all_to_all | solution.py:209
  329.4 0.9 broadcast_in_dim.28
  330.2 3.5 all-to-all-start.19
  333.7 4.0 %shard_map.55.inverse_ref = f32[128,128]{1,0:T(8,128)S(1)} custom-call(bf16[8,112,128]{2,1,0:T(8,128)(2,1)S(1)} %all_to_all.128.pieces_ref), custom_call_target="tpu_custom_call" | custom-call | flops 8388608 | bytes 294912 | tf_op jit(solution)/shard_map/pallas_call | solution.py:96
  337.7 2.9 all-to-all-done.19.rows_ref
  340.6 0.0 copy-start.3
  340.6 2.0 copy-done.3
  342.7 1.2 shard_map.56
  343.8 22.9 %all_to_all.129 = f32[16,8,896]{2,1,0:T(8,128)S(1)} all-to-all(f32[16,8,896]{2,1,0:T(8,128)S(1)} %shard_map.56), channel_id=1, replica_groups=mesh['dp'=16,'mp'=32] {'dp'}, dimensions={0} | all-to-all | bytes 917504 | tf_op jit(solution)/shard_map/all_to_all | solution.py:209
  366.7 0.7 broadcast_in_dim.29
  367.4 3.4 all-to-all-start.21
  370.8 0.9 convolution_multiply_fusion
  371.7 8.2 %all-to-all-done.21 = bf16[8,8,896]{2,1,0:T(8,128)(2,1)S(1)} async-done(((bf16[8,8,896]{2,1,0:T(8,128)(2,1)}), bf16[8,8,896]{2,1,0:T(8,128)(2,1)S(1)}, u32[]{:S(2)}, u32[]{:S(2)}) %all-to-all-start.21) | async-done | bytes 114720 | tf_op jit(solution)/shard_map/all_to_all | solution.py:209
  380.0 2.2 all_gather.7
  382.1 0.8 copy.14
  (33 shorter events, 0.6 us)
Async XLA Ops:
  0.6 0.9 copy-start
  4.7 47.0 %copy-start.4 = (bf16[2048,256]{1,0:T(8,128)(2,1)S(1)}, bf16[2048,256]{1,0:T(8,128)(2,1)}, u32[]{:S(2)}) copy-start(bf16[2048,256]{1,0:T(8,128)(2,1)} %data_ref.5) | copy-start | bytes 3145732
  108.7 43.9 %copy-start.1 = (bf16[2048,896]{1,0:T(8,128)(2,1)S(1)}, bf16[2048,896]{1,0:T(8,128)(2,1)}, u32[]{:S(2)}) copy-start(bf16[2048,896]{1,0:T(8,128)(2,1)} %grads_ref.1) | copy-start | bytes 11010052
  192.7 2.0 copy-start.2
  330.2 10.4 %all-to-all-start.19 = ((bf16[4,512,128]{2,1,0:T(8,128)(2,1)}), bf16[4,512,128]{2,1,0:T(8,128)(2,1)S(1)}, u32[]{:S(2)}, u32[]{:S(2)}) async-start(bf16[4,512,128]{2,1,0:T(8,128)(2,1)} %broadcast_in_dim.28), calls=%async_computation.19 | async-start | bytes 1048576 | tf_op jit(solution)/shard_map/all_to_all | solution.py:209
  340.6 2.0 copy-start.3
  367.4 12.6 %all-to-all-start.21 = ((bf16[8,8,896]{2,1,0:T(8,128)(2,1)}), bf16[8,8,896]{2,1,0:T(8,128)(2,1)S(1)}, u32[]{:S(2)}, u32[]{:S(2)}) async-start(bf16[8,8,896]{2,1,0:T(8,128)(2,1)} %broadcast_in_dim.29), calls=%async_computation.21 | async-start | bytes 229376 | tf_op jit(solution)/shard_map/all_to_all | solution.py:209

commit v9 on v8

--- a/solution.py
+++ b/solution.py
@@ -106,10 +106,10 @@
 
 def normalise_kernel(span, pieces_ref, rows_ref, inverse_ref):
     inverse_factor(gram_groups(pieces_ref, span), inverse_ref)
-    for y in range(N_Y):
-        rows = nt_product(pieces_ref[y, :span, :], inverse_ref[...]).astype(rows_ref.dtype)
-        for x in range(N_X):
-            rows_ref[x, span * y:span * (y + 1), :] = rows
+    product = jnp.concatenate([pieces_ref[y, :span, :] for y in range(N_Y)], axis=0)
+    rows = nt_product(product, inverse_ref[...]).astype(rows_ref.dtype)
+    for x in range(N_X):
+        rows_ref[x] = rows
 
 
 def normalise(pieces, span):

time: 384 us -> 383 us (level)
  no operation moved by 1% of the time
where the time goes in v9:
time: 383 us; the launch traced here: 382 us
  blocking collectives  330 us (86%)
  Pallas kernels  18.3 us (5%)
  waiting for transfers between devices  11.1 us (3%)
  local copies, waits for them, and re-layouts  7.94 us (2%)
  starting transfers between devices  6.84 us (2%)
  matrix products  5.53 us (1%)
    all_to_all x20, blocking collectives, exchange(): return lax.all_to_all(blocks, axis, 0, 0, axis_index_groups=groups)  326 us
    all_to_all x2, waiting for transfers between devices, exchange(): return lax.all_to_all(blocks, axis, 0, 0, axis_index_groups=groups)  11.1 us
    pallas_call x2, Pallas kernels, normalise(): pl.pallas_call(functools.partial(normalise_kernel, span), out_shape=(jax....  10.4 us
  transfers between devices with their start and end apart: 2, of which 2 were waited for; matrix products, arithmetic and copies ran while one was open for 0% of the time, Pallas kernels for 1%

profile of v9, /device:TPU:1, one launch (start us, length us, event | category | flops | bytes accessed | tf_op | source)
XLA Modules:
  0.0 381.8 jit_solution(5465526895277610292)
XLA Ops:
  0.6 0.0 copy-start
  0.6 0.9 copy-done
  1.6 3.2 convolution_convert_fusion
  4.7 0.0 copy-start.4
  4.8 26.7 %all_to_all.110 = bf16[32,64,128]{2,1,0:T(8,128)(2,1)S(1)} all-to-all(bf16[32,64,128]{2,1,0:T(8,128)(2,1)S(1)} %bitcast.44), channel_id=1, replica_groups=mesh['dp'=16,'mp'=32] {'mp'}, dimensions={0} | all-to-all | bytes 1048576 | tf_op jit(solution)/shard_map/all_to_all | solution.py:209
  31.5 0.1 reduce_sum.196
  31.5 0.1 broadcast_in_dim.20
  31.7 20.1 %all_to_all.111 = bf16[32,64,128]{2,1,0:T(8,128)(2,1)S(1)} all-to-all(bf16[32,64,128]{2,1,0:T(8,128)(2,1)S(1)} %broadcast_in_dim.20), channel_id=1, replica_groups=mesh['dp'=16,'mp'=32] {'mp'}, dimensions={0} | all-to-all | bytes 1048576 | tf_op jit(solution)/shard_map/all_to_all | solution.py:209
  51.7 0.0 copy-done.4
  51.7 0.4 convolution_bitcast_fusion.2
  52.1 0.1 copy.9
  52.2 23.0 %all_to_all.112 = f32[16,16,128]{2,1,0:T(8,128)S(1)} all-to-all(f32[16,16,128]{2,1,0:T(8,128)S(1)} %bitcast.56), channel_id=1, replica_groups=mesh['dp'=16,'mp'=32] {'dp'}, dimensions={0} | all-to-all | bytes 262144 | tf_op jit(solution)/shard_map/all_to_all | solution.py:209
  75.3 11.6 %all_to_all.113 = f32[16,16,128]{2,1,0:T(8,128)S(1)} all-to-all(f32[16,16,128]{2,1,0:T(8,128)S(1)} %broadcast_in_dim.21), channel_id=1, replica_groups=mesh['dp'=16,'mp'=32] {'dp'}, dimensions={0} | all-to-all | bytes 262144 | tf_op jit(solution)/shard_map/all_to_all | solution.py:209
  86.9 0.6 shard_map.50
  87.5 21.2 %all_to_all.114 = f32[4,640,128]{2,1,0:T(8,128)S(1)} all-to-all(f32[4,640,128]{2,1,0:T(8,128)S(1)} %shard_map.50), channel_id=1, replica_groups={{0,1,2,3},{4,5,6,7},{8,9,10,11},{12,13,14,15},{16,17,18,19},{20,21,22,2..., dimensions={0} | all-to-all | bytes 2621440 | tf_op jit(solution)/shard_map/all_to_all | solution.py:209
  108.7 0.1 slice_reduce_fusion.2
  108.7 0.0 copy-start.1
  108.8 15.3 %all_to_all.115 = f32[8,80,128]{2,1,0:T(8,128)S(1)} all-to-all(f32[8,80,128]{2,1,0:T(8,128)S(1)} %pad_maximum_fusion), channel_id=1, replica_groups={{0,4,8,12,16,20,24,28},{1,5,9,13,17,21,25,29},{2,6,10,14,18,22,26,30},{..., dimensions={0} | all-to-all | bytes 655360 | tf_op jit(solution)/shard_map/all_to_all | solution.py:209
  124.1 13.3 %all_to_all.116.pieces_ref = f32[8,80,128]{2,1,0:T(8,128)S(1)} all-to-all(f32[8,80,128]{2,1,0:T(8,128)S(1)} %broadcast_in_dim.22), channel_id=1, replica_groups={{0,4,8,12,16,20,24,28},{1,5,9,13,17,21,25,29},{2,6,10,14,18,22,26,30},{..., dimensions={0} | all-to-all | bytes 655360 | tf_op jit(solution)/shard_map/all_to_all | solution.py:209
  137.5 5.2 %shard_map.51 = (bf16[4,512,128]{2,1,0:T(8,128)(2,1)S(1)}, f32[128,128]{1,0:T(8,128)}) custom-call(f32[8,80,128]{2,1,0:T(8,128)S(1)} %all_to_all.116.pieces_ref), custom_call_target="tpu_custom_call" | custom-call | tf_op jit(solution)/shard_map/pallas_call | solution.py:116
  142.7 9.3 %all_to_all.117 = bf16[4,512,128]{2,1,0:T(8,128)(2,1)S(1)} all-to-all(bf16[4,512,128]{2,1,0:T(8,128)(2,1)S(1)} %get-tuple-element.4), channel_id=1, replica_groups={{0,1,2,3},{4,5,6,7},{8,9,10,11},{12,13,14,15},{16,17,18,19},{20,21,22,2..., dimensions={0} | all-to-all | bytes 1048576 | tf_op jit(solution)/shard_map/all_to_all | solution.py:209
  152.0 0.0 copy-done.1
  152.0 0.7 convolution_bitcast_fusion
  152.7 0.2 copy.10
  153.0 22.8 %all_to_all.118 = f32[16,56,128]{2,1,0:T(8,128)S(1)} all-to-all(f32[16,56,128]{2,1,0:T(8,128)S(1)} %bitcast.49), channel_id=1, replica_groups=mesh['dp'=16,'mp'=32] {'dp'}, dimensions={0} | all-to-all | bytes 917504 | tf_op jit(solution)/shard_map/all_to_all | solution.py:209
  175.9 14.1 %all_to_all.119 = f32[8,56,128]{2,1,0:T(8,128)S(1)} all-to-all(f32[8,56,128]{2,1,0:T(8,128)S(1)} %broadcast_in_dim.23), channel_id=1, replica_groups={{0,64,128,192,256,320,384,448},{32,96,160,224,288,352,416,480},{1,65,12..., dimensions={0} | all-to-all | bytes 458752 | tf_op jit(solution)/shard_map/all_to_all | solution.py:209
  189.9 2.2 all_gather.6.sketch_ref
  192.1 0.0 copy-start.2
  192.2 2.0 copy-done.2
  194.2 1.7 shard_map.52
  195.9 20.1 %all_to_all.120 = f32[4,640,128]{2,1,0:T(8,128)S(1)} all-to-all(f32[4,640,128]{2,1,0:T(8,128)S(1)} %shard_map.52), channel_id=1, replica_groups={{0,1,2,3},{4,5,6,7},{8,9,10,11},{12,13,14,15},{16,17,18,19},{20,21,22,2..., dimensions={0} | all-to-all | bytes 2621440 | tf_op jit(solution)/shard_map/all_to_all | solution.py:209
  216.0 0.1 slice_reduce_fusion.1
  216.1 13.4 %all_to_all.121 = f32[8,80,128]{2,1,0:T(8,128)S(1)} all-to-all(f32[8,80,128]{2,1,0:T(8,128)S(1)} %pad_maximum_fusion.1), channel_id=1, replica_groups={{0,4,8,12,16,20,24,28},{1,5,9,13,17,21,25,29},{2,6,10,14,18,22,26,30},{..., dimensions={0} | all-to-all | bytes 655360 | tf_op jit(solution)/shard_map/all_to_all | solution.py:209
  229.6 13.2 %all_to_all.122.pieces_ref = f32[8,80,128]{2,1,0:T(8,128)S(1)} all-to-all(f32[8,80,128]{2,1,0:T(8,128)S(1)} %broadcast_in_dim.24), channel_id=1, replica_groups={{0,4,8,12,16,20,24,28},{1,5,9,13,17,21,25,29},{2,6,10,14,18,22,26,30},{..., dimensions={0} | all-to-all | bytes 655360 | tf_op jit(solution)/shard_map/all_to_all | solution.py:209
  242.8 5.2 %shard_map.53 = (bf16[4,512,128]{2,1,0:T(8,128)(2,1)S(1)}, f32[128,128]{1,0:T(8,128)}) custom-call(f32[8,80,128]{2,1,0:T(8,128)S(1)} %all_to_all.122.pieces_ref), custom_call_target="tpu_custom_call" | custom-call | tf_op jit(solution)/shard_map/pallas_call | solution.py:116
  248.0 9.3 %all_to_all.123 = bf16[4,512,128]{2,1,0:T(8,128)(2,1)S(1)} all-to-all(bf16[4,512,128]{2,1,0:T(8,128)(2,1)S(1)} %get-tuple-element.5), channel_id=1, replica_groups={{0,1,2,3},{4,5,6,7},{8,9,10,11},{12,13,14,15},{16,17,18,19},{20,21,22,2..., dimensions={0} | all-to-all | bytes 1048576 | tf_op jit(solution)/shard_map/all_to_all | solution.py:209
  257.3 0.4 convolution_bitcast_fusion.1
  257.6 0.1 copy.12
  257.7 17.1 %all_to_all.124 = f32[16,16,128]{2,1,0:T(8,128)S(1)} all-to-all(f32[16,16,128]{2,1,0:T(8,128)S(1)} %bitcast.57), channel_id=1, replica_groups=mesh['dp'=16,'mp'=32] {'dp'}, dimensions={0} | all-to-all | bytes 262144 | tf_op jit(solution)/shard_map/all_to_all | solution.py:209
  274.9 11.6 %all_to_all.125 = f32[16,16,128]{2,1,0:T(8,128)S(1)} all-to-all(f32[16,16,128]{2,1,0:T(8,128)S(1)} %broadcast_in_dim.25), channel_id=1, replica_groups=mesh['dp'=16,'mp'=32] {'dp'}, dimensions={0} | all-to-all | bytes 262144 | tf_op jit(solution)/shard_map/all_to_all | solution.py:209
  286.5 0.6 shard_map.54
  287.1 16.5 %all_to_all.126 = bf16[4,896,128]{2,1,0:T(8,128)(2,1)S(1)} all-to-all(bf16[4,896,128]{2,1,0:T(8,128)(2,1)S(1)} %shard_map.54), channel_id=1, replica_groups={{0,1,2,3},{4,5,6,7},{8,9,10,11},{12,13,14,15},{16,17,18,19},{20,21,22,2..., dimensions={0} | all-to-all | bytes 1835008 | tf_op jit(solution)/shard_map/all_to_all | solution.py:209
  303.6 0.1 convert_element_type.56
  303.7 0.1 slice_reduce_fusion
  303.9 12.9 %all_to_all.127 = bf16[8,112,128]{2,1,0:T(8,128)(2,1)S(1)} all-to-all(bf16[8,112,128]{2,1,0:T(8,128)(2,1)S(1)} %pad_maximum_fusion.2), channel_id=1, replica_groups={{0,4,8,12,16,20,24,28},{1,5,9,13,17,21,25,29},{2,6,10,14,18,22,26,30},{..., dimensions={0} | all-to-all | bytes 458752 | tf_op jit(solution)/shard_map/all_to_all | solution.py:209
  317.0 11.5 %all_to_all.128.pieces_ref = bf16[8,112,128]{2,1,0:T(8,128)(2,1)S(1)} all-to-all(bf16[8,112,128]{2,1,0:T(8,128)(2,1)S(1)} %broadcast_in_dim.26), channel_id=1, replica_groups={{0,4,8,12,16,20,24,28},{1,5,9,13,17,21,25,29},{2,6,10,14,18,22,26,30},{..., dimensions={0} | all-to-all | bytes 458752 | tf_op jit(solution)/shard_map/all_to_all | solution.py:209
  328.5 0.9 broadcast_in_dim.28
  329.4 3.5 all-to-all-start.19
  332.9 4.0 %shard_map.55.inverse_ref = f32[128,128]{1,0:T(8,128)S(1)} custom-call(bf16[8,112,128]{2,1,0:T(8,128)(2,1)S(1)} %all_to_all.128.pieces_ref), custom_call_target="tpu_custom_call" | custom-call | flops 8388608 | bytes 294912 | tf_op jit(solution)/shard_map/pallas_call | solution.py:96
  336.9 2.9 all-to-all-done.19.rows_ref
  339.8 0.0 copy-start.3
  339.8 2.0 copy-done.3
  341.8 1.2 shard_map.56
  343.0 22.6 %all_to_all.129 = f32[16,8,896]{2,1,0:T(8,128)S(1)} all-to-all(f32[16,8,896]{2,1,0:T(8,128)S(1)} %shard_map.56), channel_id=1, replica_groups=mesh['dp'=16,'mp'=32] {'dp'}, dimensions={0} | all-to-all | bytes 917504 | tf_op jit(solution)/shard_map/all_to_all | solution.py:209
  365.6 0.7 broadcast_in_dim.29
  366.3 3.4 all-to-all-start.21
  369.7 0.9 convolution_multiply_fusion
  370.6 8.2 %all-to-all-done.21 = bf16[8,8,896]{2,1,0:T(8,128)(2,1)S(1)} async-done(((bf16[8,8,896]{2,1,0:T(8,128)(2,1)}), bf16[8,8,896]{2,1,0:T(8,128)(2,1)S(1)}, u32[]{:S(2)}, u32[]{:S(2)}) %all-to-all-start.21) | async-done | bytes 114720 | tf_op jit(solution)/shard_map/all_to_all | solution.py:209
  378.9 2.2 all_gather.7
  381.0 0.8 copy.14
  (33 shorter events, 0.6 us)
Async XLA Ops:
  0.6 0.9 copy-start
  4.7 47.0 %copy-start.4 = (bf16[2048,256]{1,0:T(8,128)(2,1)S(1)}, bf16[2048,256]{1,0:T(8,128)(2,1)}, u32[]{:S(2)}) copy-start(bf16[2048,256]{1,0:T(8,128)(2,1)} %data_ref.5) | copy-start | bytes 3145732
  108.7 43.3 %copy-start.1 = (bf16[2048,896]{1,0:T(8,128)(2,1)S(1)}, bf16[2048,896]{1,0:T(8,128)(2,1)}, u32[]{:S(2)}) copy-start(bf16[2048,896]{1,0:T(8,128)(2,1)} %grads_ref.1) | copy-start | bytes 11010052
  192.1 2.0 copy-start.2
  329.4 10.4 %all-to-all-start.19 = ((bf16[4,512,128]{2,1,0:T(8,128)(2,1)}), bf16[4,512,128]{2,1,0:T(8,128)(2,1)S(1)}, u32[]{:S(2)}, u32[]{:S(2)}) async-start(bf16[4,512,128]{2,1,0:T(8,128)(2,1)} %broadcast_in_dim.28), calls=%async_computation.19 | async-start | bytes 1048576 | tf_op jit(solution)/shard_map/all_to_all | solution.py:209
  339.8 2.0 copy-start.3
  366.3 12.6 %all-to-all-start.21 = ((bf16[8,8,896]{2,1,0:T(8,128)(2,1)}), bf16[8,8,896]{2,1,0:T(8,128)(2,1)S(1)}, u32[]{:S(2)}, u32[]{:S(2)}) async-start(bf16[8,8,896]{2,1,0:T(8,128)(2,1)} %broadcast_in_dim.29), calls=%async_computation.21 | async-start | bytes 229376 | tf_op jit(solution)/shard_map/all_to_all | solution.py:209
